TPU v7x, 128 devices: a whole 4x4x4 slice. The times are simulated.
128 devices in a mesh: req: 32 (over x, y, core), mlp: 4 (over z).
Axes of the slice: x: 4, y: 4, z: 4, core: 2. Of those that a mesh axis runs over, the one named last changes fastest.
Arguments:
- new_qkv: bfloat16 [1024, 3, 3072], P('req', None, 'mlp'), may hold values from -8 to 8
- prompt_cache: bfloat16 [32, 4096, 2, 3072], P('req', None, None, 'mlp'), may hold values from -6 to 6
- tail_cache: bfloat16 [512, 256, 2, 3072], P('req', None, None, 'mlp'), may hold values from -6 to 6
- residual: bfloat16 [1024, 3072], P('req', 'mlp'), may hold values from -6 to 6
- w_out: bfloat16 [3072, 3072], P('mlp'), may hold values from -0.109375 to 0.109375
- mlp_gain: float32 [3072], replicated, may hold values from 0.5 to 1.5
- w_gate: bfloat16 [3072, 8192], P(None, ('req', 'mlp')), may hold values from -0.109375 to 0.109375
- w_up: bfloat16 [3072, 8192], P(None, ('req', 'mlp')), may hold values from -0.109375 to 0.109375
- w_down: bfloat16 [8192, 3072], P(('req', 'mlp')), may hold values from -0.25 to 0.25
- final_gain: float32 [3072], replicated, may hold values from 0.5 to 1.5
- score_weight: float32 [3072], replicated, may hold values from -0.109375 to 0.109375
- slot_part: int32 [32], replicated, may hold values from 0 to 31, each once
- prompt_len: int32 [16], replicated, may hold values from 1 to 8192, 65536 in all
- tail_len: int32 [512], replicated, may hold values from 1 to 256, 65536 in all
Outputs:
- hidden_out: bfloat16 [1024, 3072], P('req', 'mlp')
- score: float32 [1024], P('req')
Inputs may be any that keep to these rules, and one draw needn't show every extreme that they name: Each value once; slot s holds half slot_part[s] % 2 of prompt slot_part[s] // 2. `prompt_len`: the largest is exactly 8192. `tail_len`: the largest is exactly 256.
All inputs are finite; a program needn't handle non-finite values.
Results may differ from a plain program's by a relative error of at most 0.015.
Values may be sent and summed in bfloat16 or wider, within the bound.
A program may use at most 192 MiB of HBM per device.

v0:
```python
import math

import jax
import jax.numpy as jnp
from jax import lax
from jax.sharding import PartitionSpec as P

HD = 96


norm_eps = 1e-05
masked_value = -1e30


def rotary(values, position):
    half_dim = HD // 2
    freqs = 10000.0 ** (-(jnp.arange(half_dim, dtype=jnp.float32) * 2.0) / HD)
    angles = position.astype(jnp.float32)[..., None] * freqs
    cosine = jnp.cos(angles)[..., None, :]
    sine = jnp.sin(angles)[..., None, :]
    first = values[..., :half_dim]
    second = values[..., half_dim:]
    return jnp.concatenate(
        [first * cosine - second * sine, second * cosine + first * sine], axis=-1
    )


def per_device(
    new_qkv,
    prompt_cache,
    tail_cache,
    residual,
    w_out,
    mlp_gain,
    w_gate,
    w_up,
    w_down,
    final_gain,
    score_weight,
    slot_part,
    prompt_len,
    tail_len,
):
    req_count = lax.axis_size("req")
    req_index = lax.axis_index("req")
    mlp_index = lax.axis_index("mlp")
    rows_here = new_qkv.shape[0]
    width_here = new_qkv.shape[2]
    heads_here = width_here // HD
    conts_here = rows_here // 2
    width = w_out.shape[1]
    score_scale = 1.0 / math.sqrt(HD)
    own_prompt = req_index // 2
    tail_here = lax.dynamic_slice_in_dim(tail_len, req_index * conts_here, conts_here)
    plen_here = lax.dynamic_index_in_dim(prompt_len, own_prompt, 0, keepdims=False)
    position = plen_here + tail_here[:, None] + jnp.arange(2, dtype=jnp.int32)[None, :]
    block = new_qkv.reshape(conts_here, 2, 3, heads_here, HD)
    query = rotary(block[:, :, 0].astype(jnp.float32), position).astype(jnp.bfloat16)
    key_new = rotary(block[:, :, 1].astype(jnp.float32), position).astype(jnp.bfloat16)
    value_new = block[:, :, 2]
    gathered = lax.all_gather(query.reshape(rows_here, width_here), "req", axis=0, tiled=True)
    slot_ids = jnp.arange(req_count, dtype=jnp.int32)
    slot_of = jnp.sum(
        jnp.where(slot_part[None, :] == slot_ids[:, None], slot_ids[None, :], 0), axis=1
    )
    held_part = lax.dynamic_index_in_dim(slot_part, req_index, 0, keepdims=False)
    owned_prompt = held_part // 2
    held_half = held_part % 2
    span = prompt_cache.shape[1]
    owned_rows = 2 * rows_here
    q_owned = lax.dynamic_slice_in_dim(gathered, owned_prompt * owned_rows, owned_rows, 0).reshape(
        owned_rows, heads_here, HD
    )
    owned_len = lax.dynamic_index_in_dim(prompt_len, owned_prompt, 0, keepdims=False)
    valid_count = jnp.clip(owned_len - held_half * span, 0, span)
    block_len = min(512, span)
    block_count = (valid_count + block_len - 1) // block_len
    cache_keys = prompt_cache[0, :, 0].reshape(span, heads_here, HD)
    cache_values = prompt_cache[0, :, 1].reshape(span, heads_here, HD)

    def score_block(number, buffer):
        key_block = lax.dynamic_slice_in_dim(cache_keys, number * block_len, block_len, 0)
        block_scores = (
            jnp.einsum("rhd,khd->hrk", q_owned, key_block, preferred_element_type=jnp.float32)
            * score_scale
        )
        places = number * block_len + jnp.arange(block_len, dtype=jnp.int32)
        block_scores = jnp.where(places[None, None, :] < valid_count, block_scores, masked_value)
        return lax.dynamic_update_slice_in_dim(buffer, block_scores, number * block_len, 2)

    empty_scores = jnp.full((heads_here, owned_rows, span), masked_value, jnp.float32)
    prefix_scores = lax.fori_loop(0, block_count, score_block, empty_scores)
    prefix_max = jnp.max(prefix_scores, axis=2)
    tail_cap = tail_cache.shape[1]
    tail_keys = tail_cache[:, :, 0].reshape(conts_here, tail_cap, heads_here, HD)
    tail_values = tail_cache[:, :, 1].reshape(conts_here, tail_cap, heads_here, HD)
    s_tail = (
        jnp.einsum("cthd,cjhd->chtj", query, tail_keys, preferred_element_type=jnp.float32)
        * score_scale
    )
    s_tail = jnp.where(
        jnp.arange(tail_cap)[None, None, None, :] < tail_here[:, None, None, None],
        s_tail,
        masked_value,
    )
    s_new = (
        jnp.einsum("cthd,cuhd->chtu", query, key_new, preferred_element_type=jnp.float32)
        * score_scale
    )
    causal = jnp.arange(2)[None, :] <= jnp.arange(2)[:, None]
    s_new = jnp.where(causal[None, None, :, :], s_new, masked_value)
    tail_max = jnp.maximum(jnp.max(s_tail, -1), jnp.max(s_new, -1))
    tail_max = jnp.transpose(tail_max, (1, 0, 2)).reshape(heads_here, rows_here)
    prefix_all, tail_all = (
        lax.all_gather(prefix_max[None], "req", axis=0, tiled=True),
        lax.all_gather(tail_max[None], "req", axis=0, tiled=True),
    )

    def prompt_max(prompt):
        slot_a = lax.dynamic_index_in_dim(slot_of, 2 * prompt, 0, keepdims=False)
        slot_b = lax.dynamic_index_in_dim(slot_of, 2 * prompt + 1, 0, keepdims=False)
        first_max = lax.dynamic_index_in_dim(prefix_all, slot_a, 0, keepdims=False)
        second_max = lax.dynamic_index_in_dim(prefix_all, slot_b, 0, keepdims=False)
        paired = lax.dynamic_slice_in_dim(tail_all, 2 * prompt, 2, 0)
        paired = jnp.transpose(paired, (1, 0, 2)).reshape(heads_here, 2 * rows_here)
        return jnp.maximum(jnp.maximum(first_max, second_max), paired)

    owner_max = prompt_max(owned_prompt)

    def value_block(number, carry):
        numer, totals = carry
        score_part = lax.dynamic_slice_in_dim(prefix_scores, number * block_len, block_len, 2)
        weights = jnp.exp(score_part - owner_max[:, :, None])
        value_part = lax.dynamic_slice_in_dim(cache_values, number * block_len, block_len, 0)
        numer = numer + jnp.einsum(
            "hrk,khd->rhd",
            weights.astype(jnp.bfloat16),
            value_part,
            preferred_element_type=jnp.float32,
        )
        return (numer, totals + jnp.sum(weights, axis=2))

    start_carry = (
        jnp.zeros((owned_rows, heads_here, HD), jnp.float32),
        jnp.zeros((heads_here, owned_rows), jnp.float32),
    )
    owner_numer, owner_total = lax.fori_loop(0, block_count, value_block, start_carry)
    numer_all, total_all = (
        lax.all_gather(owner_numer.reshape(1, owned_rows, width_here), "req", axis=0, tiled=True),
        lax.all_gather(owner_total[None], "req", axis=0, tiled=True),
    )
    row_offset = req_index % 2 * rows_here
    slot_first = lax.dynamic_index_in_dim(slot_of, 2 * own_prompt, 0, keepdims=False)
    slot_second = lax.dynamic_index_in_dim(slot_of, 2 * own_prompt + 1, 0, keepdims=False)
    numer_first = lax.dynamic_slice_in_dim(
        lax.dynamic_index_in_dim(numer_all, slot_first, 0, keepdims=False), row_offset, rows_here, 0
    )
    numer_second = lax.dynamic_slice_in_dim(
        lax.dynamic_index_in_dim(numer_all, slot_second, 0, keepdims=False),
        row_offset,
        rows_here,
        0,
    )
    total_first = lax.dynamic_slice_in_dim(
        lax.dynamic_index_in_dim(total_all, slot_first, 0, keepdims=False), row_offset, rows_here, 1
    )
    total_second = lax.dynamic_slice_in_dim(
        lax.dynamic_index_in_dim(total_all, slot_second, 0, keepdims=False),
        row_offset,
        rows_here,
        1,
    )
    row_max = lax.dynamic_slice_in_dim(prompt_max(own_prompt), row_offset, rows_here, 1)
    row_max = jnp.transpose(row_max.reshape(heads_here, conts_here, 2), (1, 0, 2))
    w_tail = jnp.exp(s_tail - row_max[..., None])
    w_new = jnp.exp(s_new - row_max[..., None])
    numer_tail = jnp.einsum(
        "chtj,cjhd->cthd",
        w_tail.astype(jnp.bfloat16),
        tail_values,
        preferred_element_type=jnp.float32,
    )
    numer_tail = numer_tail + jnp.einsum(
        "chtu,cuhd->cthd", w_new.astype(jnp.bfloat16), value_new, preferred_element_type=jnp.float32
    )
    total_tail = jnp.transpose(jnp.sum(w_tail, -1) + jnp.sum(w_new, -1), (1, 0, 2)).reshape(
        heads_here, rows_here
    )
    row_total = total_first + total_second + total_tail
    row_numer = numer_first + numer_second + numer_tail.reshape(rows_here, width_here)
    attn = (
        (row_numer.reshape(rows_here, heads_here, HD) / jnp.transpose(row_total)[:, :, None])
        .astype(jnp.bfloat16)
        .reshape(rows_here, width_here)
    )
    projected = jnp.dot(attn, w_out, preferred_element_type=jnp.float32)
    col_start = mlp_index * width_here
    proj_cols = lax.psum_scatter(projected, "mlp", scatter_dimension=1, tiled=True)
    state_cols = residual.astype(jnp.float32) + proj_cols
    square_sum = lax.psum(jnp.sum(state_cols * state_cols, axis=1), "mlp")
    gain_cols = lax.dynamic_slice_in_dim(mlp_gain, col_start, width_here)
    normed_cols = (
        state_cols * lax.rsqrt(square_sum / width + norm_eps)[:, None] * gain_cols
    ).astype(jnp.bfloat16)
    normed_full = lax.all_gather(normed_cols, "mlp", axis=1, tiled=True)
    piece = lax.all_gather(normed_full, "req", axis=0, tiled=True)
    gate = jnp.dot(piece, w_gate, preferred_element_type=jnp.float32)
    upper = jnp.dot(piece, w_up, preferred_element_type=jnp.float32)
    hidden_all = (jax.nn.silu(gate) * upper).astype(jnp.bfloat16)
    row_sums = lax.psum_scatter(
        jnp.dot(hidden_all, w_down, preferred_element_type=jnp.float32),
        "req",
        scatter_dimension=0,
        tiled=True,
    )
    mlp_cols = lax.psum_scatter(
        row_sums.astype(jnp.bfloat16), "mlp", scatter_dimension=1, tiled=True
    ).astype(jnp.float32)
    final_state = state_cols + mlp_cols
    gain_final = lax.dynamic_slice_in_dim(final_gain, col_start, width_here)
    weight_cols = lax.dynamic_slice_in_dim(score_weight, col_start, width_here)
    final_square, final_dot = lax.psum(
        (
            jnp.sum(final_state * final_state, axis=1),
            jnp.sum(final_state * gain_final * weight_cols, axis=1),
        ),
        "mlp",
    )
    scores = final_dot * lax.rsqrt(final_square / width + norm_eps)
    return (final_state.astype(jnp.bfloat16), scores)


def solution(mesh):
    in_specs = (
        P("req", None, "mlp"),
        P("req", None, None, "mlp"),
        P("req", None, None, "mlp"),
        P("req", "mlp"),
        P("mlp", None),
        P(),
        P(None, ("req", "mlp")),
        P(None, ("req", "mlp")),
        P(("req", "mlp"), None),
        P(),
        P(),
        P(),
        P(),
        P(),
    )
    out_specs = (P("req", "mlp"), P("req"))
    return jax.shard_map(
        per_device, mesh=mesh, in_specs=in_specs, out_specs=out_specs, check_vma=False
    )
```

profile of v0, /device:TPU:0, one launch (start us, length us, event | category | flops | bytes accessed | tf_op | source)
XLA Modules:
  0.0 586.6 jit_solution(12017688734714034643)
XLA Ops:
  24.9 24.7 %fusion.43 = (bf16[1,4096,1,768]{3,2,1,0:T(2,128)(2,1)}, bf16[1,4096,1,768]{3,2,1,0:T(2,128)(2,1)}) fusion(bf16[1,4096,2,768]{3,2,1,0:T(2,128)(2,1)} %param.19), kind=kLoop, calls=%fused_computation.86 | loop fusion | bytes 25165824 | tf_op jit(solution)/shard_map/slice | solution.py:79
  49.5 27.2 %copy.122 = bf16[1,4096,1,768]{1,3,2,0:T(8,128)(2,1)} copy(bf16[1,4096,1,768]{3,2,1,0:T(2,128)(2,1)} %get-tuple-element.147) | data formatting | bytes 12582912 | tf_op jit(solution)/shard_map/slice | solution.py:79
  76.7 27.1 %copy.123 = bf16[1,4096,1,768]{1,3,2,0:T(8,128)(2,1)} copy(bf16[1,4096,1,768]{3,2,1,0:T(2,128)(2,1)} %get-tuple-element.148) | data formatting | bytes 12582912 | tf_op jit(solution)/shard_map/slice | solution.py:78
  103.8 25.7 %fusion.42 = (bf16[16,256,1,768]{3,2,1,0:T(2,128)(2,1)}, bf16[16,256,1,768]{3,2,1,0:T(2,128)(2,1)}) fusion(bf16[16,256,2,768]{3,2,1,0:T(2,128)(2,1)} %param.20), kind=kLoop, calls=%fused_computation.85 | loop fusion | bytes 25165824 | tf_op jit(solution)/shard_map/slice | solution.py:96
  129.5 29.0 %copy.127 = bf16[16,256,1,768]{1,3,0,2:T(8,128)(2,1)} copy(bf16[16,256,1,768]{3,2,1,0:T(2,128)(2,1)} %get-tuple-element.146) | data formatting | bytes 12582912 | tf_op jit(solution)/shard_map/slice | solution.py:95
  162.6 25.0 %all_gather.23 = f32[32,8,32]{2,1,0:T(8,128)S(1)} all-gather(f32[1,8,32]{2,1,0:T(8,128)S(1)} %copy.132), channel_id=1, replica_groups=mesh['req'=32,'mlp'=4] {'req'}, dimensions={0}, use_global_device_ids=true | all-gather | bytes 33792 | tf_op jit(solution)/shard_map/all_gather | solution.py:116
  191.3 4.2 broadcast_in_dim.62
  195.5 17.0 %while.22 = (s32[]{:T(128)}, f32[8,64,4096]{2,1,0:T(8,128)}, s32[]{:T(128)}, s32[]{:T(128)}, bf16[4096,8,96]{0,2,1:T(8,128)(2,1)}, /*index=5*/bf16[64,8,96]{2,0,...) while((s32[]{:T(128)}, f32[8,64,4096]{2,1,0:T(8,128)}, s32[]{:T(128)}, s32[]{:T(128)}, ...), condition=%wide.region_1.2_spmd, body=%wide.region_0.1_spmd.sunk | while | flops 50856964 | bytes 1935515 | solution.py:92
  212.6 3.8 reduce_max.27
  216.4 25.1 %all-gather = f32[256,64]{1,0:T(8,128)S(1)} all-gather(f32[8,64]{1,0:T(8,128)S(1)} %reduce_max.27), channel_id=2, replica_groups=mesh['req'=32,'mlp'=4] {'req'}, dimensions={0}, use_global_device_ids=true | all-gather | bytes 67584 | tf_op jit(solution)/shard_map/all_gather | solution.py:115
  241.6 24.8 %while.23 = (s32[]{:T(128)}, f32[64,8,96]{2,0,1:T(8,128)S(1)}, f32[8,64]{1,0:T(8,128)S(1)}, s32[]{:T(128)}, bf16[4096,8,96]{0,2,1:T(8,128)(2,1)}, /*index=5*/f32...) while((s32[]{:T(128)}, f32[64,8,96]{2,0,1:T(8,128)S(1)}, ...), condition=%wide.region_8.9_spmd, body=%wide.region_6.8_spmd.sunk | while | flops 51429380 | bytes 3290271 | solution.py:147
  267.6 29.0 %copy.138 = bf16[16,256,1,768]{1,3,0,2:T(8,128)(2,1)} copy(bf16[16,256,1,768]{3,2,1,0:T(2,128)(2,1)} %get-tuple-element.145) | data formatting | bytes 12582912 | tf_op jit(solution)/shard_map/slice | solution.py:96
  297.6 4.6 fusion.14
  303.2 26.2 %all-gather.1 = f32[256,64]{1,0:T(8,128)S(1)} all-gather(f32[8,64]{1,0:T(8,128)S(1)} %get-tuple-element.76), channel_id=3, replica_groups=mesh['req'=32,'mlp'=4] {'req'}, dimensions={0}, use_global_device_ids=true | all-gather | bytes 67584 | tf_op jit(solution)/shard_map/all_gather | solution.py:150
  329.7 4.1 fusion.32
  334.8 20.7 %reduce-scatter.4.cloned.1.call-done = f32[32,768]{1,0:T(8,128)} async-done(((f32[32,3072]{1,0:T(8,128)}), f32[32,768]{1,0:T(8,128)}) %reduce-scatter.4.cloned.1.call-update) | async-done | bytes 98320 | tf_op jit(solution)/shard_map/reduce_scatter | solution.py:198
  356.5 8.4 %psum.21 = f32[32]{0:T(128)S(1)} all-reduce(f32[32]{0:T(128)S(1)} %multiply_reduce_fusion.2), channel_id=1, replica_groups=mesh['req'=32,'mlp'=4] {'mlp'}, use_global_device_ids=true, to_apply=%region_13.14 | all-reduce | flops 32 | bytes 256 | tf_op jit(solution)/shard_map/psum | solution.py:200
  365.8 12.9 %all_gather.26 = bf16[32,3072]{1,0:T(8,128)(2,1)} all-gather(bf16[32,768]{1,0:T(8,128)(2,1)S(1)} %multiply_convert_fusion), channel_id=1, replica_groups=mesh['req'=32,'mlp'=4] {'mlp'}, dimensions={1}, use_global_device_ids=true | all-gather | bytes 245760 | tf_op jit(solution)/shard_map/all_gather | solution.py:205
  378.8 48.7 %all-gather.10.cloned.1.call-done = bf16[1024,3072]{1,0:T(8,128)(2,1)} async-done(((bf16[32,3072]{1,0:T(8,128)(2,1)}), bf16[1024,3072]{1,0:T(8,128)(2,1)}) %all-gather.10.cloned.1.call-update) | async-done | bytes 6291472 | tf_op jit(solution)/shard_map/all_gather | solution.py:206
  427.5 4.8 fusion.48
  432.3 11.1 %fusion.15 = f32[1024,3072]{1,0:T(8,128)} fusion(bf16[64,3072]{1,0:T(8,128)(2,1)S(1)} %copy-done, bf16[1024,3072]{1,0:T(8,128)(2,1)} %all-gather.10.cloned.1.call-done, bf16[3072,64]{0,1:T(8,128)(2,1)S(1)} %copy-done.4, f32[1024,64]{0,1:T(8,128)S(1)} %fusion.48), kind=kOutput, calls=%fused_computation.21 | convolution fusion | flops 805699584 | bytes 19922944 | tf_op jit(solution)/shard_map/dot_general | solution.py:211
  443.5 103.4 %reduce-scatter.6.cloned.1.call-done = f32[32,3072]{1,0:T(8,128)} async-done(((f32[1024,3072]{1,0:T(8,128)}), f32[32,3072]{1,0:T(8,128)}) %reduce-scatter.6.cloned.1.call-update) | async-done | bytes 393232 | tf_op jit(solution)/shard_map/reduce_scatter | solution.py:210
  550.1 19.1 %reduce-scatter.8.cloned.1.call-done = bf16[32,768]{1,0:T(8,128)(2,1)} async-done(((bf16[32,3072]{1,0:T(8,128)(2,1)}), bf16[32,768]{1,0:T(8,128)(2,1)}) %reduce-scatter.8.cloned.1.call-update) | async-done | bytes 49168 | tf_op jit(solution)/shard_map/reduce_scatter | solution.py:216
  570.7 8.4 %all-reduce = (f32[32]{0:T(128)S(1)}, f32[32]{0:T(128)S(1)}) all-reduce(f32[32]{0:T(128)S(1)} %get-tuple-element.114, f32[32]{0:T(128)S(1)} %get-tuple-element.113), channel_id=1, replica_groups=mesh['req'=32,'mlp'=4] {'mlp'}, use_global_device_ids=true, to_apply=%region_17.18 | all-reduce | flops 64 | bytes 512 | tf_op jit(solution)/shard_map/psum | solution.py:222
  (125 shorter events, 67.9 us)
Async XLA Ops:
  7.2 425.1 %copy-start = (bf16[64,3072]{1,0:T(8,128)(2,1)S(1)}, bf16[64,3072]{1,0:T(8,128)(2,1)}, u32[]{:S(2)}) copy-start(bf16[64,3072]{1,0:T(8,128)(2,1)} %param.26) | copy-start | bytes 1179652
  7.2 183.0 %all-gather.6.cloned.1.call-start = ((), (), s32[]{:S(2)}) async-start(), calls=%async_computation.3 | async-start | bytes 1622016 | tf_op jit(solution)/shard_map/all_gather | solution.py:61
  16.8 313.0 %all-gather.8.cloned.1.call-start = ((), (), s32[]{:S(2)}) async-start(), calls=%async_computation.4 | async-start | bytes 6488064 | tf_op jit(solution)/shard_map/all_gather | solution.py:149
  267.4 88.1 %reduce-scatter.4.cloned.1.call-start = ((), (), s32[]{:S(2)}) async-start(), calls=%async_computation.5 | async-start | bytes 491520 | tf_op jit(solution)/shard_map/reduce_scatter | solution.py:198
  297.6 57.9 %copy-start.2 = (bf16[32,768]{1,0:T(8,128)(2,1)S(1)}, bf16[32,768]{1,0:T(8,128)(2,1)}, u32[]{:S(2)}) copy-start(bf16[32,768]{1,0:T(8,128)(2,1)} %param.21) | copy-start | bytes 147460
  297.6 129.9 %copy-start.3 = (bf16[3072,64]{0,1:T(8,128)(2,1)S(1)}, bf16[3072,64]{0,1:T(8,128)(2,1)}, u32[]{:S(2)}) copy-start(bf16[3072,64]{0,1:T(8,128)(2,1)} %param.24) | copy-start | bytes 1179652
  329.7 102.6 %copy-start.4 = (bf16[3072,64]{0,1:T(8,128)(2,1)S(1)}, bf16[3072,64]{0,1:T(8,128)(2,1)}, u32[]{:S(2)}) copy-start(bf16[3072,64]{0,1:T(8,128)(2,1)} %param.25) | copy-start | bytes 1179652
  333.9 93.6 %all-gather.10.cloned.1.call-start = ((), (), s32[]{:S(2)}) async-start(), calls=%async_computation.6 | async-start | bytes 6488064 | tf_op jit(solution)/shard_map/all_gather | solution.py:206
  378.7 168.1 %reduce-scatter.6.cloned.1.call-start = ((), (), s32[]{:S(2)}) async-start(), calls=%async_computation.7 | async-start | bytes 12976128 | tf_op jit(solution)/shard_map/reduce_scatter | solution.py:210
  443.4 125.8 %copy-start.1 = (f32[32,768]{1,0:T(8,128)S(1)}, f32[32,768]{1,0:T(8,128)}, u32[]{:S(2)}) copy-start(f32[32,768]{1,0:T(8,128)} %reduce-scatter.4.cloned.1.call-done) | copy-start | bytes 294916
  443.4 125.8 %reduce-scatter.8.cloned.1.call-start = ((), (), s32[]{:S(2)}) async-start(), calls=%async_computation.8 | async-start | bytes 245760 | tf_op jit(solution)/shard_map/reduce_scatter | solution.py:216
Sparse Core Ops, SparseCore 0:
  16.9 45.6 all-gather.5
  267.5 51.9 all-gather.7
  334.0 21.3 reduce-scatter.3
  378.9 48.5 all-gather.9
  443.5 103.2 reduce-scatter.5
  549.0 20.1 reduce-scatter.7
where the time goes:
time: 591 us; the launch traced here: 587 us
  waiting for transfers between devices  192 us (32%)
  local copies, waits for them, and re-layouts  179 us (30%)
  blocking collectives  106 us (18%)
  matrix products  59.6 us (10%)
  between operations  25.1 us (4%)
  other arithmetic  24.6 us (4%)
    reduce_scatter x1, waiting for transfers between devices, per_device(): lax.psum_scatter(jnp.dot(hidden_all, w_down, preferred_element_type=jnp.f...  103 us
    slice x2, local copies, waits for them, and re-layouts, per_device(): tail_cache[:, :, 1].reshape(conts_here, tail_cap, heads_here, HD)  54.7 us
    slice x2, local copies, waits for them, and re-layouts, per_device(): cache_values = prompt_cache[0, :, 1].reshape(span, heads_here, HD)  51.8 us
    all_gather x1, waiting for transfers between devices, per_device(): piece = lax.all_gather(normed_full, 'req', axis=0, tiled=True)  48.7 us
    slice x1, local copies, waits for them, and re-layouts, per_device(): tail_cache[:, :, 0].reshape(conts_here, tail_cap, heads_here, HD)  29 us
    slice x1, local copies, waits for them, and re-layouts, per_device(): cache_keys = prompt_cache[0, :, 0].reshape(span, heads_here, HD)  27.1 us
    all_gather x1, blocking collectives, per_device(): lax.all_gather(owner_total[None], 'req', axis=0, tiled=True)  26.2 us
    all_gather x1, blocking collectives, per_device(): lax.all_gather(prefix_max[None], 'req', axis=0, tiled=True)  25.1 us
  transfers between devices with their start and end apart: 6, of which 4 were waited for; matrix products, arithmetic and copies ran while one was open for 30% of the time, Pallas kernels for 0%

commit v1 on v0

v1 whole, which is shorter than its diff:
```python
import math

import jax
import jax.numpy as jnp
from jax import lax
from jax.sharding import PartitionSpec as P

HD = 96


norm_eps = 1e-05
masked_value = -1e30


def rotary(values, position):
    half_dim = HD // 2
    freqs = 10000.0 ** (-(jnp.arange(half_dim, dtype=jnp.float32) * 2.0) / HD)
    angles = position.astype(jnp.float32)[..., None] * freqs
    cosine = jnp.cos(angles)[..., None, :]
    sine = jnp.sin(angles)[..., None, :]
    first = values[..., :half_dim]
    second = values[..., half_dim:]
    return jnp.concatenate(
        [first * cosine - second * sine, second * cosine + first * sine], axis=-1
    )


def per_device(
    new_qkv,
    prompt_cache,
    tail_cache,
    residual,
    w_out,
    mlp_gain,
    w_gate,
    w_up,
    w_down,
    final_gain,
    score_weight,
    slot_part,
    prompt_len,
    tail_len,
):
    req_count = lax.axis_size("req")
    req_index = lax.axis_index("req")
    mlp_index = lax.axis_index("mlp")
    rows_here = new_qkv.shape[0]
    width_here = new_qkv.shape[2]
    heads_here = width_here // HD
    conts_here = rows_here // 2
    width = w_out.shape[1]
    score_scale = 1.0 / math.sqrt(HD)
    own_prompt = req_index // 2
    tail_here = lax.dynamic_slice_in_dim(tail_len, req_index * conts_here, conts_here)
    plen_here = lax.dynamic_index_in_dim(prompt_len, own_prompt, 0, keepdims=False)
    position = plen_here + tail_here[:, None] + jnp.arange(2, dtype=jnp.int32)[None, :]
    block = new_qkv.reshape(conts_here, 2, 3, heads_here, HD)
    query = rotary(block[:, :, 0].astype(jnp.float32), position).astype(jnp.bfloat16)
    key_new = rotary(block[:, :, 1].astype(jnp.float32), position).astype(jnp.bfloat16)
    value_new = block[:, :, 2]
    gathered = lax.all_gather(query.reshape(rows_here, width_here), "req", axis=0, tiled=True)
    slot_ids = jnp.arange(req_count, dtype=jnp.int32)
    slot_of = jnp.sum(
        jnp.where(slot_part[None, :] == slot_ids[:, None], slot_ids[None, :], 0), axis=1
    )
    held_part = lax.dynamic_index_in_dim(slot_part, req_index, 0, keepdims=False)
    owned_prompt = held_part // 2
    held_half = held_part % 2
    span = prompt_cache.shape[1]
    owned_rows = 2 * rows_here
    q_owned = lax.dynamic_slice_in_dim(gathered, owned_prompt * owned_rows, owned_rows, 0).reshape(
        owned_rows, heads_here, HD
    )
    owned_len = lax.dynamic_index_in_dim(prompt_len, owned_prompt, 0, keepdims=False)
    valid_count = jnp.clip(owned_len - held_half * span, 0, span)
    block_len = min(512, span)
    block_count = (valid_count + block_len - 1) // block_len
    cache_keys = prompt_cache[0, :, 0].reshape(span, heads_here, HD)
    cache_values = prompt_cache[0, :, 1].reshape(span, heads_here, HD)

    def score_block(number, buffer):
        key_block = lax.dynamic_slice_in_dim(cache_keys, number * block_len, block_len, 0)
        block_scores = (
            jnp.einsum("rhd,khd->hrk", q_owned, key_block, preferred_element_type=jnp.float32)
            * score_scale
        )
        places = number * block_len + jnp.arange(block_len, dtype=jnp.int32)
        block_scores = jnp.where(places[None, None, :] < valid_count, block_scores, masked_value)
        return lax.dynamic_update_slice_in_dim(buffer, block_scores, number * block_len, 2)

    empty_scores = jnp.full((heads_here, owned_rows, span), masked_value, jnp.float32)
    prefix_scores = lax.fori_loop(0, block_count, score_block, empty_scores)
    prefix_max = jnp.max(prefix_scores, axis=2)

    def value_block(number, carry):
        numer, totals = carry
        score_part = lax.dynamic_slice_in_dim(prefix_scores, number * block_len, block_len, 2)
        weights = jnp.exp(score_part - prefix_max[:, :, None])
        value_part = lax.dynamic_slice_in_dim(cache_values, number * block_len, block_len, 0)
        numer = numer + jnp.einsum(
            "hrk,khd->rhd",
            weights.astype(jnp.bfloat16),
            value_part,
            preferred_element_type=jnp.float32,
        )
        return (numer, totals + jnp.sum(weights, axis=2))

    start_carry = (
        jnp.zeros((owned_rows, heads_here, HD), jnp.float32),
        jnp.zeros((heads_here, owned_rows), jnp.float32),
    )
    owner_numer, owner_total = lax.fori_loop(0, block_count, value_block, start_carry)
    packed = jnp.concatenate(
        [
            owner_numer.reshape(owned_rows, width_here),
            jnp.transpose(owner_total),
            jnp.transpose(prefix_max),
        ],
        axis=1,
    )
    packed_all = lax.all_gather(packed[None], "req", axis=0, tiled=True)
    row_offset = req_index % 2 * rows_here
    slot_first = lax.dynamic_index_in_dim(slot_of, 2 * own_prompt, 0, keepdims=False)
    slot_second = lax.dynamic_index_in_dim(slot_of, 2 * own_prompt + 1, 0, keepdims=False)

    def part_of(slot):
        piece = lax.dynamic_slice_in_dim(
            lax.dynamic_index_in_dim(packed_all, slot, 0, keepdims=False), row_offset, rows_here, 0
        )
        numer = piece[:, :width_here].reshape(rows_here, heads_here, HD)
        total = piece[:, width_here : width_here + heads_here]
        top = piece[:, width_here + heads_here :]
        return numer, total, top

    numer_first, total_first, max_first = part_of(slot_first)
    numer_second, total_second, max_second = part_of(slot_second)

    tail_cap = tail_cache.shape[1]
    tail_keys = tail_cache[:, :, 0].reshape(conts_here, tail_cap, heads_here, HD)
    tail_values = tail_cache[:, :, 1].reshape(conts_here, tail_cap, heads_here, HD)
    s_tail = (
        jnp.einsum("cthd,cjhd->chtj", query, tail_keys, preferred_element_type=jnp.float32)
        * score_scale
    )
    s_tail = jnp.where(
        jnp.arange(tail_cap)[None, None, None, :] < tail_here[:, None, None, None],
        s_tail,
        masked_value,
    )
    s_new = (
        jnp.einsum("cthd,cuhd->chtu", query, key_new, preferred_element_type=jnp.float32)
        * score_scale
    )
    causal = jnp.arange(2)[None, :] <= jnp.arange(2)[:, None]
    s_new = jnp.where(causal[None, None, :, :], s_new, masked_value)
    tail_max = jnp.maximum(jnp.max(s_tail, -1), jnp.max(s_new, -1))
    w_tail = jnp.exp(s_tail - tail_max[..., None])
    w_new = jnp.exp(s_new - tail_max[..., None])
    numer_tail = jnp.einsum(
        "chtj,cjhd->cthd",
        w_tail.astype(jnp.bfloat16),
        tail_values,
        preferred_element_type=jnp.float32,
    )
    numer_tail = numer_tail + jnp.einsum(
        "chtu,cuhd->cthd", w_new.astype(jnp.bfloat16), value_new, preferred_element_type=jnp.float32
    )
    numer_tail = numer_tail.reshape(rows_here, heads_here, HD)
    total_tail = jnp.transpose(jnp.sum(w_tail, -1) + jnp.sum(w_new, -1), (0, 2, 1)).reshape(
        rows_here, heads_here
    )
    max_tail = jnp.transpose(tail_max, (0, 2, 1)).reshape(rows_here, heads_here)
    row_max = jnp.maximum(jnp.maximum(max_first, max_second), max_tail)
    scale_first = jnp.exp(max_first - row_max)
    scale_second = jnp.exp(max_second - row_max)
    scale_tail = jnp.exp(max_tail - row_max)
    row_total = total_first * scale_first + total_second * scale_second + total_tail * scale_tail
    row_numer = (
        numer_first * scale_first[..., None]
        + numer_second * scale_second[..., None]
        + numer_tail * scale_tail[..., None]
    )
    attn = (row_numer / row_total[:, :, None]).astype(jnp.bfloat16).reshape(rows_here, width_here)
    residual_full = lax.all_gather(residual, "mlp", axis=1, tiled=True)
    projected = lax.psum(jnp.dot(attn, w_out, preferred_element_type=jnp.float32), "mlp")
    state = residual_full.astype(jnp.float32) + projected
    mean_square = jnp.mean(state * state, axis=1, keepdims=True)
    normed = (state * lax.rsqrt(mean_square + norm_eps) * mlp_gain).astype(jnp.bfloat16)
    mlp_count = lax.axis_size("mlp")
    share = rows_here // mlp_count
    normed_share = lax.dynamic_slice_in_dim(normed, mlp_index * share, share, 0)
    piece = lax.all_gather(normed_share, "req", axis=0, tiled=True)
    gate_w = lax.all_gather(w_gate, "mlp", axis=1, tiled=True)
    up_w = lax.all_gather(w_up, "mlp", axis=1, tiled=True)
    down_w = lax.all_gather(w_down, "mlp", axis=0, tiled=True)
    gate = jnp.dot(piece, gate_w, preferred_element_type=jnp.float32)
    upper = jnp.dot(piece, up_w, preferred_element_type=jnp.float32)
    hidden_all = (jax.nn.silu(gate) * upper).astype(jnp.bfloat16)
    row_sums = lax.psum_scatter(
        jnp.dot(hidden_all, down_w, preferred_element_type=jnp.float32),
        "req",
        scatter_dimension=0,
        tiled=True,
    )
    state_share = lax.dynamic_slice_in_dim(state, mlp_index * share, share, 0)
    final_share = state_share + row_sums
    final_square = jnp.mean(final_share * final_share, axis=1)
    final_dot = jnp.sum(final_share * final_gain * score_weight, axis=1)
    score_share = final_dot * lax.rsqrt(final_square + norm_eps)
    scores = lax.all_gather(score_share, "mlp", axis=0, tiled=True)
    out_rows = lax.all_to_all(
        final_share.astype(jnp.bfloat16), "mlp", split_axis=1, concat_axis=0, tiled=True
    )
    return (out_rows, scores)


def solution(mesh):
    in_specs = (
        P("req", None, "mlp"),
        P("req", None, None, "mlp"),
        P("req", None, None, "mlp"),
        P("req", "mlp"),
        P("mlp", None),
        P(),
        P(None, ("req", "mlp")),
        P(None, ("req", "mlp")),
        P(("req", "mlp"), None),
        P(),
        P(),
        P(),
        P(),
        P(),
    )
    out_specs = (P("req", "mlp"), P("req"))
    return jax.shard_map(
        per_device, mesh=mesh, in_specs=in_specs, out_specs=out_specs, check_vma=False
    )
```

time: 591 us -> 551 us (0.932)
  blocking collectives: 106 us -> 25.1 us
  waiting for transfers between devices: 192 us -> 254 us
  matrix products: 59.6 us -> 43.2 us
    all_gather x2 -> x5, waiting for transfers between devices: 48.7 us -> 125 us  [the longest x1 46 us: per_device(): piece = lax.all_gather(normed_share, 'req', axis=0, tiled=True)]
    all_gather x4 -> x1, blocking collectives: 89.2 us -> 13.7 us  [per_device(): residual_full = lax.all_gather(residual, 'mlp', axis=1, tiled=True)]
    reduce_scatter x3 -> x1, waiting for transfers between devices: 143 us -> 79.1 us  [per_device(): lax.psum_scatter(jnp.dot(hidden_all, down_w, preferred_element_type=jnp.f...]
    psum x0 -> x1, waiting for transfers between devices: none -> 47.9 us  [per_device(): lax.psum(jnp.dot(attn, w_out, preferred_element_type=jnp.float32), 'mlp')]
    psum x2 -> x0, blocking collectives: 16.8 us -> none  [the longest x1 8.44 us: per_device(): lax.psum((jnp.sum(final_state * final_state, axis=1), jnp.sum(final_state...]
    unnamed x0 -> x1, blocking collectives: none -> 11.4 us
    dot_general x3, matrix products: 20 us -> 12.3 us  [the longest x1 5.84 us: per_device(): jnp.dot(hidden_all, down_w, preferred_element_type=jnp.float32)]
    dot_general x7 -> x5, matrix products: 17 us -> 12.1 us  [score_block(): jnp.einsum('rhd,khd->hrk', q_owned, key_block, preferred_element_type=jnp...]
  transfers between devices with their start and end apart: 6 -> 9, of which waited for: 4 -> 6; matrix products, arithmetic and copies ran while one was open for 30% -> 33% of each run, Pallas kernels for 0% -> 0%
where the time goes in v1:
time: 551 us; the launch traced here: 547 us
  waiting for transfers between devices  254 us (46%)
  local copies, waits for them, and re-layouts  178 us (32%)
  matrix products  43.2 us (8%)
  blocking collectives  25.1 us (5%)
  between operations  22.4 us (4%)
  other arithmetic  19.5 us (4%)
    reduce_scatter x1, waiting for transfers between devices, per_device(): lax.psum_scatter(jnp.dot(hidden_all, down_w, preferred_element_type=jnp.f...  79.1 us
    slice x2, local copies, waits for them, and re-layouts, per_device(): tail_cache[:, :, 1].reshape(conts_here, tail_cap, heads_here, HD)  54.8 us
    slice x2, local copies, waits for them, and re-layouts, per_device(): cache_values = prompt_cache[0, :, 1].reshape(span, heads_here, HD)  51.7 us
    psum x1, waiting for transfers between devices, per_device(): lax.psum(jnp.dot(attn, w_out, preferred_element_type=jnp.float32), 'mlp')  47.9 us
    all_gather x1, waiting for transfers between devices, per_device(): piece = lax.all_gather(normed_share, 'req', axis=0, tiled=True)  46 us
    slice x1, local copies, waits for them, and re-layouts, per_device(): tail_cache[:, :, 0].reshape(conts_here, tail_cap, heads_here, HD)  29.2 us
    all_gather x1, waiting for transfers between devices, per_device(): down_w = lax.all_gather(w_down, 'mlp', axis=0, tiled=True)  28.5 us
    slice x1, local copies, waits for them, and re-layouts, per_device(): cache_keys = prompt_cache[0, :, 0].reshape(span, heads_here, HD)  27.2 us
  transfers between devices with their start and end apart: 9, of which 6 were waited for; matrix products, arithmetic and copies ran while one was open for 33% of the time, Pallas kernels for 0%

profile of v1, /device:TPU:0, one launch (start us, length us, event | category | flops | bytes accessed | tf_op | source)
XLA Modules:
  0.0 547.1 jit_solution(2006875817612300921)
XLA Ops:
  17.5 24.7 %fusion.44 = (bf16[1,4096,1,768]{3,2,1,0:T(2,128)(2,1)}, bf16[1,4096,1,768]{3,2,1,0:T(2,128)(2,1)}) fusion(bf16[1,4096,2,768]{3,2,1,0:T(2,128)(2,1)} %param.19), kind=kLoop, calls=%fused_computation.90 | loop fusion | bytes 25165824 | tf_op jit(solution)/shard_map/slice | solution.py:79
  42.2 27.2 %copy.87 = bf16[1,4096,1,768]{1,3,2,0:T(8,128)(2,1)} copy(bf16[1,4096,1,768]{3,2,1,0:T(2,128)(2,1)} %get-tuple-element.154) | data formatting | bytes 12582912 | tf_op jit(solution)/shard_map/slice | solution.py:78
  69.4 27.0 %copy.86 = bf16[1,4096,1,768]{1,3,2,0:T(8,128)(2,1)} copy(bf16[1,4096,1,768]{3,2,1,0:T(2,128)(2,1)} %get-tuple-element.153) | data formatting | bytes 12582912 | tf_op jit(solution)/shard_map/slice | solution.py:79
  97.5 4.2 broadcast_in_dim.60
  101.8 12.1 %while.22 = (s32[]{:T(128)}, f32[8,64,4096]{2,1,0:T(8,128)}, s32[]{:T(128)}, s32[]{:T(128)}, bf16[4096,8,96]{0,2,1:T(8,128)(2,1)}, /*index=5*/bf16[64,8,96]{2,0,...) while((s32[]{:T(128)}, f32[8,64,4096]{2,1,0:T(8,128)}, s32[]{:T(128)}, s32[]{:T(128)}, ...), condition=%wide.region_1.2_spmd, body=%wide.region_0.1_spmd.sunk | while | flops 50856964 | bytes 1935515 | solution.py:92
  113.9 3.8 reduce_max.27
  117.8 17.7 %while.23 = (s32[]{:T(128)}, f32[64,8,96]{2,0,1:T(8,128)S(1)}, f32[8,64]{1,0:T(8,128)S(1)}, s32[]{:T(128)}, bf16[4096,8,96]{0,2,1:T(8,128)(2,1)}, /*index=5*/f32...) while((s32[]{:T(128)}, f32[64,8,96]{2,0,1:T(8,128)S(1)}, ...), condition=%wide.region_5.6_spmd, body=%wide.region_3.5_spmd.sunk | while | flops 51429380 | bytes 3290271 | solution.py:112
  140.1 25.7 %fusion.43 = (bf16[16,256,1,768]{3,2,1,0:T(2,128)(2,1)}, bf16[16,256,1,768]{3,2,1,0:T(2,128)(2,1)}) fusion(bf16[16,256,2,768]{3,2,1,0:T(2,128)(2,1)} %param.20), kind=kLoop, calls=%fused_computation.89 | loop fusion | bytes 25165824 | tf_op jit(solution)/shard_map/slice | solution.py:140
  165.9 29.2 %copy.94 = bf16[16,256,1,768]{1,3,0,2:T(8,128)(2,1)} copy(bf16[16,256,1,768]{3,2,1,0:T(2,128)(2,1)} %get-tuple-element.152) | data formatting | bytes 12582912 | tf_op jit(solution)/shard_map/slice | solution.py:139
  196.1 4.0 fusion.48
  200.5 29.1 %copy.99 = bf16[16,256,1,768]{1,3,0,2:T(8,128)(2,1)} copy(bf16[16,256,1,768]{3,2,1,0:T(2,128)(2,1)} %get-tuple-element.151) | data formatting | bytes 12582912 | tf_op jit(solution)/shard_map/slice | solution.py:140
  229.8 4.6 fusion.15
  238.7 4.0 fusion.34
  243.3 13.7 %all_gather.24 = bf16[32,3072]{1,0:T(8,128)(2,1)S(1)} all-gather(bf16[32,768]{1,0:T(8,128)(2,1)S(1)} %copy-done), channel_id=1, replica_groups=mesh['req'=32,'mlp'=4] {'mlp'}, dimensions={1}, use_global_device_ids=true | all-gather | bytes 245760 | tf_op jit(solution)/shard_map/all_gather | solution.py:184
  257.0 47.9 %all-reduce.3.cloned.1.call-done = f32[32,3072]{1,0:T(8,128)} async-done(((f32[32,3072]{1,0:T(8,128)}), f32[32,3072]{1,0:T(8,128)}) %all-reduce.3.cloned.1.call-update) | async-done | bytes 393232 | tf_op jit(solution)/shard_map/psum | solution.py:185
  308.2 25.4 %all-gather.12.cloned.1.call-done = bf16[3072,256]{0,1:T(8,128)(2,1)} async-done(((bf16[3072,64]{0,1:T(8,128)(2,1)}), bf16[3072,256]{0,1:T(8,128)(2,1)}) %all-gather.12.cloned.1.call-update) | async-done | bytes 1572880 | tf_op jit(solution)/shard_map/all_gather | solution.py:193
  333.6 46.0 %all-gather.10.cloned.1.call-done = bf16[256,3072]{1,0:T(8,128)(2,1)} async-done(((bf16[8,3072]{1,0:T(8,128)(2,1)}), bf16[256,3072]{1,0:T(8,128)(2,1)}) %all-gather.10.cloned.1.call-update) | async-done | bytes 1572880 | tf_op jit(solution)/shard_map/all_gather | solution.py:192
  379.6 2.5 fusion.49
  382.1 25.2 %all-gather.14.cloned.1.call-done = bf16[3072,256]{0,1:T(8,128)(2,1)} async-done(((bf16[3072,64]{0,1:T(8,128)(2,1)}), bf16[3072,256]{0,1:T(8,128)(2,1)}) %all-gather.14.cloned.1.call-update) | async-done | bytes 1572880 | tf_op jit(solution)/shard_map/all_gather | solution.py:194
  407.3 28.5 %all-gather.16.cloned.1.call-done = bf16[256,3072]{1,0:T(8,128)(2,1)} async-done(((bf16[64,3072]{1,0:T(8,128)(2,1)}), bf16[256,3072]{1,0:T(8,128)(2,1)}) %all-gather.16.cloned.1.call-update) | async-done | bytes 1572880 | tf_op jit(solution)/shard_map/all_gather | solution.py:195
  435.8 5.8 %fusion.14 = f32[256,3072]{1,0:T(8,128)} fusion(bf16[256,3072]{1,0:T(8,128)(2,1)} %all-gather.16.cloned.1.call-done, bf16[256,3072]{1,0:T(8,128)(2,1)} %all-gather.10.cloned.1.call-done, bf16[3072,256]{0,1:T(8,128)(2,1)} %all-gather.14.cloned.1.call-done, f32[256,256]{1,0:T(8,128)S(1)} %fusion.49), kind=kOutput, calls=%fused_computation.19 | convolution fusion | flops 805699584 | bytes 8126464 | tf_op jit(solution)/shard_map/dot_general | solution.py:200
  442.9 79.1 %reduce-scatter.2.cloned.1.call-done = f32[8,3072]{1,0:T(8,128)} async-done(((f32[256,3072]{1,0:T(8,128)}), f32[8,3072]{1,0:T(8,128)}) %reduce-scatter.2.cloned.1.call-update) | async-done | bytes 98320 | tf_op jit(solution)/shard_map/reduce_scatter | solution.py:199
  523.7 4.4 all-to-all-start
  528.2 11.4 %all-reduce = f32[32]{0:T(128)} all-reduce(f32[32]{0:T(128)S(1)} %multiply_dynamic-update-slice_fusion), channel_id=1, replica_groups=mesh['req'=32,'mlp'=4] {'mlp'}, use_global_device_ids=true, to_apply=%add | all-reduce | flops 32 | bytes 256
  (119 shorter events, 51.1 us)
Async XLA Ops:
  7.2 89.3 %all-gather.8.cloned.1.call-start = ((), (), s32[]{:S(2)}) async-start(), calls=%async_computation.2 | async-start | bytes 1622016 | tf_op jit(solution)/shard_map/all_gather | solution.py:61
  16.8 220.0 %all-gather.18.cloned.1.call-start = ((), (), s32[]{:S(2)}) async-start(), calls=%async_computation.9 | async-start | bytes 7569408 | tf_op jit(solution)/shard_map/all_gather | solution.py:121
  117.8 19.0 %copy-start.4 = (s32[32]{0:T(128)S(1)}, s32[32]{0:T(128)}, u32[]{:S(2)}) copy-start(s32[32]{0:T(128)} %param.29) | copy-start | bytes 388
  136.8 168.1 %all-reduce.3.cloned.1.call-start = ((), (), s32[]{:S(2)}) async-start(), calls=%async_computation.3 | async-start | bytes 786432 | tf_op jit(solution)/shard_map/psum | solution.py:185
  234.4 8.9 %copy-start = (bf16[32,768]{1,0:T(8,128)(2,1)S(1)}, bf16[32,768]{1,0:T(8,128)(2,1)}, u32[]{:S(2)}) copy-start(bf16[32,768]{1,0:T(8,128)(2,1)} %param.21) | copy-start | bytes 147460
  234.4 71.7 %copy-start.3 = (f32[3072]{0:T(1024)S(1)}, f32[3072]{0:T(1024)}, u32[]{:S(2)}) copy-start(f32[3072]{0:T(1024)} %param.23) | copy-start | bytes 36868
  242.7 90.9 %all-gather.12.cloned.1.call-start = ((), (), s32[]{:S(2)}) async-start(), calls=%async_computation.5 | async-start | bytes 1966080 | tf_op jit(solution)/shard_map/all_gather | solution.py:193
  243.3 136.3 %all-gather.10.cloned.1.call-start = ((), (), s32[]{:S(2)}) async-start(), calls=%async_computation.4 | async-start | bytes 1622016 | tf_op jit(solution)/shard_map/all_gather | solution.py:192
  306.8 100.5 %all-gather.14.cloned.1.call-start = ((), (), s32[]{:S(2)}) async-start(), calls=%async_computation.6 | async-start | bytes 1966080 | tf_op jit(solution)/shard_map/all_gather | solution.py:194
  307.4 128.4 %all-gather.16.cloned.1.call-start = ((), (), s32[]{:S(2)}) async-start(), calls=%async_computation.7 | async-start | bytes 1966080 | tf_op jit(solution)/shard_map/all_gather | solution.py:195
  308.2 213.9 %reduce-scatter.2.cloned.1.call-start = ((), (), s32[]{:S(2)}) async-start(), calls=%async_computation.8 | async-start | bytes 3244032 | tf_op jit(solution)/shard_map/reduce_scatter | solution.py:199
  382.1 59.6 %copy-start.5 = (u32[128]{0:T(128)S(1)}, u32[128]{0:T(128)}, u32[]{:S(2)}) copy-start(u32[128]{0:T(128)} %constant.186) | copy-start | bytes 1540
  382.1 139.9 %copy-start.1 = (f32[3072]{0:T(1024)S(1)}, f32[3072]{0:T(1024)}, u32[]{:S(2)}) copy-start(f32[3072]{0:T(1024)} %param.28) | copy-start | bytes 36868
  382.1 139.9 %copy-start.2 = (f32[3072]{0:T(1024)S(1)}, f32[3072]{0:T(1024)}, u32[]{:S(2)}) copy-start(f32[3072]{0:T(1024)} %param.27) | copy-start | bytes 36868
  523.7 16.0 %all-to-all-start = ((bf16[8,4,768]{2,0,1:T(8,128)(2,1)}), bf16[8,4,768]{2,0,1:T(8,128)(2,1)S(1)}, u32[]{:S(2)}, u32[]{:S(2)}) async-start(bf16[8,4,768]{2,0,1:T(8,128)(2,1)} %bitcast.26), calls=%async_computation.1 | async-start | bytes 98304 | tf_op jit(solution)/shard_map/all_to_all | solution.py:211
Sparse Core Ops, SparseCore 0:
  16.9 45.5 all-gather.7
  136.9 70.3 all-gather.17
  242.8 62.0 all-reduce.2
  306.5 27.0 all-gather.11
  336.5 43.0 all-gather.9
  381.2 26.1 all-gather.13
  409.1 26.6 all-gather.15
  441.8 80.1 reduce-scatter.1

commit v2 on v1

--- a/solution.py
+++ b/solution.py
@@ -59,6 +59,9 @@
     key_new = rotary(block[:, :, 1].astype(jnp.float32), position).astype(jnp.bfloat16)
     value_new = block[:, :, 2]
     gathered = lax.all_gather(query.reshape(rows_here, width_here), "req", axis=0, tiled=True)
+    weights_cat = jnp.concatenate([w_gate, w_up, jnp.transpose(w_down)], axis=1)
+    weights_all = lax.all_gather(weights_cat, "mlp", axis=0, tiled=False)
+    gathered, weights_all = lax.optimization_barrier((gathered, weights_all))
     slot_ids = jnp.arange(req_count, dtype=jnp.int32)
     slot_of = jnp.sum(
         jnp.where(slot_part[None, :] == slot_ids[:, None], slot_ids[None, :], 0), axis=1
@@ -190,14 +193,16 @@
     share = rows_here // mlp_count
     normed_share = lax.dynamic_slice_in_dim(normed, mlp_index * share, share, 0)
     piece = lax.all_gather(normed_share, "req", axis=0, tiled=True)
-    gate_w = lax.all_gather(w_gate, "mlp", axis=1, tiled=True)
-    up_w = lax.all_gather(w_up, "mlp", axis=1, tiled=True)
-    down_w = lax.all_gather(w_down, "mlp", axis=0, tiled=True)
-    gate = jnp.dot(piece, gate_w, preferred_element_type=jnp.float32)
-    upper = jnp.dot(piece, up_w, preferred_element_type=jnp.float32)
+    hidden_here = w_gate.shape[1]
+    gate_w = weights_all[:, :, :hidden_here]
+    up_w = weights_all[:, :, hidden_here : 2 * hidden_here]
+    down_w = weights_all[:, :, 2 * hidden_here :]
+    gate = jnp.einsum("rk,mkj->rmj", piece, gate_w, preferred_element_type=jnp.float32)
+    upper = jnp.einsum("rk,mkj->rmj", piece, up_w, preferred_element_type=jnp.float32)
     hidden_all = (jax.nn.silu(gate) * upper).astype(jnp.bfloat16)
+    down_sum = jnp.einsum("rmj,mfj->rf", hidden_all, down_w, preferred_element_type=jnp.float32)
     row_sums = lax.psum_scatter(
-        jnp.dot(hidden_all, down_w, preferred_element_type=jnp.float32),
+        down_sum,
         "req",
         scatter_dimension=0,
         tiled=True,

time: 551 us -> 481 us (0.87)
  waiting for transfers between devices: 254 us -> 198 us
  matrix products: 43.2 us -> 20.8 us
  local copies, waits for them, and re-layouts: 178 us -> 193 us
    all_gather x3 -> x1, waiting for transfers between devices: 79.1 us -> 0.01 us  [per_device(): weights_all = lax.all_gather(weights_cat, 'mlp', axis=0, tiled=False)]
    psum x1, waiting for transfers between devices: 47.9 us -> 76.6 us  [per_device(): lax.psum(jnp.dot(attn, w_out, preferred_element_type=jnp.float32), 'mlp')]
    dot_general x12 -> x1, matrix products: 30.1 us -> 3.71 us  [per_device(): jnp.einsum('rmj,mfj->rf', hidden_all, down_w, preferred_element_type=jnp....]
    all_gather x0 -> x1, local copies, waits for them, and re-layouts: none -> 8.26 us  [per_device(): weights_all = lax.all_gather(weights_cat, 'mlp', axis=0, tiled=False)]
    reduce_sum x5 -> x0, other arithmetic: 7.79 us -> none  [value_block(): return (numer, totals + jnp.sum(weights, axis=2))]
    all_gather x1, waiting for transfers between devices: 46 us -> 38.2 us  [per_device(): piece = lax.all_gather(normed_share, 'req', axis=0, tiled=True)]
  transfers between devices with their start and end apart: 9 -> 7, of which waited for: 6 -> 4; matrix products, arithmetic and copies ran while one was open for 33% -> 41% of each run, Pallas kernels for 0% -> 0%
where the time goes in v2:
time: 481 us; the launch traced here: 476 us
  waiting for transfers between devices  198 us (41%)
  local copies, waits for them, and re-layouts  193 us (40%)
  blocking collectives  24 us (5%)
  between operations  22.4 us (5%)
  matrix products  20.8 us (4%)
  other arithmetic  14 us (3%)
  starting transfers between devices  4.86 us (1%)
    reduce_scatter x1, waiting for transfers between devices, per_device(): lax.psum_scatter(down_sum, 'req', scatter_dimension=0, tiled=True)  78.5 us
    psum x1, waiting for transfers between devices, per_device(): lax.psum(jnp.dot(attn, w_out, preferred_element_type=jnp.float32), 'mlp')  76.6 us
    slice x2, local copies, waits for them, and re-layouts, per_device(): tail_cache[:, :, 1].reshape(conts_here, tail_cap, heads_here, HD)  55 us
    slice x2, local copies, waits for them, and re-layouts, per_device(): cache_values = prompt_cache[0, :, 1].reshape(span, heads_here, HD)  51.9 us
    all_gather x1, waiting for transfers between devices, per_device(): piece = lax.all_gather(normed_share, 'req', axis=0, tiled=True)  38.2 us
    slice x1, local copies, waits for them, and re-layouts, per_device(): tail_cache[:, :, 0].reshape(conts_here, tail_cap, heads_here, HD)  29 us
    slice x1, local copies, waits for them, and re-layouts, per_device(): cache_keys = prompt_cache[0, :, 0].reshape(span, heads_here, HD)  27.1 us
    all_gather x1, blocking collectives, per_device(): residual_full = lax.all_gather(residual, 'mlp', axis=1, tiled=True)  12.6 us
  transfers between devices with their start and end apart: 7, of which 4 were waited for; matrix products, arithmetic and copies ran while one was open for 41% of the time, Pallas kernels for 0%

profile of v2, /device:TPU:0, one launch (start us, length us, event | category | flops | bytes accessed | tf_op | source)
XLA Modules:
  0.0 476.3 jit_solution(7769775506889511861)
XLA Ops:
  7.2 2.3 pad_maximum_fusion
  19.9 24.8 %fusion.38 = (bf16[1,4096,1,768]{3,2,1,0:T(2,128)(2,1)}, bf16[1,4096,1,768]{3,2,1,0:T(2,128)(2,1)}) fusion(bf16[1,4096,2,768]{3,2,1,0:T(2,128)(2,1)} %param.19), kind=kLoop, calls=%fused_computation.86 | loop fusion | bytes 25165824 | tf_op jit(solution)/shard_map/slice | solution.py:82
  44.7 27.1 %copy.98 = bf16[1,4096,1,768]{1,3,2,0:T(8,128)(2,1)} copy(bf16[1,4096,1,768]{3,2,1,0:T(2,128)(2,1)} %get-tuple-element.158) | data formatting | bytes 12582912 | tf_op jit(solution)/shard_map/slice | solution.py:81
  71.8 27.1 %copy.97 = bf16[1,4096,1,768]{1,3,2,0:T(8,128)(2,1)} copy(bf16[1,4096,1,768]{3,2,1,0:T(2,128)(2,1)} %get-tuple-element.157) | data formatting | bytes 12582912 | tf_op jit(solution)/shard_map/slice | solution.py:82
  98.9 8.3 %reshape.144 = bf16[4,3072,192]{1,0,2:T(4,128)(2,1)} reshape(bf16[12288,192]{0,1:T(8,128)(2,1)} %all-gather.11.cloned.1.call-done) | data formatting | bytes 9437184 | tf_op jit(solution)/shard_map/all_gather | solution.py:63
  107.1 4.1 all-gather.7.cloned.1.call-done
  112.4 4.3 broadcast_in_dim.60
  116.6 3.8 reduce_max.27
  125.3 25.7 %fusion.37 = (bf16[16,256,1,768]{3,2,1,0:T(2,128)(2,1)}, bf16[16,256,1,768]{3,2,1,0:T(2,128)(2,1)}) fusion(bf16[16,256,2,768]{3,2,1,0:T(2,128)(2,1)} %param.20), kind=kLoop, calls=%fused_computation.85 | loop fusion | bytes 25165824 | tf_op jit(solution)/shard_map/slice | solution.py:143
  151.1 29.0 %copy.105 = bf16[16,256,1,768]{1,3,0,2:T(8,128)(2,1)} copy(bf16[16,256,1,768]{3,2,1,0:T(2,128)(2,1)} %get-tuple-element.156) | data formatting | bytes 12582912 | tf_op jit(solution)/shard_map/slice | solution.py:142
  181.1 3.8 fusion.43
  185.4 29.3 %copy.110 = bf16[16,256,1,768]{1,3,0,2:T(8,128)(2,1)} copy(bf16[16,256,1,768]{3,2,1,0:T(2,128)(2,1)} %get-tuple-element.155) | data formatting | bytes 12582912 | tf_op jit(solution)/shard_map/slice | solution.py:143
  214.9 4.7 fusion.14
  223.9 4.0 fusion.28
  228.0 12.6 %all_gather.21 = bf16[32,3072]{1,0:T(8,128)(2,1)S(1)} all-gather(bf16[32,768]{1,0:T(8,128)(2,1)S(1)} %copy-done.1), channel_id=1, replica_groups=mesh['req'=32,'mlp'=4] {'mlp'}, dimensions={1}, use_global_device_ids=true | all-gather | bytes 245760 | tf_op jit(solution)/shard_map/all_gather | solution.py:187
  240.6 76.6 %all-reduce.3.cloned.1.call-done = f32[32,3072]{1,0:T(8,128)} async-done(((f32[32,3072]{1,0:T(8,128)}), f32[32,3072]{1,0:T(8,128)}) %all-reduce.3.cloned.1.call-update) | async-done | bytes 393232 | tf_op jit(solution)/shard_map/psum | solution.py:188
  319.3 3.7 copy.117
  323.0 2.1 copy-done
  325.4 38.2 %all-gather.9.cloned.1.call-done = bf16[256,3072]{1,0:T(8,128)(2,1)} async-done(((bf16[8,3072]{1,0:T(8,128)(2,1)}), bf16[256,3072]{1,0:T(8,128)(2,1)}) %all-gather.9.cloned.1.call-update) | async-done | bytes 1572880 | tf_op jit(solution)/shard_map/all_gather | solution.py:195
  365.7 2.0 fusion.45
  367.7 3.7 convolution_bitcast_fusion.1
  372.7 78.5 %reduce-scatter.2.cloned.1.call-done = f32[8,3072]{1,0:T(8,128)} async-done(((f32[256,3072]{1,0:T(8,128)}), f32[8,3072]{1,0:T(8,128)}) %reduce-scatter.2.cloned.1.call-update) | async-done | bytes 98320 | tf_op jit(solution)/shard_map/reduce_scatter | solution.py:204
  452.9 4.4 all-to-all-start
  457.4 11.4 %all-reduce = f32[32]{0:T(128)} all-reduce(f32[32]{0:T(128)S(1)} %multiply_dynamic-update-slice_fusion), channel_id=1, replica_groups=mesh['req'=32,'mlp'=4] {'mlp'}, use_global_device_ids=true, to_apply=%add | all-reduce | flops 32 | bytes 256
  (95 shorter events, 22.2 us)
Async XLA Ops:
  7.2 91.7 %all-gather.11.cloned.1.call-start = ((), (), s32[]{:S(2)}) async-start(), calls=%async_computation.6 | async-start | bytes 5898240 | tf_op jit(solution)/shard_map/all_gather | solution.py:63
  9.6 101.7 %all-gather.7.cloned.1.call-start = ((), (), s32[]{:S(2)}) async-start(), calls=%async_computation.2 | async-start | bytes 1622016 | tf_op jit(solution)/shard_map/all_gather | solution.py:61
  19.1 202.9 %all-gather.13.cloned.1.call-start = ((), (), s32[]{:S(2)}) async-start(), calls=%async_computation.7 | async-start | bytes 7569408 | tf_op jit(solution)/shard_map/all_gather | solution.py:124
  120.5 1.5 copy-start.5
  121.8 195.5 %all-reduce.3.cloned.1.call-start = ((), (), s32[]{:S(2)}) async-start(), calls=%async_computation.3 | async-start | bytes 786432 | tf_op jit(solution)/shard_map/psum | solution.py:188
  219.7 8.3 %copy-start.1 = (bf16[32,768]{1,0:T(8,128)(2,1)S(1)}, bf16[32,768]{1,0:T(8,128)(2,1)}, u32[]{:S(2)}) copy-start(bf16[32,768]{1,0:T(8,128)(2,1)} %param.21) | copy-start | bytes 147460
  222.0 96.5 %copy-start.4 = (f32[3072]{0:T(1024)S(1)}, f32[3072]{0:T(1024)}, u32[]{:S(2)}) copy-start(f32[3072]{0:T(1024)} %param.23) | copy-start | bytes 36868
  228.0 135.7 %all-gather.9.cloned.1.call-start = ((), (), s32[]{:S(2)}) async-start(), calls=%async_computation.4 | async-start | bytes 1622016 | tf_op jit(solution)/shard_map/all_gather | solution.py:195
  319.2 132.0 %reduce-scatter.2.cloned.1.call-start = ((), (), s32[]{:S(2)}) async-start(), calls=%async_computation.5 | async-start | bytes 3244032 | tf_op jit(solution)/shard_map/reduce_scatter | solution.py:204
  323.0 2.1 copy-start
  367.7 3.8 copy-start.6
  367.7 83.5 %copy-start.2 = (f32[3072]{0:T(1024)S(1)}, f32[3072]{0:T(1024)}, u32[]{:S(2)}) copy-start(f32[3072]{0:T(1024)} %param.28) | copy-start | bytes 36868
  367.7 83.5 %copy-start.3 = (f32[3072]{0:T(1024)S(1)}, f32[3072]{0:T(1024)}, u32[]{:S(2)}) copy-start(f32[3072]{0:T(1024)} %param.27) | copy-start | bytes 36868
  452.9 16.0 %all-to-all-start = ((bf16[8,4,768]{2,0,1:T(8,128)(2,1)}), bf16[8,4,768]{2,0,1:T(8,128)(2,1)S(1)}, u32[]{:S(2)}, u32[]{:S(2)}) async-start(bf16[8,4,768]{2,0,1:T(8,128)(2,1)} %bitcast.34), calls=%async_computation.1 | async-start | bytes 98304 | tf_op jit(solution)/shard_map/all_to_all | solution.py:216
Sparse Core Ops, SparseCore 0:
  9.7 55.2 all-gather.10
  67.8 43.3 all-gather.6
  121.9 97.7 all-gather.12
  228.1 89.1 all-reduce.2
  320.2 43.4 all-gather.8
  371.6 79.6 reduce-scatter.1

commit v3 on v2

--- a/solution.py
+++ b/solution.py
@@ -1,8 +1,11 @@
+import functools
 import math
 
 import jax
 import jax.numpy as jnp
 from jax import lax
+from jax.experimental import pallas as pl
+from jax.experimental.pallas import tpu as pltpu
 from jax.sharding import PartitionSpec as P
 
 HD = 96
@@ -23,6 +26,116 @@
     return jnp.concatenate(
         [first * cosine - second * sine, second * cosine + first * sine], axis=-1
     )
+
+
+def prompt_kernel(block_len, score_scale, valid_ref, q_ref, cache_ref, acc_ref, top_ref, sum_ref):
+    number = pl.program_id(0)
+
+    @pl.when(number == 0)
+    def _():
+        acc_ref[...] = jnp.zeros_like(acc_ref)
+        top_ref[...] = jnp.full_like(top_ref, masked_value)
+        sum_ref[...] = jnp.zeros_like(sum_ref)
+
+    @pl.when(number * block_len < valid_ref[0])
+    def _():
+        keys = cache_ref[:, 0, :]
+        values = cache_ref[:, 1, :]
+        scores = (
+            lax.dot_general(
+                q_ref[...], keys, (((1,), (1,)), ((), ())), preferred_element_type=jnp.float32
+            )
+            * score_scale
+        )
+        places = number * block_len + lax.broadcasted_iota(jnp.int32, scores.shape, 1)
+        scores = jnp.where(places < valid_ref[0], scores, masked_value)
+        top_old = top_ref[...]
+        top_new = jnp.maximum(top_old, jnp.max(scores, axis=1, keepdims=True))
+        shrink = jnp.exp(top_old - top_new)
+        weights = jnp.exp(scores - top_new)
+        sum_ref[...] = shrink * sum_ref[...] + jnp.sum(weights, axis=1, keepdims=True)
+        acc_ref[...] = shrink * acc_ref[...] + jnp.dot(
+            weights.astype(jnp.bfloat16), values, preferred_element_type=jnp.float32
+        )
+        top_ref[...] = top_new
+
+
+def prompt_attention(q_diag, cache, valid_count, score_scale):
+    span = cache.shape[1]
+    block_len = min(512, span)
+    lanes = cache.shape[3]
+    rows = q_diag.shape[0]
+
+    def cache_block(number, valid):
+        last = (valid[0] + block_len - 1) // block_len - 1
+        return (0, jnp.maximum(jnp.minimum(number, last), 0), 0, 0)
+
+    spec = pltpu.PrefetchScalarGridSpec(
+        num_scalar_prefetch=1,
+        grid=(span // block_len,),
+        in_specs=[
+            pl.BlockSpec((rows, lanes), lambda number, valid: (0, 0)),
+            pl.BlockSpec((None, block_len, 2, lanes), cache_block),
+        ],
+        out_specs=[
+            pl.BlockSpec((rows, lanes), lambda number, valid: (0, 0)),
+            pl.BlockSpec((rows, 1), lambda number, valid: (0, 0)),
+            pl.BlockSpec((rows, 1), lambda number, valid: (0, 0)),
+        ],
+    )
+    return pl.pallas_call(
+        functools.partial(prompt_kernel, block_len, score_scale),
+        grid_spec=spec,
+        out_shape=[
+            jax.ShapeDtypeStruct((rows, lanes), jnp.float32),
+            jax.ShapeDtypeStruct((rows, 1), jnp.float32),
+            jax.ShapeDtypeStruct((rows, 1), jnp.float32),
+        ],
+    )(valid_count.reshape(1), q_diag, cache)
+
+
+def tail_kernel(score_scale, lens_ref, q_ref, cache_ref, acc_ref, top_ref, sum_ref):
+    number = pl.program_id(0)
+    keys = cache_ref[:, 0, :]
+    values = cache_ref[:, 1, :]
+    scores = (
+        lax.dot_general(q_ref[...], keys, (((1,), (1,)), ((), ())), preferred_element_type=jnp.float32)
+        * score_scale
+    )
+    places = lax.broadcasted_iota(jnp.int32, scores.shape, 1)
+    scores = jnp.where(places < lens_ref[number], scores, masked_value)
+    top = jnp.max(scores, axis=1, keepdims=True)
+    weights = jnp.exp(scores - top)
+    top_ref[...] = top
+    sum_ref[...] = jnp.sum(weights, axis=1, keepdims=True)
+    acc_ref[...] = jnp.dot(weights.astype(jnp.bfloat16), values, preferred_element_type=jnp.float32)
+
+
+def tail_attention(q_diag, cache, lens, score_scale):
+    conts, rows, lanes = q_diag.shape
+    cap = cache.shape[1]
+    spec = pltpu.PrefetchScalarGridSpec(
+        num_scalar_prefetch=1,
+        grid=(conts,),
+        in_specs=[
+            pl.BlockSpec((None, rows, lanes), lambda number, lens: (number, 0, 0)),
+            pl.BlockSpec((None, cap, 2, lanes), lambda number, lens: (number, 0, 0, 0)),
+        ],
+        out_specs=[
+            pl.BlockSpec((None, rows, lanes), lambda number, lens: (number, 0, 0)),
+            pl.BlockSpec((None, rows, 1), lambda number, lens: (number, 0, 0)),
+            pl.BlockSpec((None, rows, 1), lambda number, lens: (number, 0, 0)),
+        ],
+    )
+    return pl.pallas_call(
+        functools.partial(tail_kernel, score_scale),
+        grid_spec=spec,
+        out_shape=[
+            jax.ShapeDtypeStruct((conts, rows, lanes), jnp.float32),
+            jax.ShapeDtypeStruct((conts, rows, 1), jnp.float32),
+            jax.ShapeDtypeStruct((conts, rows, 1), jnp.float32),
+        ],
+    )(lens, q_diag, cache)
 
 
 def per_device(
@@ -76,43 +189,13 @@
     )
     owned_len = lax.dynamic_index_in_dim(prompt_len, owned_prompt, 0, keepdims=False)
     valid_count = jnp.clip(owned_len - held_half * span, 0, span)
-    block_len = min(512, span)
-    block_count = (valid_count + block_len - 1) // block_len
-    cache_keys = prompt_cache[0, :, 0].reshape(span, heads_here, HD)
-    cache_values = prompt_cache[0, :, 1].reshape(span, heads_here, HD)
-
-    def score_block(number, buffer):
-        key_block = lax.dynamic_slice_in_dim(cache_keys, number * block_len, block_len, 0)
-        block_scores = (
-            jnp.einsum("rhd,khd->hrk", q_owned, key_block, preferred_element_type=jnp.float32)
-            * score_scale
-        )
-        places = number * block_len + jnp.arange(block_len, dtype=jnp.int32)
-        block_scores = jnp.where(places[None, None, :] < valid_count, block_scores, masked_value)
-        return lax.dynamic_update_slice_in_dim(buffer, block_scores, number * block_len, 2)
-
-    empty_scores = jnp.full((heads_here, owned_rows, span), masked_value, jnp.float32)
-    prefix_scores = lax.fori_loop(0, block_count, score_block, empty_scores)
-    prefix_max = jnp.max(prefix_scores, axis=2)
-
-    def value_block(number, carry):
-        numer, totals = carry
-        score_part = lax.dynamic_slice_in_dim(prefix_scores, number * block_len, block_len, 2)
-        weights = jnp.exp(score_part - prefix_max[:, :, None])
-        value_part = lax.dynamic_slice_in_dim(cache_values, number * block_len, block_len, 0)
-        numer = numer + jnp.einsum(
-            "hrk,khd->rhd",
-            weights.astype(jnp.bfloat16),
-            value_part,
-            preferred_element_type=jnp.float32,
-        )
-        return (numer, totals + jnp.sum(weights, axis=2))
-
-    start_carry = (
-        jnp.zeros((owned_rows, heads_here, HD), jnp.float32),
-        jnp.zeros((heads_here, owned_rows), jnp.float32),
-    )
-    owner_numer, owner_total = lax.fori_loop(0, block_count, value_block, start_carry)
+    eye = jnp.eye(heads_here, dtype=jnp.bfloat16)
+    q_diag = jnp.einsum("rhd,hg->hrgd", q_owned, eye).reshape(heads_here * owned_rows, width_here)
+    prompt_acc, prompt_top, prompt_sum = prompt_attention(q_diag, prompt_cache, valid_count, score_scale)
+    prompt_acc = prompt_acc.reshape(heads_here, owned_rows, heads_here, HD)
+    owner_numer = jnp.stack([prompt_acc[h, :, h, :] for h in range(heads_here)], axis=1)
+    owner_total = prompt_sum.reshape(heads_here, owned_rows)
+    prefix_max = prompt_top.reshape(heads_here, owned_rows)
     packed = jnp.concatenate(
         [
             owner_numer.reshape(owned_rows, width_here),
@@ -138,38 +221,29 @@
     numer_first, total_first, max_first = part_of(slot_first)
     numer_second, total_second, max_second = part_of(slot_second)
 
-    tail_cap = tail_cache.shape[1]
-    tail_keys = tail_cache[:, :, 0].reshape(conts_here, tail_cap, heads_here, HD)
-    tail_values = tail_cache[:, :, 1].reshape(conts_here, tail_cap, heads_here, HD)
-    s_tail = (
-        jnp.einsum("cthd,cjhd->chtj", query, tail_keys, preferred_element_type=jnp.float32)
-        * score_scale
-    )
-    s_tail = jnp.where(
-        jnp.arange(tail_cap)[None, None, None, :] < tail_here[:, None, None, None],
-        s_tail,
-        masked_value,
-    )
+    tail_diag = jnp.einsum("cthd,hg->chtgd", query, eye).reshape(
+        conts_here, heads_here * 2, width_here
+    )
+    tail_acc, tail_top, tail_sum = tail_attention(tail_diag, tail_cache, tail_here, score_scale)
+    tail_acc = tail_acc.reshape(conts_here, heads_here, 2, heads_here, HD)
+    cache_numer = jnp.stack([tail_acc[:, h, :, h, :] for h in range(heads_here)], axis=2)
+    cache_top = tail_top.reshape(conts_here, heads_here, 2)
+    cache_sum = tail_sum.reshape(conts_here, heads_here, 2)
     s_new = (
         jnp.einsum("cthd,cuhd->chtu", query, key_new, preferred_element_type=jnp.float32)
         * score_scale
     )
     causal = jnp.arange(2)[None, :] <= jnp.arange(2)[:, None]
     s_new = jnp.where(causal[None, None, :, :], s_new, masked_value)
-    tail_max = jnp.maximum(jnp.max(s_tail, -1), jnp.max(s_new, -1))
-    w_tail = jnp.exp(s_tail - tail_max[..., None])
+    tail_max = jnp.maximum(cache_top, jnp.max(s_new, -1))
+    cache_scale = jnp.exp(cache_top - tail_max)
     w_new = jnp.exp(s_new - tail_max[..., None])
-    numer_tail = jnp.einsum(
-        "chtj,cjhd->cthd",
-        w_tail.astype(jnp.bfloat16),
-        tail_values,
-        preferred_element_type=jnp.float32,
-    )
+    numer_tail = cache_numer * jnp.transpose(cache_scale, (0, 2, 1))[..., None]
     numer_tail = numer_tail + jnp.einsum(
         "chtu,cuhd->cthd", w_new.astype(jnp.bfloat16), value_new, preferred_element_type=jnp.float32
     )
     numer_tail = numer_tail.reshape(rows_here, heads_here, HD)
-    total_tail = jnp.transpose(jnp.sum(w_tail, -1) + jnp.sum(w_new, -1), (0, 2, 1)).reshape(
+    total_tail = jnp.transpose(cache_sum * cache_scale + jnp.sum(w_new, -1), (0, 2, 1)).reshape(
         rows_here, heads_here
     )
     max_tail = jnp.transpose(tail_max, (0, 2, 1)).reshape(rows_here, heads_here)

time: 481 us -> 414 us (0.86)
  local copies, waits for them, and re-layouts: 193 us -> 31.3 us
  waiting for transfers between devices: 198 us -> 257 us
  Pallas kernels: 0 us -> 52 us
  matrix products: 20.8 us -> 11 us
    slice x6 -> x1, local copies, waits for them, and re-layouts: 163 us -> 0.11 us  [per_device(): tail_acc[:, h, :, h, :]]
    pallas_call x0 -> x2, Pallas kernels: none -> 52 us  [the longest x1 30.8 us: tail_attention(): pl.pallas_call(functools.partial(tail_kernel, score_scale), grid_spec=spe...]
    psum x1, waiting for transfers between devices: 76.6 us -> 28.9 us  [per_device(): lax.psum(jnp.dot(attn, w_out, preferred_element_type=jnp.float32), 'mlp')]
    all_gather x1, waiting for transfers between devices: 0.01 us -> 46.9 us  [per_device(): weights_all = lax.all_gather(weights_cat, 'mlp', axis=0, tiled=False)]
    all_gather x1, waiting for transfers between devices: 4.13 us -> 38 us  [per_device(): lax.all_gather(query.reshape(rows_here, width_here), 'req', axis=0, tiled...]
    all_gather x1, waiting for transfers between devices: 0.01 us -> 26.6 us  [per_device(): packed_all = lax.all_gather(packed[None], 'req', axis=0, tiled=True)]
    dot_general x2 -> x0, matrix products: 8.52 us -> none  [the longest x1 4.71 us: per_device(): jnp.einsum('chtj,cjhd->cthd', w_tail.astype(jnp.bfloat16), tail_values, p...]
    reshape x0 -> x8, local copies, waits for them, and re-layouts: none -> 7.12 us  [the longest x1 2.17 us: per_device(): prompt_acc = prompt_acc.reshape(heads_here, owned_rows, heads_here, HD)]
  transfers between devices with their start and end apart: 7 -> 7, of which waited for: 4 -> 6; matrix products, arithmetic and copies ran while one was open for 41% -> 6% of each run, Pallas kernels for 0% -> 7%
where the time goes in v3:
time: 414 us; the launch traced here: 413 us
  waiting for transfers between devices  257 us (62%)
  Pallas kernels  52 us (13%)
  local copies, waits for them, and re-layouts  31.3 us (8%)
  blocking collectives  24.3 us (6%)
  between operations  22.5 us (5%)
  other arithmetic  11 us (3%)
  matrix products  11 us (3%)
  starting transfers between devices  4.86 us (1%)
    reduce_scatter x1, waiting for transfers between devices, per_device(): lax.psum_scatter(down_sum, 'req', scatter_dimension=0, tiled=True)  77.9 us
    all_gather x1, waiting for transfers between devices, per_device(): weights_all = lax.all_gather(weights_cat, 'mlp', axis=0, tiled=False)  46.9 us
    all_gather x1, waiting for transfers between devices, per_device(): piece = lax.all_gather(normed_share, 'req', axis=0, tiled=True)  38.2 us
    all_gather x1, waiting for transfers between devices, per_device(): lax.all_gather(query.reshape(rows_here, width_here), 'req', axis=0, tiled...  38 us
    pallas_call x1, Pallas kernels, tail_attention(): pl.pallas_call(functools.partial(tail_kernel, score_scale), grid_spec=spe...  30.8 us
    psum x1, waiting for transfers between devices, per_device(): lax.psum(jnp.dot(attn, w_out, preferred_element_type=jnp.float32), 'mlp')  28.9 us
    all_gather x1, waiting for transfers between devices, per_device(): packed_all = lax.all_gather(packed[None], 'req', axis=0, tiled=True)  26.6 us
    pallas_call x1, Pallas kernels, prompt_attention(): pl.pallas_call(functools.partial(prompt_kernel, block_len, score_scale),...  21.2 us
  transfers between devices with their start and end apart: 7, of which 6 were waited for; matrix products, arithmetic and copies ran while one was open for 6% of the time, Pallas kernels for 7%

profile of v3, /device:TPU:0, one launch (start us, length us, event | category | flops | bytes accessed | tf_op | source)
XLA Modules:
  0.0 413.5 jit_solution(11619562464474481962)
XLA Ops:
  7.2 2.4 pad_maximum_fusion
  13.8 1.9 broadcast_add_fusion
  18.2 46.9 %all-gather.11.cloned.1.call-done = bf16[12288,192]{0,1:T(8,128)(2,1)} async-done(((bf16[3072,192]{0,1:T(8,128)(2,1)}), bf16[12288,192]{0,1:T(8,128)(2,1)}) %all-gather.11.cloned.1.call-update) | async-done | bytes 4718608 | tf_op jit(solution)/shard_map/all_gather | solution.py:176
  65.1 8.3 %reshape.158 = bf16[4,3072,192]{1,0,2:T(4,128)(2,1)} reshape(bf16[12288,192]{0,1:T(8,128)(2,1)} %all-gather.11.cloned.1.call-done) | data formatting | bytes 9437184 | tf_op jit(solution)/shard_map/all_gather | solution.py:176
  73.3 38.0 %all-gather.7.cloned.1.call-done = bf16[1024,768]{1,0:T(8,128)(2,1)} async-done(((bf16[32,768]{1,0:T(8,128)(2,1)}), bf16[1024,768]{1,0:T(8,128)(2,1)}) %all-gather.7.cloned.1.call-update) | async-done | bytes 1572880 | tf_op jit(solution)/shard_map/all_gather | solution.py:174
  112.6 1.8 reshape.144.q_ref
  114.3 21.2 %shard_map.149 = (f32[512,768]{1,0:T(8,128)}, f32[512,1]{1,0:T(8,128)}, f32[512,1]{1,0:T(8,128)}) custom-call(s32[1]{0:T(128)} %bitcast.2.valid_ref, bf16[512,768]{1,0:T(8,128)(2,1)} %reshape.144.q_ref, bf16[1,4096,2,768]{3,2,1,0:T(2,128)(2,1)} %cache_ref.2), custom_call_target="tpu_custom_call" | custom-call | tf_op jit(solution)/shard_map/pallas_call | solution.py:86
  135.5 2.2 reshape.145
  143.9 1.2 reshape.149.q_ref
  145.2 30.8 %shard_map.150 = (f32[16,16,768]{2,1,0:T(8,128)}, f32[16,16,1]{2,1,0:T(8,128)}, f32[16,16,1]{2,1,0:T(8,128)}) custom-call(s32[16]{0:T(128)} %get-tuple-element.30.lens_ref, bf16[16,16,768]{2,1,0:T(8,128)(2,1)} %reshape.149.q_ref, bf16[16,256,2,768]{3,2,1,0:T(2,128)(2,1)} %cache_ref.3), custom_call_target="tpu_custom_call" | custom-call | tf_op jit(solution)/shard_map/pallas_call | solution.py:130
  175.9 1.6 reshape.152
  181.4 26.6 %all-gather.13.cloned.1.call-done = f32[2048,784]{1,0:T(8,128)} async-done(((f32[64,784]{1,0:T(8,128)}), f32[2048,784]{1,0:T(8,128)}) %all-gather.13.cloned.1.call-update) | async-done | bytes 6422544 | tf_op jit(solution)/shard_map/all_gather | solution.py:207
  209.9 4.0 fusion.10
  213.9 12.8 %all_gather.21 = bf16[32,3072]{1,0:T(8,128)(2,1)S(1)} all-gather(bf16[32,768]{1,0:T(8,128)(2,1)S(1)} %copy-done.7), channel_id=1, replica_groups=mesh['req'=32,'mlp'=4] {'mlp'}, dimensions={1}, use_global_device_ids=true | all-gather | bytes 245760 | tf_op jit(solution)/shard_map/all_gather | solution.py:261
  226.8 28.9 %all-reduce.3.cloned.1.call-done = f32[32,3072]{1,0:T(8,128)} async-done(((f32[32,3072]{1,0:T(8,128)}), f32[32,3072]{1,0:T(8,128)}) %all-reduce.3.cloned.1.call-update) | async-done | bytes 393232 | tf_op jit(solution)/shard_map/psum | solution.py:262
  257.8 3.7 copy.175
  261.5 2.1 copy-done
  263.9 38.2 %all-gather.9.cloned.1.call-done = bf16[256,3072]{1,0:T(8,128)(2,1)} async-done(((bf16[8,3072]{1,0:T(8,128)(2,1)}), bf16[256,3072]{1,0:T(8,128)(2,1)}) %all-gather.9.cloned.1.call-update) | async-done | bytes 1572880 | tf_op jit(solution)/shard_map/all_gather | solution.py:269
  302.1 2.1 fusion.28
  304.9 3.7 convolution_bitcast_fusion
  310.5 77.9 %reduce-scatter.2.cloned.1.call-done = f32[8,3072]{1,0:T(8,128)} async-done(((f32[256,3072]{1,0:T(8,128)}), f32[8,3072]{1,0:T(8,128)}) %reduce-scatter.2.cloned.1.call-update) | async-done | bytes 98320 | tf_op jit(solution)/shard_map/reduce_scatter | solution.py:278
  388.4 1.7 multiply_reduce_fusion.1
  390.1 4.4 %all-to-all-start = ((bf16[8,4,768]{2,0,1:T(8,128)(2,1)}), bf16[8,4,768]{2,0,1:T(8,128)(2,1)S(1)}, u32[]{:S(2)}, u32[]{:S(2)}) async-start(bf16[8,4,768]{2,0,1:T(8,128)(2,1)} %bitcast.52), calls=%async_computation.1 | async-start | bytes 98304 | tf_op jit(solution)/shard_map/all_to_all | solution.py:290
  394.6 11.4 %all-reduce = f32[32]{0:T(128)} all-reduce(f32[32]{0:T(128)S(1)} %multiply_dynamic-update-slice_fusion), channel_id=1, replica_groups=mesh['req'=32,'mlp'=4] {'mlp'}, use_global_device_ids=true, to_apply=%add | all-reduce | flops 32 | bytes 256
  (117 shorter events, 17.2 us)
Async XLA Ops:
  7.2 57.9 %all-gather.11.cloned.1.call-start = ((), (), s32[]{:S(2)}) async-start(), calls=%async_computation.6 | async-start | bytes 5898240 | tf_op jit(solution)/shard_map/all_gather | solution.py:176
  7.2 2.5 copy-start.12
  7.2 5.7 %copy-start.4 = (bf16[32,3,768]{2,0,1:T(8,128)(2,1)S(1)}, bf16[32,3,768]{2,0,1:T(8,128)(2,1)}, u32[]{:S(2)}) copy-start(bf16[32,3,768]{2,0,1:T(8,128)(2,1)} %param.14) | copy-start | bytes 442372
  7.2 5.9 %copy-start.11 = (s32[16]{0:T(128)S(1)}, s32[16]{0:T(128)}, u32[]{:S(2)}) copy-start(s32[16]{0:T(128)} %param.26) | copy-start | bytes 196
  9.6 101.7 %all-gather.7.cloned.1.call-start = ((), (), s32[]{:S(2)}) async-start(), calls=%async_computation.2 | async-start | bytes 1622016 | tf_op jit(solution)/shard_map/all_gather | solution.py:174
  17.5 190.5 %all-gather.13.cloned.1.call-start = ((), (), s32[]{:S(2)}) async-start(), calls=%async_computation.7 | async-start | bytes 7569408 | tf_op jit(solution)/shard_map/all_gather | solution.py:207
  137.7 1.0 copy-start.3
  137.7 1.3 copy-start.2
  140.1 115.7 %all-reduce.3.cloned.1.call-start = ((), (), s32[]{:S(2)}) async-start(), calls=%async_computation.3 | async-start | bytes 786432 | tf_op jit(solution)/shard_map/psum | solution.py:262
  175.9 2.4 copy-start.6
  178.2 1.6 copy-start.5
  209.9 4.1 copy-start.7
  213.9 43.1 %copy-start.10 = (f32[3072]{0:T(1024)S(1)}, f32[3072]{0:T(1024)}, u32[]{:S(2)}) copy-start(f32[3072]{0:T(1024)} %param.19) | copy-start | bytes 36868
  213.9 88.2 %all-gather.9.cloned.1.call-start = ((), (), s32[]{:S(2)}) async-start(), calls=%async_computation.4 | async-start | bytes 1622016 | tf_op jit(solution)/shard_map/all_gather | solution.py:269
  257.7 130.7 %reduce-scatter.2.cloned.1.call-start = ((), (), s32[]{:S(2)}) async-start(), calls=%async_computation.5 | async-start | bytes 3244032 | tf_op jit(solution)/shard_map/reduce_scatter | solution.py:278
  261.5 2.1 copy-start
  302.1 2.1 copy-start.1
  308.6 0.7 copy-start.13
  308.6 79.8 %copy-start.8 = (f32[3072]{0:T(1024)S(1)}, f32[3072]{0:T(1024)}, u32[]{:S(2)}) copy-start(f32[3072]{0:T(1024)} %param.24) | copy-start | bytes 36868
  308.6 79.8 %copy-start.9 = (f32[3072]{0:T(1024)S(1)}, f32[3072]{0:T(1024)}, u32[]{:S(2)}) copy-start(f32[3072]{0:T(1024)} %param.23) | copy-start | bytes 36868
  390.1 16.0 %all-to-all-start = ((bf16[8,4,768]{2,0,1:T(8,128)(2,1)}), bf16[8,4,768]{2,0,1:T(8,128)(2,1)S(1)}, u32[]{:S(2)}, u32[]{:S(2)}) async-start(bf16[8,4,768]{2,0,1:T(8,128)(2,1)} %bitcast.52), calls=%async_computation.1 | async-start | bytes 98304 | tf_op jit(solution)/shard_map/all_to_all | solution.py:290
Sparse Core Ops, SparseCore 0:
  9.7 55.2 all-gather.10
  67.9 43.3 all-gather.6
  140.2 67.7 all-gather.12
  214.0 41.6 all-reduce.2
  258.7 43.4 all-gather.8
  308.7 79.6 reduce-scatter.1

commit v4 on v3

--- a/solution.py
+++ b/solution.py
@@ -172,9 +172,17 @@
     key_new = rotary(block[:, :, 1].astype(jnp.float32), position).astype(jnp.bfloat16)
     value_new = block[:, :, 2]
     gathered = lax.all_gather(query.reshape(rows_here, width_here), "req", axis=0, tiled=True)
+    mlp_count = lax.axis_size("mlp")
     weights_cat = jnp.concatenate([w_gate, w_up, jnp.transpose(w_down)], axis=1)
-    weights_all = lax.all_gather(weights_cat, "mlp", axis=0, tiled=False)
-    gathered, weights_all = lax.optimization_barrier((gathered, weights_all))
+    weights_all = jnp.stack(
+        [weights_cat]
+        + [
+            lax.ppermute(
+                weights_cat, "mlp", [(m, (m + shift) % mlp_count) for m in range(mlp_count)]
+            )
+            for shift in range(1, mlp_count)
+        ]
+    )
     slot_ids = jnp.arange(req_count, dtype=jnp.int32)
     slot_of = jnp.sum(
         jnp.where(slot_part[None, :] == slot_ids[:, None], slot_ids[None, :], 0), axis=1
@@ -204,6 +212,7 @@
         ],
         axis=1,
     )
+    packed, weights_all = lax.optimization_barrier((packed, weights_all))
     packed_all = lax.all_gather(packed[None], "req", axis=0, tiled=True)
     row_offset = req_index % 2 * rows_here
     slot_first = lax.dynamic_index_in_dim(slot_of, 2 * own_prompt, 0, keepdims=False)
@@ -258,12 +267,15 @@
         + numer_tail * scale_tail[..., None]
     )
     attn = (row_numer / row_total[:, :, None]).astype(jnp.bfloat16).reshape(rows_here, width_here)
-    residual_full = lax.all_gather(residual, "mlp", axis=1, tiled=True)
-    projected = lax.psum(jnp.dot(attn, w_out, preferred_element_type=jnp.float32), "mlp")
-    state = residual_full.astype(jnp.float32) + projected
+    partial = jnp.dot(attn, w_out, preferred_element_type=jnp.float32)
+    col_start = mlp_index * width_here
+    own_cols = lax.dynamic_slice_in_dim(partial, col_start, width_here, 1)
+    partial = lax.dynamic_update_slice_in_dim(
+        partial, own_cols + residual.astype(jnp.float32), col_start, 1
+    )
+    state = lax.psum(partial, "mlp")
     mean_square = jnp.mean(state * state, axis=1, keepdims=True)
     normed = (state * lax.rsqrt(mean_square + norm_eps) * mlp_gain).astype(jnp.bfloat16)
-    mlp_count = lax.axis_size("mlp")
     share = rows_here // mlp_count
     normed_share = lax.dynamic_slice_in_dim(normed, mlp_index * share, share, 0)
     piece = lax.all_gather(normed_share, "req", axis=0, tiled=True)
@@ -286,10 +298,16 @@
     final_square = jnp.mean(final_share * final_share, axis=1)
     final_dot = jnp.sum(final_share * final_gain * score_weight, axis=1)
     score_share = final_dot * lax.rsqrt(final_square + norm_eps)
-    scores = lax.all_gather(score_share, "mlp", axis=0, tiled=True)
-    out_rows = lax.all_to_all(
-        final_share.astype(jnp.bfloat16), "mlp", split_axis=1, concat_axis=0, tiled=True
-    )
+    payload = jnp.concatenate(
+        [
+            final_share.reshape(share, mlp_count, width_here),
+            jnp.broadcast_to(score_share[:, None, None], (share, mlp_count, 1)),
+        ],
+        axis=2,
+    )
+    arrived = lax.all_to_all(payload, "mlp", split_axis=1, concat_axis=0, tiled=True)
+    out_rows = arrived[:, 0, :width_here].astype(jnp.bfloat16)
+    scores = arrived[:, 0, width_here]
     return (out_rows, scores)
 
 

time: 414 us -> 381 us (0.920)
  Pallas kernels: 52 us -> 34.2 us
  blocking collectives: 24.3 us -> 10.1 us
  local copies, waits for them, and re-layouts: 31.3 us -> 23.6 us
  other arithmetic: 11 us -> 15.7 us
    ppermute x0 -> x3, waiting for transfers between devices: none -> 48.9 us  [per_device(): lax.ppermute(weights_cat, 'mlp', [(m, (m + shift) % mlp_count) for m in r...]
    all_gather x1 -> x0, waiting for transfers between devices: 46.9 us -> none  [per_device(): weights_all = lax.all_gather(weights_cat, 'mlp', axis=0, tiled=False)]
    all_gather x1, waiting for transfers between devices: 38 us -> 0.01 us  [per_device(): lax.all_gather(query.reshape(rows_here, width_here), 'req', axis=0, tiled...]
    all_gather x1, waiting for transfers between devices: 26.6 us -> 45.6 us  [per_device(): packed_all = lax.all_gather(packed[None], 'req', axis=0, tiled=True)]
    pallas_call x1, Pallas kernels: 21.2 us -> 3.4 us  [prompt_attention(): pl.pallas_call(functools.partial(prompt_kernel, block_len, score_scale),...]
    all_gather x1 -> x0, blocking collectives: 12.8 us -> none  [per_device(): residual_full = lax.all_gather(residual, 'mlp', axis=1, tiled=True)]
    psum x1, waiting for transfers between devices: 28.9 us -> 41.8 us  [per_device(): state = lax.psum(partial, 'mlp')]
    unnamed x1 -> x0, blocking collectives: 11.4 us -> none
  transfers between devices with their start and end apart: 7 -> 8, of which waited for: 6 -> 6; matrix products, arithmetic and copies ran while one was open for 6% -> 4% of each run, Pallas kernels for 7% -> 8%
where the time goes in v4:
time: 381 us; the launch traced here: 380 us
  waiting for transfers between devices  257 us (67%)
  Pallas kernels  34.2 us (9%)
  local copies, waits for them, and re-layouts  23.6 us (6%)
  between operations  21.6 us (6%)
  other arithmetic  15.7 us (4%)
  matrix products  10.3 us (3%)
  blocking collectives  10.1 us (3%)
  starting transfers between devices  6.98 us (2%)
    reduce_scatter x1, waiting for transfers between devices, per_device(): lax.psum_scatter(down_sum, 'req', scatter_dimension=0, tiled=True)  79.8 us
    ppermute x3, waiting for transfers between devices, per_device(): lax.ppermute(weights_cat, 'mlp', [(m, (m + shift) % mlp_count) for m in r...  48.9 us
    all_gather x1, waiting for transfers between devices, per_device(): packed_all = lax.all_gather(packed[None], 'req', axis=0, tiled=True)  45.6 us
    psum x1, waiting for transfers between devices, per_device(): state = lax.psum(partial, 'mlp')  41.8 us
    all_gather x1, waiting for transfers between devices, per_device(): piece = lax.all_gather(normed_share, 'req', axis=0, tiled=True)  41.3 us
    pallas_call x1, Pallas kernels, tail_attention(): pl.pallas_call(functools.partial(tail_kernel, score_scale), grid_spec=spe...  30.8 us
    all_to_all x1, blocking collectives, per_device(): lax.all_to_all(payload, 'mlp', split_axis=1, concat_axis=0, tiled=True)  10.1 us
  transfers between devices with their start and end apart: 8, of which 6 were waited for; matrix products, arithmetic and copies ran while one was open for 4% of the time, Pallas kernels for 8%

profile of v4, /device:TPU:0, one launch (start us, length us, event | category | flops | bytes accessed | tf_op | source)
XLA Modules:
  0.0 380.0 jit_solution(10338252687718531940)
XLA Ops:
  7.2 1.3 dynamic_slice.45
  11.2 1.3 fusion.29
  12.6 2.0 broadcast_add_fusion
  20.0 1.3 fusion.24
  21.3 2.0 collective-permute-start
  23.3 3.6 collective-permute-start.1
  29.1 22.5 %collective-permute-done = bf16[3072,192]{0,1:T(8,128)(2,1)S(1)} collective-permute-done((bf16[3072,192]{0,1:T(8,128)(2,1)}, bf16[3072,192]{0,1:T(8,128)(2,1)S(1)}, u32[]{:S(2)}, u32[]{:S(2)}) %collective-permute-start) | collective-permute-done | bytes 1179680 | tf_op jit(solution)/shard_map/ppermute | solution.py:180
  51.6 26.5 %collective-permute-done.1 = bf16[3072,192]{0,1:T(8,128)(2,1)S(1)} collective-permute-done((bf16[3072,192]{0,1:T(8,128)(2,1)}, bf16[3072,192]{0,1:T(8,128)(2,1)S(1)}, u32[]{:S(2)}, u32[]{:S(2)}) %collective-permute-start.1) | collective-permute-done | bytes 1179680 | tf_op jit(solution)/shard_map/ppermute | solution.py:180
  78.1 3.6 pad_maximum_fusion
  83.6 1.8 reshape.155.q_ref
  85.3 3.4 shard_map.149
  88.8 2.2 reshape.156
  98.4 30.8 %shard_map.150 = (f32[16,16,768]{2,1,0:T(8,128)}, f32[16,16,1]{2,1,0:T(8,128)}, f32[16,16,1]{2,1,0:T(8,128)}) custom-call(s32[16]{0:T(128)} %get-tuple-element.28.lens_ref, bf16[16,16,768]{2,1,0:T(8,128)(2,1)} %reshape.160.q_ref, bf16[16,256,2,768]{3,2,1,0:T(2,128)(2,1)} %cache_ref.3), custom_call_target="tpu_custom_call" | custom-call | tf_op jit(solution)/shard_map/pallas_call | solution.py:130
  129.2 1.7 reshape.163
  134.7 45.6 %all-gather.9.cloned.1.call-done = f32[2048,784]{1,0:T(8,128)} async-done(((f32[64,784]{1,0:T(8,128)}), f32[2048,784]{1,0:T(8,128)}) %all-gather.9.cloned.1.call-update) | async-done | bytes 6422544 | tf_op jit(solution)/shard_map/all_gather | solution.py:216
  182.3 3.2 fusion.10
  186.4 41.8 %all-reduce.2.cloned.1.call-done = f32[32,3072]{1,0:T(8,128)} async-done(((f32[32,3072]{1,0:T(8,128)}), f32[32,3072]{1,0:T(8,128)}) %all-reduce.2.cloned.1.call-update) | async-done | bytes 393232 | tf_op jit(solution)/shard_map/psum | solution.py:276
  229.4 1.6 multiply_convert_fusion.2
  231.1 2.2 fusion.25
  233.3 41.3 %all-gather.7.cloned.1.call-done = bf16[256,3072]{1,0:T(8,128)(2,1)} async-done(((bf16[8,3072]{1,0:T(8,128)(2,1)}), bf16[256,3072]{1,0:T(8,128)(2,1)}) %all-gather.7.cloned.1.call-update) | async-done | bytes 1572880 | tf_op jit(solution)/shard_map/all_gather | solution.py:281
  274.6 2.1 fusion.30
  277.4 3.7 convolution_bitcast_fusion
  281.1 79.8 %reduce-scatter.2.cloned.1.call-done = f32[8,3072]{1,0:T(8,128)} async-done(((f32[256,3072]{1,0:T(8,128)}), f32[8,3072]{1,0:T(8,128)}) %reduce-scatter.2.cloned.1.call-update) | async-done | bytes 98320 | tf_op jit(solution)/shard_map/reduce_scatter | solution.py:290
  362.1 10.1 %all_to_all.18 = f32[8,4,769]{2,0,1:T(8,128)S(1)} all-to-all(f32[8,4,769]{2,0,1:T(8,128)S(1)} %pad_maximum_fusion.3), channel_id=1, replica_groups=mesh['req'=32,'mlp'=4] {'mlp'}, dimensions={1} | all-to-all | bytes 196864 | tf_op jit(solution)/shard_map/all_to_all | solution.py:308
  (140 shorter events, 23.1 us)
Async XLA Ops:
  7.2 12.8 %copy-start.7 = (bf16[64,3072]{1,0:T(8,128)(2,1)S(1)}, bf16[64,3072]{1,0:T(8,128)(2,1)}, u32[]{:S(2)}) copy-start(bf16[64,3072]{1,0:T(8,128)(2,1)} %param.22) | copy-start | bytes 1179652
  7.2 12.8 %copy-start.9 = (bf16[3072,64]{0,1:T(8,128)(2,1)S(1)}, bf16[3072,64]{0,1:T(8,128)(2,1)}, u32[]{:S(2)}) copy-start(bf16[3072,64]{0,1:T(8,128)(2,1)} %param.20) | copy-start | bytes 1179652
  7.2 12.8 %copy-start.8 = (bf16[3072,64]{0,1:T(8,128)(2,1)S(1)}, bf16[3072,64]{0,1:T(8,128)(2,1)}, u32[]{:S(2)}) copy-start(bf16[3072,64]{0,1:T(8,128)(2,1)} %param.21) | copy-start | bytes 1179652
  7.2 74.4 %all-gather.5.cloned.1.call-start = ((), (), s32[]{:S(2)}) async-start(), calls=%async_computation.2 | async-start | bytes 1622016 | tf_op jit(solution)/shard_map/all_gather | solution.py:174
  16.7 3.2 copy-start.14
  19.9 160.4 %all-gather.9.cloned.1.call-start = ((), (), s32[]{:S(2)}) async-start(), calls=%async_computation.6 | async-start | bytes 7569408 | tf_op jit(solution)/shard_map/all_gather | solution.py:216
  21.3 30.3 %collective-permute-start = (bf16[3072,192]{0,1:T(8,128)(2,1)}, bf16[3072,192]{0,1:T(8,128)(2,1)S(1)}, u32[]{:S(2)}, u32[]{:S(2)}) collective-permute-start(bf16[3072,192]{0,1:T(8,128)(2,1)} %get-tuple-element.42), channel_id=1, source_target_pairs={{0,1},{1,2},{2,3},{3,0},{4,5},{5,6},{6,7},{7,4},{8,9},{9,10},{10,1... | collective-permute-start | bytes 3538952 | tf_op jit(solution)/shard_map/ppermute | solution.py:180
  23.3 54.8 %collective-permute-start.1 = (bf16[3072,192]{0,1:T(8,128)(2,1)}, bf16[3072,192]{0,1:T(8,128)(2,1)S(1)}, u32[]{:S(2)}, u32[]{:S(2)}) collective-permute-start(bf16[3072,192]{0,1:T(8,128)(2,1)} %get-tuple-element.42), channel_id=1, source_target_pairs={{0,2},{1,3},{2,0},{3,1},{4,6},{5,7},{6,4},{7,5},{8,10},{9,11},{10,... | collective-permute-start | bytes 3538952 | tf_op jit(solution)/shard_map/ppermute | solution.py:180
  26.9 51.2 %collective-permute-start.2 = (bf16[3072,192]{0,1:T(8,128)(2,1)}, bf16[3072,192]{0,1:T(8,128)(2,1)}, u32[]{:S(2)}, u32[]{:S(2)}) collective-permute-start(bf16[3072,192]{0,1:T(8,128)(2,1)} %get-tuple-element.42), channel_id=1, source_target_pairs={{0,3},{1,0},{2,1},{3,2},{4,7},{5,4},{6,5},{7,6},{8,11},{9,8},{10,9... | collective-permute-start | bytes 3538952 | tf_op jit(solution)/shard_map/ppermute | solution.py:180
  90.9 2.6 copy-start.24
  91.0 5.9 %copy-start.4 = (bf16[16,2,8,48]{3,1,2,0:T(2,128)(2,1)S(1)}, bf16[16,2,8,48]{3,1,2,0:T(2,128)(2,1)}, u32[]{:S(2)}) copy-start(bf16[16,2,8,48]{3,1,2,0:T(2,128)(2,1)} %copy-done.3) | copy-start | bytes 73732
  91.0 5.9 %copy-start.6 = (bf16[16,2,8,48]{3,1,2,0:T(2,128)(2,1)S(1)}, bf16[16,2,8,48]{3,1,2,0:T(2,128)(2,1)}, u32[]{:S(2)}) copy-start(bf16[16,2,8,48]{3,1,2,0:T(2,128)(2,1)} %copy-done.5) | copy-start | bytes 73732
  91.0 6.1 %copy-start.20 = (bf16[8,8]{1,0:T(8,128)(2,1)S(1)}, bf16[8,8]{1,0:T(8,128)(2,1)}, u32[]{:S(2)}) copy-start(bf16[8,8]{1,0:T(8,128)(2,1)} %fusion.20) | copy-start | bytes 388
  93.3 134.8 %all-reduce.2.cloned.1.call-start = ((), (), s32[]{:S(2)}) async-start(), calls=%async_computation.3 | async-start | bytes 786432 | tf_op jit(solution)/shard_map/psum | solution.py:276
  129.2 1.9 copy-start.2
  129.2 2.1 copy-start.11
  129.2 3.4 copy-start.18
  182.3 3.3 copy-start.19
  182.3 47.1 %copy-start.23 = (f32[3072]{0:T(1024)S(1)}, f32[3072]{0:T(1024)}, u32[]{:S(2)}) copy-start(f32[3072]{0:T(1024)} %param.19) | copy-start | bytes 36868
  186.3 88.2 %all-gather.7.cloned.1.call-start = ((), (), s32[]{:S(2)}) async-start(), calls=%async_computation.4 | async-start | bytes 1622016 | tf_op jit(solution)/shard_map/all_gather | solution.py:281
  231.0 129.8 %reduce-scatter.2.cloned.1.call-start = ((), (), s32[]{:S(2)}) async-start(), calls=%async_computation.5 | async-start | bytes 3244032 | tf_op jit(solution)/shard_map/reduce_scatter | solution.py:290
  274.6 2.1 copy-start
  281.0 79.8 %copy-start.21 = (f32[3072]{0:T(1024)S(1)}, f32[3072]{0:T(1024)}, u32[]{:S(2)}) copy-start(f32[3072]{0:T(1024)} %param.24) | copy-start | bytes 36868
  281.0 79.8 %copy-start.22 = (f32[3072]{0:T(1024)S(1)}, f32[3072]{0:T(1024)}, u32[]{:S(2)}) copy-start(f32[3072]{0:T(1024)} %param.23) | copy-start | bytes 36868
  (9 other events, 10.3 us)
Sparse Core Ops, SparseCore 0:
  20.0 45.5 all-gather.4
  93.4 86.8 all-gather.8
  186.5 41.6 all-reduce.1
  231.1 43.4 all-gather.6
  281.2 79.6 reduce-scatter.1

commit v5 on v4

--- a/solution.py
+++ b/solution.py
@@ -86,6 +86,11 @@
     return pl.pallas_call(
         functools.partial(prompt_kernel, block_len, score_scale),
         grid_spec=spec,
+        cost_estimate=pl.CostEstimate(
+            flops=4 * rows * lanes * span,
+            transcendentals=rows * span,
+            bytes_accessed=cache.size * 2 + rows * lanes * 6,
+        ),
         out_shape=[
             jax.ShapeDtypeStruct((rows, lanes), jnp.float32),
             jax.ShapeDtypeStruct((rows, 1), jnp.float32),
@@ -130,6 +135,11 @@
     return pl.pallas_call(
         functools.partial(tail_kernel, score_scale),
         grid_spec=spec,
+        cost_estimate=pl.CostEstimate(
+            flops=4 * conts * rows * lanes * cap,
+            transcendentals=conts * rows * cap,
+            bytes_accessed=cache.size * 2 + conts * rows * lanes * 6,
+        ),
         out_shape=[
             jax.ShapeDtypeStruct((conts, rows, lanes), jnp.float32),
             jax.ShapeDtypeStruct((conts, rows, 1), jnp.float32),
@@ -212,7 +222,6 @@
         ],
         axis=1,
     )
-    packed, weights_all = lax.optimization_barrier((packed, weights_all))
     packed_all = lax.all_gather(packed[None], "req", axis=0, tiled=True)
     row_offset = req_index % 2 * rows_here
     slot_first = lax.dynamic_index_in_dim(slot_of, 2 * own_prompt, 0, keepdims=False)
@@ -267,17 +276,24 @@
         + numer_tail * scale_tail[..., None]
     )
     attn = (row_numer / row_total[:, :, None]).astype(jnp.bfloat16).reshape(rows_here, width_here)
+    attn, weights_all = lax.optimization_barrier((attn, weights_all))
     partial = jnp.dot(attn, w_out, preferred_element_type=jnp.float32)
     col_start = mlp_index * width_here
     own_cols = lax.dynamic_slice_in_dim(partial, col_start, width_here, 1)
     partial = lax.dynamic_update_slice_in_dim(
         partial, own_cols + residual.astype(jnp.float32), col_start, 1
     )
-    state = lax.psum(partial, "mlp")
-    mean_square = jnp.mean(state * state, axis=1, keepdims=True)
-    normed = (state * lax.rsqrt(mean_square + norm_eps) * mlp_gain).astype(jnp.bfloat16)
     share = rows_here // mlp_count
-    normed_share = lax.dynamic_slice_in_dim(normed, mlp_index * share, share, 0)
+    state_share = lax.dynamic_slice_in_dim(partial, mlp_index * share, share, 0)
+    for shift in range(1, mlp_count):
+        target = (mlp_index + shift) % mlp_count
+        state_share = state_share + lax.ppermute(
+            lax.dynamic_slice_in_dim(partial, target * share, share, 0),
+            "mlp",
+            [(m, (m + shift) % mlp_count) for m in range(mlp_count)],
+        )
+    mean_square = jnp.mean(state_share * state_share, axis=1, keepdims=True)
+    normed_share = (state_share * lax.rsqrt(mean_square + norm_eps) * mlp_gain).astype(jnp.bfloat16)
     piece = lax.all_gather(normed_share, "req", axis=0, tiled=True)
     hidden_here = w_gate.shape[1]
     gate_w = weights_all[:, :, :hidden_here]
@@ -288,13 +304,12 @@
     hidden_all = (jax.nn.silu(gate) * upper).astype(jnp.bfloat16)
     down_sum = jnp.einsum("rmj,mfj->rf", hidden_all, down_w, preferred_element_type=jnp.float32)
     row_sums = lax.psum_scatter(
-        down_sum,
+        down_sum.astype(jnp.bfloat16),
         "req",
         scatter_dimension=0,
         tiled=True,
     )
-    state_share = lax.dynamic_slice_in_dim(state, mlp_index * share, share, 0)
-    final_share = state_share + row_sums
+    final_share = state_share + row_sums.astype(jnp.float32)
     final_square = jnp.mean(final_share * final_share, axis=1)
     final_dot = jnp.sum(final_share * final_gain * score_weight, axis=1)
     score_share = final_dot * lax.rsqrt(final_square + norm_eps)

time: 381 us -> 334 us (0.88)
  waiting for transfers between devices: 257 us -> 169 us
  Pallas kernels: 34.2 us -> 69.8 us
    ppermute x3, waiting for transfers between devices: 48.9 us -> 0.01 us  [per_device(): lax.ppermute(weights_cat, 'mlp', [(m, (m + shift) % mlp_count) for m in r...]
    all_gather x1, waiting for transfers between devices: 45.6 us -> 0.01 us  [per_device(): packed_all = lax.all_gather(packed[None], 'req', axis=0, tiled=True)]
    all_gather x1, waiting for transfers between devices: 0.01 us -> 44.9 us  [per_device(): lax.all_gather(query.reshape(rows_here, width_here), 'req', axis=0, tiled...]
    psum x1 -> x0, waiting for transfers between devices: 41.8 us -> none  [per_device(): state = lax.psum(partial, 'mlp')]
    pallas_call x1, Pallas kernels: 3.4 us -> 39 us  [prompt_attention(): pl.pallas_call(functools.partial(prompt_kernel, block_len, score_scale),...]
    ppermute x0 -> x3, waiting for transfers between devices: none -> 6.12 us  [per_device(): lax.ppermute(lax.dynamic_slice_in_dim(partial, target * share, share, 0),...]
  transfers between devices with their start and end apart: 8 -> 10, of which waited for: 6 -> 6; matrix products, arithmetic and copies ran while one was open for 4% -> 6% of each run, Pallas kernels for 8% -> 9%
where the time goes in v5:
time: 334 us; the launch traced here: 333 us
  waiting for transfers between devices  169 us (51%)
  Pallas kernels  69.8 us (21%)
  local copies, waits for them, and re-layouts  25.2 us (8%)
  between operations  21.7 us (6%)
  other arithmetic  16.4 us (5%)
  matrix products  10.7 us (3%)
  blocking collectives  10.1 us (3%)
  starting transfers between devices  9.86 us (3%)
    reduce_scatter x1, waiting for transfers between devices, per_device(): lax.psum_scatter(down_sum.astype(jnp.bfloat16), 'req', scatter_dimension=...  77.6 us
    all_gather x1, waiting for transfers between devices, per_device(): lax.all_gather(query.reshape(rows_here, width_here), 'req', axis=0, tiled...  44.9 us
    all_gather x1, waiting for transfers between devices, per_device(): piece = lax.all_gather(normed_share, 'req', axis=0, tiled=True)  40.8 us
    pallas_call x1, Pallas kernels, prompt_attention(): pl.pallas_call(functools.partial(prompt_kernel, block_len, score_scale),...  39 us
    pallas_call x1, Pallas kernels, tail_attention(): pl.pallas_call(functools.partial(tail_kernel, score_scale), grid_spec=spe...  30.8 us
    all_to_all x1, blocking collectives, per_device(): lax.all_to_all(payload, 'mlp', split_axis=1, concat_axis=0, tiled=True)  10.1 us
  transfers between devices with their start and end apart: 10, of which 6 were waited for; matrix products, arithmetic and copies ran while one was open for 6% of the time, Pallas kernels for 9%

profile of v5, /device:TPU:0, one launch (start us, length us, event | category | flops | bytes accessed | tf_op | source)
XLA Modules:
  0.0 333.3 jit_solution(4937291888869402478)
XLA Ops:
  7.2 1.2 dynamic_slice.51
  11.1 1.4 fusion.28
  12.5 1.9 broadcast_add_fusion
  18.7 44.9 %all-gather.5.cloned.1.call-done = bf16[1024,768]{1,0:T(8,128)(2,1)} async-done(((bf16[32,768]{1,0:T(8,128)(2,1)}), bf16[1024,768]{1,0:T(8,128)(2,1)}) %all-gather.5.cloned.1.call-update) | async-done | bytes 1572880 | tf_op jit(solution)/shard_map/all_gather | solution.py:184
  64.9 1.8 reshape.155.q_ref
  66.6 39.0 %shard_map.149 = (f32[512,768]{1,0:T(8,128)}, f32[512,1]{1,0:T(8,128)}, f32[512,1]{1,0:T(8,128)}) custom-call(s32[1]{0:T(128)} %bitcast.2.valid_ref, bf16[512,768]{1,0:T(8,128)(2,1)} %reshape.155.q_ref, bf16[1,4096,2,768]{3,2,1,0:T(2,128)(2,1)} %cache_ref.2), custom_call_target="tpu_custom_call" | custom-call | flops 6442450944 | bytes 14942208 | tf_op jit(solution)/shard_map/pallas_call | solution.py:86
  108.8 2.2 reshape.156
  111.8 1.5 pad_maximum_fusion.2
  113.4 1.4 fusion.23
  114.8 3.2 collective-permute-start.1
  118.6 2.6 collective-permute-start.2
  123.4 30.8 %shard_map.150 = (f32[16,16,768]{2,1,0:T(8,128)}, f32[16,16,1]{2,1,0:T(8,128)}, f32[16,16,1]{2,1,0:T(8,128)}) custom-call(s32[16]{0:T(128)} %get-tuple-element.30.lens_ref, bf16[16,16,768]{2,1,0:T(8,128)(2,1)} %reshape.160.q_ref, bf16[16,256,2,768]{3,2,1,0:T(2,128)(2,1)} %cache_ref.3), custom_call_target="tpu_custom_call" | custom-call | flops 201326592 | bytes 13762560 | tf_op jit(solution)/shard_map/pallas_call | solution.py:135
  156.4 1.6 reshape.163
  168.4 3.7 %pad_maximum_fusion = bf16[4,3072,192]{1,2,0:T(8,128)(2,1)} fusion(bf16[1,3072,192]{1,2,0:T(8,128)(2,1)} %bitcast.48, bf16[1,3072,192]{1,2,0:T(8,128)(2,1)S(1)} %bitcast.148, bf16[1,3072,192]{1,2,0:T(8,128)(2,1)} %bitcast.46, bf16[1,3072,192]{1,2,0:T(8,128)(2,1)S(1)} %get-tuple-element.43), kind=kLoop, calls=%fused_computation | loop fusion | flops 7077888 | bytes 9437184 | tf_op jit(solution)/shard_map/stack | solution.py:187
  174.0 3.3 fusion.29
  177.4 3.2 collective-permute-start.5
  180.7 2.6 collective-permute-done.3
  183.9 2.9 collective-permute-done.4
  187.7 2.2 fusion.24
  189.9 40.8 %all-gather.7.cloned.1.call-done = bf16[256,3072]{1,0:T(8,128)(2,1)} async-done(((bf16[8,3072]{1,0:T(8,128)(2,1)}), bf16[256,3072]{1,0:T(8,128)(2,1)}) %all-gather.7.cloned.1.call-update) | async-done | bytes 1572880 | tf_op jit(solution)/shard_map/all_gather | solution.py:297
  230.7 2.1 fusion.30
  233.5 3.2 fusion
  236.7 77.6 %reduce-scatter.2.cloned.1.call-done = bf16[8,3072]{1,0:T(8,128)(2,1)} async-done(((bf16[256,3072]{1,0:T(8,128)(2,1)}), bf16[8,3072]{1,0:T(8,128)(2,1)}) %reduce-scatter.2.cloned.1.call-update) | async-done | bytes 49168 | tf_op jit(solution)/shard_map/reduce_scatter | solution.py:306
  315.4 10.1 %all_to_all.18 = f32[8,4,769]{2,0,1:T(8,128)S(1)} all-to-all(f32[8,4,769]{2,0,1:T(8,128)S(1)} %pad_maximum_fusion.3), channel_id=1, replica_groups=mesh['req'=32,'mlp'=4] {'mlp'}, dimensions={1} | all-to-all | bytes 196864 | tf_op jit(solution)/shard_map/all_to_all | solution.py:323
  (110 shorter events, 26.4 us)
Async XLA Ops:
  7.2 56.4 %all-gather.5.cloned.1.call-start = ((), (), s32[]{:S(2)}) async-start(), calls=%async_computation.2 | async-start | bytes 1622016 | tf_op jit(solution)/shard_map/all_gather | solution.py:184
  17.9 154.1 %all-gather.9.cloned.1.call-start = ((), (), s32[]{:S(2)}) async-start(), calls=%async_computation.5 | async-start | bytes 7569408 | tf_op jit(solution)/shard_map/all_gather | solution.py:225
  111.0 2.4 copy-start.1
  111.0 2.4 copy-start.2
  111.2 2.2 copy-start.3
  113.3 117.4 %all-gather.7.cloned.1.call-start = ((), (), s32[]{:S(2)}) async-start(), calls=%async_computation.3 | async-start | bytes 1622016 | tf_op jit(solution)/shard_map/all_gather | solution.py:297
  114.8 53.5 %collective-permute-start.1 = (bf16[3072,192]{0,1:T(8,128)(2,1)}, bf16[3072,192]{0,1:T(8,128)(2,1)S(1)}, u32[]{:S(2)}, u32[]{:S(2)}) collective-permute-start(bf16[3072,192]{0,1:T(8,128)(2,1)} %get-tuple-element.44), channel_id=1, source_target_pairs={{0,2},{1,3},{2,0},{3,1},{4,6},{5,7},{6,4},{7,5},{8,10},{9,11},{10,... | collective-permute-start | bytes 3538952 | tf_op jit(solution)/shard_map/ppermute | solution.py:190
  118.0 50.4 %collective-permute-start = (bf16[3072,192]{0,1:T(8,128)(2,1)}, bf16[3072,192]{0,1:T(8,128)(2,1)}, u32[]{:S(2)}, u32[]{:S(2)}) collective-permute-start(bf16[3072,192]{0,1:T(8,128)(2,1)} %get-tuple-element.44), channel_id=1, source_target_pairs={{0,1},{1,2},{2,3},{3,0},{4,5},{5,6},{6,7},{7,4},{8,9},{9,10},{10,1... | collective-permute-start | bytes 3538952 | tf_op jit(solution)/shard_map/ppermute | solution.py:190
  118.6 49.7 %collective-permute-start.2 = (bf16[3072,192]{0,1:T(8,128)(2,1)}, bf16[3072,192]{0,1:T(8,128)(2,1)}, u32[]{:S(2)}, u32[]{:S(2)}) collective-permute-start(bf16[3072,192]{0,1:T(8,128)(2,1)} %get-tuple-element.44), channel_id=1, source_target_pairs={{0,3},{1,0},{2,1},{3,2},{4,7},{5,4},{6,5},{7,6},{8,11},{9,8},{10,9... | collective-permute-start | bytes 3538952 | tf_op jit(solution)/shard_map/ppermute | solution.py:190
  174.0 3.3 copy-start.4
  174.0 12.9 %copy-start.7 = (f32[3072]{0:T(1024)S(1)}, f32[3072]{0:T(1024)}, u32[]{:S(2)}) copy-start(f32[3072]{0:T(1024)} %param.19) | copy-start | bytes 36868
  177.3 5.9 %collective-permute-start.3 = (f32[8,3072]{1,0:T(8,128)S(1)}, f32[8,3072]{1,0:T(8,128)S(1)}, u32[]{:S(2)}, u32[]{:S(2)}) collective-permute-start(f32[8,3072]{1,0:T(8,128)S(1)} %get-tuple-element.53), channel_id=1, source_target_pairs={{0,1},{1,2},{2,3},{3,0},{4,5},{5,6},{6,7},{7,4},{8,9},{9,10},{10,1... | collective-permute-start | bytes 294920 | tf_op jit(solution)/shard_map/ppermute | solution.py:290
  177.4 6.4 %collective-permute-start.5 = (f32[8,3072]{1,0:T(8,128)S(1)}, f32[8,3072]{1,0:T(8,128)S(1)}, u32[]{:S(2)}, u32[]{:S(2)}) collective-permute-start(f32[8,3072]{1,0:T(8,128)S(1)} %get-tuple-element.54), channel_id=1, source_target_pairs={{0,3},{1,0},{2,1},{3,2},{4,7},{5,4},{6,5},{7,6},{8,11},{9,8},{10,9... | collective-permute-start | bytes 294920 | tf_op jit(solution)/shard_map/ppermute | solution.py:290
  180.7 6.1 %collective-permute-start.4 = (f32[8,3072]{1,0:T(8,128)S(1)}, f32[8,3072]{1,0:T(8,128)S(1)}, u32[]{:S(2)}, u32[]{:S(2)}) collective-permute-start(f32[8,3072]{1,0:T(8,128)S(1)} %get-tuple-element.55), channel_id=1, source_target_pairs={{0,2},{1,3},{2,0},{3,1},{4,6},{5,7},{6,4},{7,5},{8,10},{9,11},{10,... | collective-permute-start | bytes 294920 | tf_op jit(solution)/shard_map/ppermute | solution.py:290
  187.7 126.7 %reduce-scatter.2.cloned.1.call-start = ((), (), s32[]{:S(2)}) async-start(), calls=%async_computation.4 | async-start | bytes 1622016 | tf_op jit(solution)/shard_map/reduce_scatter | solution.py:306
  230.7 2.1 copy-start
  236.7 77.6 %copy-start.5 = (f32[3072]{0:T(1024)S(1)}, f32[3072]{0:T(1024)}, u32[]{:S(2)}) copy-start(f32[3072]{0:T(1024)} %param.24) | copy-start | bytes 36868
  236.7 77.6 %copy-start.6 = (f32[3072]{0:T(1024)S(1)}, f32[3072]{0:T(1024)}, u32[]{:S(2)}) copy-start(f32[3072]{0:T(1024)} %param.23) | copy-start | bytes 36868
Sparse Core Ops, SparseCore 0:
  18.0 45.5 all-gather.4
  113.4 50.0 all-gather.8
  187.8 42.8 all-gather.6
  236.8 77.4 reduce-scatter.1

commit v6 on v5

--- a/solution.py
+++ b/solution.py
@@ -294,7 +294,13 @@
         )
     mean_square = jnp.mean(state_share * state_share, axis=1, keepdims=True)
     normed_share = (state_share * lax.rsqrt(mean_square + norm_eps) * mlp_gain).astype(jnp.bfloat16)
-    piece = lax.all_gather(normed_share, "req", axis=0, tiled=True)
+    piece = lax.all_to_all(
+        jnp.broadcast_to(normed_share[None], (req_count,) + normed_share.shape),
+        "req",
+        split_axis=0,
+        concat_axis=0,
+        tiled=True,
+    ).reshape(req_count * share, width)
     hidden_here = w_gate.shape[1]
     gate_w = weights_all[:, :, :hidden_here]
     up_w = weights_all[:, :, hidden_here : 2 * hidden_here]
@@ -303,13 +309,13 @@
     upper = jnp.einsum("rk,mkj->rmj", piece, up_w, preferred_element_type=jnp.float32)
     hidden_all = (jax.nn.silu(gate) * upper).astype(jnp.bfloat16)
     down_sum = jnp.einsum("rmj,mfj->rf", hidden_all, down_w, preferred_element_type=jnp.float32)
-    row_sums = lax.psum_scatter(
-        down_sum.astype(jnp.bfloat16),
-        "req",
-        scatter_dimension=0,
-        tiled=True,
-    )
-    final_share = state_share + row_sums.astype(jnp.float32)
+    row_sums = jnp.sum(
+        lax.all_to_all(
+            down_sum.reshape(req_count, share, width), "req", split_axis=0, concat_axis=0, tiled=True
+        ),
+        axis=0,
+    )
+    final_share = state_share + row_sums
     final_square = jnp.mean(final_share * final_share, axis=1)
     final_dot = jnp.sum(final_share * final_gain * score_weight, axis=1)
     score_share = final_dot * lax.rsqrt(final_square + norm_eps)

time: 334 us -> 287 us (0.86)
  waiting for transfers between devices: 169 us -> 69.8 us
  blocking collectives: 10.1 us -> 51.3 us
  starting transfers between devices: 9.86 us -> 27.3 us
  Pallas kernels: 69.8 us -> 60.9 us
  local copies, waits for them, and re-layouts: 25.2 us -> 30.5 us
    reduce_scatter x1 -> x0, waiting for transfers between devices: 77.6 us -> none  [per_device(): lax.psum_scatter(down_sum.astype(jnp.bfloat16), 'req', scatter_dimension=...]
    all_to_all x0 -> x1, blocking collectives: none -> 42.5 us  [per_device(): lax.all_to_all(down_sum.reshape(req_count, share, width), 'req', split_ax...]
    all_gather x1 -> x0, waiting for transfers between devices: 40.8 us -> none  [per_device(): piece = lax.all_gather(normed_share, 'req', axis=0, tiled=True)]
    all_to_all x0 -> x1, waiting for transfers between devices: none -> 19.8 us  [per_device(): lax.all_to_all(jnp.broadcast_to(normed_share[None], (req_count,) + normed...]
    all_to_all x0 -> x1, starting transfers between devices: none -> 15.6 us  [per_device(): lax.all_to_all(jnp.broadcast_to(normed_share[None], (req_count,) + normed...]
    pallas_call x1, Pallas kernels: 39 us -> 30.1 us  [prompt_attention(): pl.pallas_call(functools.partial(prompt_kernel, block_len, score_scale),...]
  transfers between devices with their start and end apart: 10 -> 9, of which waited for: 6 -> 6; matrix products, arithmetic and copies ran while one was open for 6% -> 7% of each run, Pallas kernels for 9% -> 11%
where the time goes in v6:
time: 287 us; the launch traced here: 286 us
  waiting for transfers between devices  69.8 us (24%)
  Pallas kernels  60.9 us (21%)
  blocking collectives  51.3 us (18%)
  local copies, waits for them, and re-layouts  30.5 us (11%)
  starting transfers between devices  27.3 us (10%)
  between operations  21.7 us (8%)
  other arithmetic  15.3 us (5%)
  matrix products  9.41 us (3%)
    all_gather x1, waiting for transfers between devices, per_device(): lax.all_gather(query.reshape(rows_here, width_here), 'req', axis=0, tiled...  45.1 us
    all_to_all x1, blocking collectives, per_device(): lax.all_to_all(down_sum.reshape(req_count, share, width), 'req', split_ax...  42.5 us
    pallas_call x1, Pallas kernels, tail_attention(): pl.pallas_call(functools.partial(tail_kernel, score_scale), grid_spec=spe...  30.8 us
    pallas_call x1, Pallas kernels, prompt_attention(): pl.pallas_call(functools.partial(prompt_kernel, block_len, score_scale),...  30.1 us
    all_to_all x1, waiting for transfers between devices, per_device(): lax.all_to_all(jnp.broadcast_to(normed_share[None], (req_count,) + normed...  19.8 us
    all_to_all x1, starting transfers between devices, per_device(): lax.all_to_all(jnp.broadcast_to(normed_share[None], (req_count,) + normed...  15.6 us
    all_to_all x1, blocking collectives, per_device(): lax.all_to_all(payload, 'mlp', split_axis=1, concat_axis=0, tiled=True)  8.79 us
    ppermute x3, starting transfers between devices, per_device(): lax.ppermute(weights_cat, 'mlp', [(m, (m + shift) % mlp_count) for m in r...  6.39 us
  transfers between devices with their start and end apart: 9, of which 6 were waited for; matrix products, arithmetic and copies ran while one was open for 7% of the time, Pallas kernels for 11%

profile of v6, /device:TPU:0, one launch (start us, length us, event | category | flops | bytes accessed | tf_op | source)
XLA Modules:
  0.0 286.1 jit_solution(15145596281488462766)
XLA Ops:
  12.4 1.9 broadcast_add_fusion
  18.8 45.1 %all-gather.4.cloned.1.call-done = bf16[1024,768]{1,0:T(8,128)(2,1)} async-done(((bf16[32,768]{1,0:T(8,128)(2,1)}), bf16[1024,768]{1,0:T(8,128)(2,1)}) %all-gather.4.cloned.1.call-update) | async-done | bytes 1572880 | tf_op jit(solution)/shard_map/all_gather | solution.py:184
  65.1 1.8 reshape.162.q_ref
  66.9 30.1 %shard_map.149 = (f32[512,768]{1,0:T(8,128)}, f32[512,1]{1,0:T(8,128)}, f32[512,1]{1,0:T(8,128)}) custom-call(s32[1]{0:T(128)} %bitcast.2.valid_ref, bf16[512,768]{1,0:T(8,128)(2,1)} %reshape.162.q_ref, bf16[1,4096,2,768]{3,2,1,0:T(2,128)(2,1)} %cache_ref.2), custom_call_target="tpu_custom_call" | custom-call | flops 6442450944 | bytes 14942208 | tf_op jit(solution)/shard_map/pallas_call | solution.py:86
  100.7 2.2 reshape.163
  105.2 1.5 pad_maximum_fusion.2
  106.8 1.4 fusion.26
  108.3 3.2 %collective-permute-start.1 = (bf16[3072,192]{0,1:T(8,128)(2,1)}, bf16[3072,192]{0,1:T(8,128)(2,1)S(1)}, u32[]{:S(2)}, u32[]{:S(2)}) collective-permute-start(bf16[3072,192]{0,1:T(8,128)(2,1)} %get-tuple-element.44), channel_id=1, source_target_pairs={{0,2},{1,3},{2,0},{3,1},{4,6},{5,7},{6,4},{7,5},{8,10},{9,11},{10,... | collective-permute-start | bytes 3538952 | tf_op jit(solution)/shard_map/ppermute | solution.py:190
  112.1 2.6 collective-permute-start.2
  116.9 30.8 %shard_map.150 = (f32[16,16,768]{2,1,0:T(8,128)}, f32[16,16,1]{2,1,0:T(8,128)}, f32[16,16,1]{2,1,0:T(8,128)}) custom-call(s32[16]{0:T(128)} %get-tuple-element.30.lens_ref, bf16[16,16,768]{2,1,0:T(8,128)(2,1)} %reshape.167.q_ref, bf16[16,256,2,768]{3,2,1,0:T(2,128)(2,1)} %cache_ref.3), custom_call_target="tpu_custom_call" | custom-call | flops 201326592 | bytes 13762560 | tf_op jit(solution)/shard_map/pallas_call | solution.py:135
  149.8 1.6 reshape.170
  161.6 3.7 %pad_maximum_fusion = bf16[4,3072,192]{1,2,0:T(8,128)(2,1)} fusion(bf16[1,3072,192]{1,2,0:T(8,128)(2,1)} %bitcast.48, bf16[1,3072,192]{1,2,0:T(8,128)(2,1)S(1)} %bitcast.151, bf16[1,3072,192]{1,2,0:T(8,128)(2,1)} %bitcast.46, bf16[1,3072,192]{1,2,0:T(8,128)(2,1)S(1)} %get-tuple-element.43), kind=kLoop, calls=%fused_computation | loop fusion | flops 7077888 | bytes 9437184 | tf_op jit(solution)/shard_map/stack | solution.py:187
  167.9 3.3 %fusion.32 = f32[32,3072]{1,0:T(8,128)S(1)} fusion(bf16[32,768]{1,0:T(8,128)(2,1)S(1)} %fusion.10, bf16[768,3072]{1,0:T(8,128)(2,1)} %param.18), kind=kOutput, calls=%fused_computation.104 | convolution fusion | flops 150994944 | bytes 5160960 | tf_op jit(solution)/shard_map/dot_general | solution.py:280
  171.3 1.6 collective-permute-start.3
  172.9 1.7 collective-permute-start.5
  174.6 1.9 collective-permute-start.4
  177.9 2.9 collective-permute-done.4
  182.3 15.6 %all-to-all-start = ((bf16[32,8,3072]{2,1,0:T(8,128)(2,1)}), bf16[32,8,3072]{2,1,0:T(8,128)(2,1)S(1)}, u32[]{:S(2)}, u32[]{:S(2)}) async-start(bf16[32,8,3072]{2,1,0:T(8,128)(2,1)} %broadcast_in_dim.35), calls=%async_computation | async-start | bytes 3145728 | tf_op jit(solution)/shard_map/all_to_all | solution.py:297
  197.9 3.3 %fusion.27 = (bf16[4,3072,64]{1,2,0:T(8,128)(2,1)}, bf16[4,3072,64]{1,2,0:T(8,128)(2,1)S(1)}) fusion(bf16[4,3072,192]{1,2,0:T(8,128)(2,1)} %pad_maximum_fusion), kind=kLoop, calls=%fused_computation.99 | loop fusion | bytes 6291456 | tf_op jit(solution)/shard_map/slice | solution.py:305
  201.3 19.8 %all-to-all-done = bf16[32,8,3072]{2,1,0:T(8,128)(2,1)S(1)} async-done(((bf16[32,8,3072]{2,1,0:T(8,128)(2,1)}), bf16[32,8,3072]{2,1,0:T(8,128)(2,1)S(1)}, u32[]{:S(2)}, u32[]{:S(2)}) %all-to-all-start) | async-done | bytes 1572896 | tf_op jit(solution)/shard_map/all_to_all | solution.py:297
  221.1 2.0 fusion.2
  223.7 2.1 convolution_bitcast_fusion
  225.7 42.5 %all_to_all.28 = f32[32,8,3072]{2,1,0:T(8,128)S(1)} all-to-all(f32[32,8,3072]{2,1,0:T(8,128)S(1)} %convolution_bitcast_fusion), channel_id=1, replica_groups=mesh['req'=32,'mlp'=4] {'req'}, dimensions={0} | all-to-all | bytes 6291456 | tf_op jit(solution)/shard_map/all_to_all | solution.py:313
  269.2 8.8 %all_to_all.29 = f32[8,4,769]{2,0,1:T(8,128)S(1)} all-to-all(f32[8,4,769]{2,0,1:T(8,128)S(1)} %pad_maximum_fusion.3), channel_id=1, replica_groups=mesh['req'=32,'mlp'=4] {'mlp'}, dimensions={1} | all-to-all | bytes 196864 | tf_op jit(solution)/shard_map/all_to_all | solution.py:329
  (119 shorter events, 33.1 us)
Async XLA Ops:
  7.2 56.7 %all-gather.4.cloned.1.call-start = ((), (), s32[]{:S(2)}) async-start(), calls=%async_computation.3 | async-start | bytes 1622016 | tf_op jit(solution)/shard_map/all_gather | solution.py:184
  16.5 0.6 copy-start.5
  17.3 49.5 %copy-start.3 = (bf16[16,2,8,96]{3,1,2,0:T(2,128)(2,1)}, bf16[16,2,8,96]{3,1,2,0:T(2,128)(2,1)S(1)}, u32[]{:S(2)}) copy-start(bf16[16,2,8,96]{3,1,2,0:T(2,128)(2,1)S(1)} %maximum_convert_fusion) | copy-start | bytes 147460
  18.1 147.8 %all-gather.6.cloned.1.call-start = ((), (), s32[]{:S(2)}) async-start(), calls=%async_computation.4 | async-start | bytes 7569408 | tf_op jit(solution)/shard_map/all_gather | solution.py:225
  18.8 48.1 %copy-start.8 = (bf16[8,8]{1,0:T(8,128)(2,1)}, bf16[8,8]{1,0:T(8,128)(2,1)S(1)}, u32[]{:S(2)}) copy-start(bf16[8,8]{1,0:T(8,128)(2,1)S(1)} %fusion.22) | copy-start | bytes 388
  102.9 3.9 %copy-start = (bf16[64,3072]{1,0:T(8,128)(2,1)S(1)}, bf16[64,3072]{1,0:T(8,128)(2,1)}, u32[]{:S(2)}) copy-start(bf16[64,3072]{1,0:T(8,128)(2,1)} %param.22) | copy-start | bytes 1179652
  102.9 3.9 %copy-start.1 = (bf16[3072,64]{0,1:T(8,128)(2,1)S(1)}, bf16[3072,64]{0,1:T(8,128)(2,1)}, u32[]{:S(2)}) copy-start(bf16[3072,64]{0,1:T(8,128)(2,1)} %param.21) | copy-start | bytes 1179652
  102.9 3.9 %copy-start.2 = (bf16[3072,64]{0,1:T(8,128)(2,1)S(1)}, bf16[3072,64]{0,1:T(8,128)(2,1)}, u32[]{:S(2)}) copy-start(bf16[3072,64]{0,1:T(8,128)(2,1)} %param.20) | copy-start | bytes 1179652
  106.8 7.8 %copy-start.6 = (f32[16,2,48]{2,1,0:T(2,128)S(1)}, f32[16,2,48]{2,1,0:T(2,128)}, u32[]{:S(2)}) copy-start(f32[16,2,48]{2,1,0:T(2,128)} %copy-done.5) | copy-start | bytes 18436
  106.8 8.1 %copy-start.4 = (bf16[16,2,8,96]{3,1,2,0:T(2,128)(2,1)S(1)}, bf16[16,2,8,96]{3,1,2,0:T(2,128)(2,1)}, u32[]{:S(2)}) copy-start(bf16[16,2,8,96]{3,1,2,0:T(2,128)(2,1)} %copy-done.3) | copy-start | bytes 147460
  106.8 8.8 %copy-start.9 = (bf16[8,8]{1,0:T(8,128)(2,1)S(1)}, bf16[8,8]{1,0:T(8,128)(2,1)}, u32[]{:S(2)}) copy-start(bf16[8,8]{1,0:T(8,128)(2,1)} %copy-done.8) | copy-start | bytes 388
  108.3 53.3 %collective-permute-start.1 = (bf16[3072,192]{0,1:T(8,128)(2,1)}, bf16[3072,192]{0,1:T(8,128)(2,1)S(1)}, u32[]{:S(2)}, u32[]{:S(2)}) collective-permute-start(bf16[3072,192]{0,1:T(8,128)(2,1)} %get-tuple-element.44), channel_id=1, source_target_pairs={{0,2},{1,3},{2,0},{3,1},{4,6},{5,7},{6,4},{7,5},{8,10},{9,11},{10,... | collective-permute-start | bytes 3538952 | tf_op jit(solution)/shard_map/ppermute | solution.py:190
  111.4 50.2 %collective-permute-start = (bf16[3072,192]{0,1:T(8,128)(2,1)}, bf16[3072,192]{0,1:T(8,128)(2,1)}, u32[]{:S(2)}, u32[]{:S(2)}) collective-permute-start(bf16[3072,192]{0,1:T(8,128)(2,1)} %get-tuple-element.44), channel_id=1, source_target_pairs={{0,1},{1,2},{2,3},{3,0},{4,5},{5,6},{6,7},{7,4},{8,9},{9,10},{10,1... | collective-permute-start | bytes 3538952 | tf_op jit(solution)/shard_map/ppermute | solution.py:190
  112.1 49.5 %collective-permute-start.2 = (bf16[3072,192]{0,1:T(8,128)(2,1)}, bf16[3072,192]{0,1:T(8,128)(2,1)}, u32[]{:S(2)}, u32[]{:S(2)}) collective-permute-start(bf16[3072,192]{0,1:T(8,128)(2,1)} %get-tuple-element.44), channel_id=1, source_target_pairs={{0,3},{1,0},{2,1},{3,2},{4,7},{5,4},{6,5},{7,6},{8,11},{9,8},{10,9... | collective-permute-start | bytes 3538952 | tf_op jit(solution)/shard_map/ppermute | solution.py:190
  167.9 3.3 %copy-start.7 = (bf16[32,768]{1,0:T(8,128)(2,1)S(1)}, bf16[32,768]{1,0:T(8,128)(2,1)}, u32[]{:S(2)}) copy-start(bf16[32,768]{1,0:T(8,128)(2,1)} %param.17) | copy-start | bytes 147460
  167.9 13.0 %copy-start.12 = (f32[3072]{0:T(1024)S(1)}, f32[3072]{0:T(1024)}, u32[]{:S(2)}) copy-start(f32[3072]{0:T(1024)} %param.19) | copy-start | bytes 36868
  171.3 6.2 %collective-permute-start.3 = (f32[8,3072]{1,0:T(8,128)S(1)}, f32[8,3072]{1,0:T(8,128)S(1)}, u32[]{:S(2)}, u32[]{:S(2)}) collective-permute-start(f32[8,3072]{1,0:T(8,128)S(1)} %get-tuple-element.53), channel_id=1, source_target_pairs={{0,1},{1,2},{2,3},{3,0},{4,5},{5,6},{6,7},{7,4},{8,9},{9,10},{10,1... | collective-permute-start | bytes 294920 | tf_op jit(solution)/shard_map/ppermute | solution.py:290
  172.9 5.0 %collective-permute-start.5 = (f32[8,3072]{1,0:T(8,128)S(1)}, f32[8,3072]{1,0:T(8,128)S(1)}, u32[]{:S(2)}, u32[]{:S(2)}) collective-permute-start(f32[8,3072]{1,0:T(8,128)S(1)} %get-tuple-element.54), channel_id=1, source_target_pairs={{0,3},{1,0},{2,1},{3,2},{4,7},{5,4},{6,5},{7,6},{8,11},{9,8},{10,9... | collective-permute-start | bytes 294920 | tf_op jit(solution)/shard_map/ppermute | solution.py:290
  174.6 6.2 %collective-permute-start.4 = (f32[8,3072]{1,0:T(8,128)S(1)}, f32[8,3072]{1,0:T(8,128)S(1)}, u32[]{:S(2)}, u32[]{:S(2)}) collective-permute-start(f32[8,3072]{1,0:T(8,128)S(1)} %get-tuple-element.55), channel_id=1, source_target_pairs={{0,2},{1,3},{2,0},{3,1},{4,6},{5,7},{6,4},{7,5},{8,10},{9,11},{10,... | collective-permute-start | bytes 294920 | tf_op jit(solution)/shard_map/ppermute | solution.py:290
  182.3 38.7 %all-to-all-start = ((bf16[32,8,3072]{2,1,0:T(8,128)(2,1)}), bf16[32,8,3072]{2,1,0:T(8,128)(2,1)S(1)}, u32[]{:S(2)}, u32[]{:S(2)}) async-start(bf16[32,8,3072]{2,1,0:T(8,128)(2,1)} %broadcast_in_dim.35), calls=%async_computation | async-start | bytes 3145728 | tf_op jit(solution)/shard_map/all_to_all | solution.py:297
  268.2 0.7 copy-start.10
  268.2 0.7 copy-start.11
Sparse Core Ops, SparseCore 0:
  18.2 45.5 all-gather.3
  106.9 59.0 all-gather.5

commit v7 on v6

--- a/solution.py
+++ b/solution.py
@@ -182,6 +182,14 @@
     key_new = rotary(block[:, :, 1].astype(jnp.float32), position).astype(jnp.bfloat16)
     value_new = block[:, :, 2]
     gathered = lax.all_gather(query.reshape(rows_here, width_here), "req", axis=0, tiled=True)
+    eye = jnp.eye(heads_here, dtype=jnp.bfloat16)
+    tail_diag = jnp.einsum("cthd,hg->chtgd", query, eye).reshape(
+        conts_here, heads_here * 2, width_here
+    )
+    tail_acc, tail_top, tail_sum = tail_attention(tail_diag, tail_cache, tail_here, score_scale)
+    gathered, tail_acc, tail_top, tail_sum = lax.optimization_barrier(
+        (gathered, tail_acc, tail_top, tail_sum)
+    )
     mlp_count = lax.axis_size("mlp")
     weights_cat = jnp.concatenate([w_gate, w_up, jnp.transpose(w_down)], axis=1)
     weights_all = jnp.stack(
@@ -207,7 +215,6 @@
     )
     owned_len = lax.dynamic_index_in_dim(prompt_len, owned_prompt, 0, keepdims=False)
     valid_count = jnp.clip(owned_len - held_half * span, 0, span)
-    eye = jnp.eye(heads_here, dtype=jnp.bfloat16)
     q_diag = jnp.einsum("rhd,hg->hrgd", q_owned, eye).reshape(heads_here * owned_rows, width_here)
     prompt_acc, prompt_top, prompt_sum = prompt_attention(q_diag, prompt_cache, valid_count, score_scale)
     prompt_acc = prompt_acc.reshape(heads_here, owned_rows, heads_here, HD)
@@ -239,10 +246,6 @@
     numer_first, total_first, max_first = part_of(slot_first)
     numer_second, total_second, max_second = part_of(slot_second)
 
-    tail_diag = jnp.einsum("cthd,hg->chtgd", query, eye).reshape(
-        conts_here, heads_here * 2, width_here
-    )
-    tail_acc, tail_top, tail_sum = tail_attention(tail_diag, tail_cache, tail_here, score_scale)
     tail_acc = tail_acc.reshape(conts_here, heads_here, 2, heads_here, HD)
     cache_numer = jnp.stack([tail_acc[:, h, :, h, :] for h in range(heads_here)], axis=2)
     cache_top = tail_top.reshape(conts_here, heads_here, 2)
@@ -311,8 +314,12 @@
     down_sum = jnp.einsum("rmj,mfj->rf", hidden_all, down_w, preferred_element_type=jnp.float32)
     row_sums = jnp.sum(
         lax.all_to_all(
-            down_sum.reshape(req_count, share, width), "req", split_axis=0, concat_axis=0, tiled=True
-        ),
+            down_sum.astype(jnp.bfloat16).reshape(req_count, share, width),
+            "req",
+            split_axis=0,
+            concat_axis=0,
+            tiled=True,
+        ).astype(jnp.float32),
         axis=0,
     )
     final_share = state_share + row_sums
@@ -326,9 +333,23 @@
         ],
         axis=2,
     )
-    arrived = lax.all_to_all(payload, "mlp", split_axis=1, concat_axis=0, tiled=True)
-    out_rows = arrived[:, 0, :width_here].astype(jnp.bfloat16)
-    scores = arrived[:, 0, width_here]
+    arrived = lax.dynamic_update_slice_in_dim(
+        jnp.zeros((rows_here, width_here + 1), jnp.float32),
+        lax.dynamic_index_in_dim(payload, mlp_index, 1, keepdims=False),
+        mlp_index * share,
+        0,
+    )
+    for shift in range(1, mlp_count):
+        target = (mlp_index + shift) % mlp_count
+        source = (mlp_index + mlp_count - shift) % mlp_count
+        got = lax.ppermute(
+            lax.dynamic_index_in_dim(payload, target, 1, keepdims=False),
+            "mlp",
+            [(m, (m + shift) % mlp_count) for m in range(mlp_count)],
+        )
+        arrived = lax.dynamic_update_slice_in_dim(arrived, got, source * share, 0)
+    out_rows = arrived[:, :width_here].astype(jnp.bfloat16)
+    scores = arrived[:, width_here]
     return (out_rows, scores)
 
 

time: 287 us -> 272 us (0.948)
  waiting for transfers between devices: 69.8 us -> 124 us
  blocking collectives: 51.3 us -> 0 us
  Pallas kernels: 60.9 us -> 34.2 us
  starting transfers between devices: 27.3 us -> 38.1 us
  local copies, waits for them, and re-layouts: 30.5 us -> 26.9 us
    all_to_all x2 -> x0, blocking collectives: 51.3 us -> none  [the longest x1 42.5 us: per_device(): lax.all_to_all(down_sum.reshape(req_count, share, width), 'req', split_ax...]
    ppermute x3, waiting for transfers between devices: 0.01 us -> 40.1 us  [per_device(): lax.ppermute(weights_cat, 'mlp', [(m, (m + shift) % mlp_count) for m in r...]
    all_gather x1, waiting for transfers between devices: 45.1 us -> 12.7 us  [per_device(): lax.all_gather(query.reshape(rows_here, width_here), 'req', axis=0, tiled...]
    pallas_call x1, Pallas kernels: 30.1 us -> 3.41 us  [prompt_attention(): pl.pallas_call(functools.partial(prompt_kernel, block_len, score_scale),...]
    all_to_all x0 -> x1, waiting for transfers between devices: none -> 23.1 us  [per_device(): lax.all_to_all(down_sum.astype(jnp.bfloat16).reshape(req_count, share, wi...]
    all_gather x1, waiting for transfers between devices: 0.63 us -> 21.1 us  [per_device(): packed_all = lax.all_gather(packed[None], 'req', axis=0, tiled=True)]
    ppermute x0 -> x3, starting transfers between devices: none -> 4.42 us  [per_device(): lax.ppermute(lax.dynamic_index_in_dim(payload, target, 1, keepdims=False)...]
    all_to_all x0 -> x1, starting transfers between devices: none -> 3.97 us  [per_device(): lax.all_to_all(down_sum.astype(jnp.bfloat16).reshape(req_count, share, wi...]
  transfers between devices with their start and end apart: 9 -> 13, of which waited for: 6 -> 11; matrix products, arithmetic and copies ran while one was open for 7% -> 7% of each run, Pallas kernels for 11% -> 11%
where the time goes in v7:
time: 272 us; the launch traced here: 271 us
  waiting for transfers between devices  124 us (46%)
  starting transfers between devices  38.1 us (14%)
  Pallas kernels  34.2 us (13%)
  local copies, waits for them, and re-layouts  26.9 us (10%)
  between operations  21.9 us (8%)
  other arithmetic  14.5 us (5%)
  matrix products  11.3 us (4%)
    ppermute x3, waiting for transfers between devices, per_device(): lax.ppermute(weights_cat, 'mlp', [(m, (m + shift) % mlp_count) for m in r...  40.1 us
    pallas_call x1, Pallas kernels, tail_attention(): pl.pallas_call(functools.partial(tail_kernel, score_scale), grid_spec=spe...  30.8 us
    all_to_all x1, waiting for transfers between devices, per_device(): lax.all_to_all(down_sum.astype(jnp.bfloat16).reshape(req_count, share, wi...  23.1 us
    all_gather x1, waiting for transfers between devices, per_device(): packed_all = lax.all_gather(packed[None], 'req', axis=0, tiled=True)  21.1 us
    all_to_all x1, waiting for transfers between devices, per_device(): lax.all_to_all(jnp.broadcast_to(normed_share[None], (req_count,) + normed...  19.8 us
    all_to_all x1, starting transfers between devices, per_device(): lax.all_to_all(jnp.broadcast_to(normed_share[None], (req_count,) + normed...  17.9 us
    all_gather x1, waiting for transfers between devices, per_device(): lax.all_gather(query.reshape(rows_here, width_here), 'req', axis=0, tiled...  12.7 us
    ppermute x3, starting transfers between devices, per_device(): lax.ppermute(lax.dynamic_slice_in_dim(partial, target * share, share, 0),...  5.85 us
  transfers between devices with their start and end apart: 13, of which 11 were waited for; matrix products, arithmetic and copies ran while one was open for 7% of the time, Pallas kernels for 11%

profile of v7, /device:TPU:0, one launch (start us, length us, event | category | flops | bytes accessed | tf_op | source)
XLA Modules:
  0.0 270.8 jit_solution(3999877359828121106)
XLA Ops:
  12.5 2.0 broadcast_add_fusion
  21.5 30.8 %shard_map.149 = (f32[16,16,768]{2,1,0:T(8,128)}, f32[16,16,1]{2,1,0:T(8,128)}, f32[16,16,1]{2,1,0:T(8,128)}) custom-call(s32[16]{0:T(128)} %get-tuple-element.38.lens_ref, bf16[16,16,768]{2,1,0:T(8,128)(2,1)} %reshape.159.q_ref, bf16[16,256,2,768]{3,2,1,0:T(2,128)(2,1)} %cache_ref.2), custom_call_target="tpu_custom_call" | custom-call | flops 201326592 | bytes 13762560 | tf_op jit(solution)/shard_map/pallas_call | solution.py:135
  52.3 12.7 %all-gather.4.cloned.1.call-done = bf16[1024,768]{1,0:T(8,128)(2,1)} async-done(((bf16[32,768]{1,0:T(8,128)(2,1)}), bf16[1024,768]{1,0:T(8,128)(2,1)}) %all-gather.4.cloned.1.call-update) | async-done | bytes 1572880 | tf_op jit(solution)/shard_map/all_gather | solution.py:184
  66.3 1.8 reshape.162.q_ref
  68.1 3.4 %shard_map.150 = (f32[512,768]{1,0:T(8,128)}, f32[512,1]{1,0:T(8,128)}, f32[512,1]{1,0:T(8,128)}) custom-call(s32[1]{0:T(128)} %bitcast.2.valid_ref, bf16[512,768]{1,0:T(8,128)(2,1)} %reshape.162.q_ref, bf16[1,4096,2,768]{3,2,1,0:T(2,128)(2,1)} %cache_ref.3), custom_call_target="tpu_custom_call" | custom-call | flops 6442450944 | bytes 14942208 | tf_op jit(solution)/shard_map/pallas_call | solution.py:86
  71.5 2.2 reshape.163
  81.3 2.9 %collective-permute-start.1 = (bf16[3072,192]{0,1:T(8,128)(2,1)}, bf16[3072,192]{0,1:T(8,128)(2,1)S(1)}, u32[]{:S(2)}, u32[]{:S(2)}) collective-permute-start(bf16[3072,192]{0,1:T(8,128)(2,1)} %get-tuple-element.52), channel_id=1, source_target_pairs={{0,2},{1,3},{2,0},{3,1},{4,6},{5,7},{6,4},{7,5},{8,10},{9,11},{10,... | collective-permute-start | bytes 3538952 | tf_op jit(solution)/shard_map/ppermute | solution.py:198
  90.8 1.8 fusion.15
  95.7 13.7 %collective-permute-done = bf16[3072,192]{0,1:T(8,128)(2,1)S(1)} collective-permute-done((bf16[3072,192]{0,1:T(8,128)(2,1)}, bf16[3072,192]{0,1:T(8,128)(2,1)S(1)}, u32[]{:S(2)}, u32[]{:S(2)}) %collective-permute-start) | collective-permute-done | bytes 1179680 | tf_op jit(solution)/shard_map/ppermute | solution.py:198
  109.4 26.5 %collective-permute-done.1 = bf16[3072,192]{0,1:T(8,128)(2,1)S(1)} collective-permute-done((bf16[3072,192]{0,1:T(8,128)(2,1)}, bf16[3072,192]{0,1:T(8,128)(2,1)S(1)}, u32[]{:S(2)}, u32[]{:S(2)}) %collective-permute-start.1) | collective-permute-done | bytes 1179680 | tf_op jit(solution)/shard_map/ppermute | solution.py:198
  135.8 3.5 %pad_maximum_fusion = bf16[4,3072,192]{1,2,0:T(8,128)(2,1)} fusion(bf16[1,3072,192]{1,2,0:T(8,128)(2,1)} %bitcast.48, bf16[1,3072,192]{1,2,0:T(8,128)(2,1)S(1)} %bitcast.159, bf16[1,3072,192]{1,2,0:T(8,128)(2,1)S(1)} %bitcast.158, bf16[1,3072,192]{1,2,0:T(8,128)(2,1)S(1)} %get-tuple-element.51), kind=kLoop, calls=%fused_computation | loop fusion | flops 7077888 | bytes 9437184 | tf_op jit(solution)/shard_map/stack | solution.py:195
  142.7 21.1 %all-gather.6.cloned.1.call-done = f32[2048,784]{1,0:T(8,128)} async-done(((f32[64,784]{1,0:T(8,128)}), f32[2048,784]{1,0:T(8,128)}) %all-gather.6.cloned.1.call-update) | async-done | bytes 6422544 | tf_op jit(solution)/shard_map/all_gather | solution.py:232
  165.8 3.3 %fusion.42 = f32[32,3072]{1,0:T(8,128)S(1)} fusion(bf16[32,768]{1,0:T(8,128)(2,1)S(1)} %fusion.12, bf16[768,3072]{1,0:T(8,128)(2,1)} %param.18), kind=kOutput, calls=%fused_computation.125 | convolution fusion | flops 150994944 | bytes 5160960 | tf_op jit(solution)/shard_map/dot_general | solution.py:283
  169.2 1.7 collective-permute-start.3
  170.9 2.8 %collective-permute-start.4 = (f32[8,3072]{1,0:T(8,128)S(1)}, f32[8,3072]{1,0:T(8,128)S(1)}, u32[]{:S(2)}, u32[]{:S(2)}) collective-permute-start(f32[8,3072]{1,0:T(8,128)S(1)} %get-tuple-element.63), channel_id=1, source_target_pairs={{0,2},{1,3},{2,0},{3,1},{4,6},{5,7},{6,4},{7,5},{8,10},{9,11},{10,... | collective-permute-start | bytes 294920 | tf_op jit(solution)/shard_map/ppermute | solution.py:293
  175.4 3.3 %collective-permute-done.4 = f32[8,3072]{1,0:T(8,128)S(1)} collective-permute-done((f32[8,3072]{1,0:T(8,128)S(1)}, f32[8,3072]{1,0:T(8,128)S(1)}, u32[]{:S(2)}, u32[]{:S(2)}) %collective-permute-start.4) | collective-permute-done | bytes 98336 | tf_op jit(solution)/shard_map/ppermute | solution.py:293
  180.3 17.9 %all-to-all-start = ((bf16[32,8,3072]{2,1,0:T(8,128)(2,1)}), bf16[32,8,3072]{2,1,0:T(8,128)(2,1)S(1)}, u32[]{:S(2)}, u32[]{:S(2)}) async-start(bf16[32,8,3072]{2,1,0:T(8,128)(2,1)} %broadcast_in_dim.38), calls=%async_computation | async-start | bytes 3145728 | tf_op jit(solution)/shard_map/all_to_all | solution.py:300
  198.2 3.3 %fusion.37 = (bf16[4,3072,64]{1,2,0:T(8,128)(2,1)}, bf16[4,3072,64]{1,2,0:T(8,128)(2,1)S(1)}) fusion(bf16[4,3072,192]{1,2,0:T(8,128)(2,1)} %pad_maximum_fusion), kind=kLoop, calls=%fused_computation.120 | loop fusion | bytes 6291456 | tf_op jit(solution)/shard_map/slice | solution.py:308
  201.5 19.8 %all-to-all-done = bf16[32,8,3072]{2,1,0:T(8,128)(2,1)S(1)} async-done(((bf16[32,8,3072]{2,1,0:T(8,128)(2,1)}), bf16[32,8,3072]{2,1,0:T(8,128)(2,1)S(1)}, u32[]{:S(2)}, u32[]{:S(2)}) %all-to-all-start) | async-done | bytes 1572896 | tf_op jit(solution)/shard_map/all_to_all | solution.py:300
  221.3 2.0 fusion.4
  224.0 3.2 %fusion.1 = bf16[32,8,3072]{2,1,0:T(8,128)(2,1)} fusion(bf16[4,3072,192]{1,2,0:T(8,128)(2,1)} %pad_maximum_fusion, f32[256,4,64]{0,2,1:T(8,128)S(1)} %bitcast.165, f32[256,4,64]{0,2,1:T(8,128)S(1)} %bitcast.164), kind=kOutput, calls=%fused_computation.3 | convolution fusion | flops 403832832 | bytes 3670016 | tf_op jit(solution)/shard_map/rmj,mfj->rf/dot_general | solution.py:314
  227.2 4.0 %all-to-all-start.1 = ((bf16[32,8,3072]{2,1,0:T(8,128)(2,1)}), bf16[32,8,3072]{2,1,0:T(8,128)(2,1)S(1)}, u32[]{:S(2)}, u32[]{:S(2)}) async-start(bf16[32,8,3072]{2,1,0:T(8,128)(2,1)} %fusion.1), calls=%async_computation.1 | async-start | bytes 3145728 | tf_op jit(solution)/shard_map/all_to_all | solution.py:316
  231.2 23.1 %all-to-all-done.1 = bf16[32,8,3072]{2,1,0:T(8,128)(2,1)S(1)} async-done(((bf16[32,8,3072]{2,1,0:T(8,128)(2,1)}), bf16[32,8,3072]{2,1,0:T(8,128)(2,1)S(1)}, u32[]{:S(2)}, u32[]{:S(2)}) %all-to-all-start.1) | async-done | bytes 1572896 | tf_op jit(solution)/shard_map/all_to_all | solution.py:316
  255.9 3.0 %collective-permute-start.7 = (f32[8,769]{1,0:T(8,128)S(1)}, f32[8,769]{1,0:T(8,128)S(1)}, u32[]{:S(2)}, u32[]{:S(2)}) collective-permute-start(f32[8,769]{1,0:T(8,128)S(1)} %get-tuple-element.73), channel_id=1, source_target_pairs={{0,2},{1,3},{2,0},{3,1},{4,6},{5,7},{6,4},{7,5},{8,10},{9,11},{10,... | collective-permute-start | bytes 73832 | tf_op jit(solution)/shard_map/ppermute | solution.py:345
  (136 shorter events, 39.1 us)
Async XLA Ops:
  7.2 57.9 %all-gather.4.cloned.1.call-start = ((), (), s32[]{:S(2)}) async-start(), calls=%async_computation.2 | async-start | bytes 1622016 | tf_op jit(solution)/shard_map/all_gather | solution.py:184
  19.2 144.6 %all-gather.6.cloned.1.call-start = ((), (), s32[]{:S(2)}) async-start(), calls=%async_computation.3 | async-start | bytes 7569408 | tf_op jit(solution)/shard_map/all_gather | solution.py:232
  73.6 3.5 %copy-start.4 = (f32[512,1]{1,0:T(8,128)S(1)}, f32[512,1]{1,0:T(8,128)}, u32[]{:S(2)}) copy-start(f32[512,1]{1,0:T(8,128)} %get-tuple-element.20) | copy-start | bytes 6148
  73.7 4.7 %copy-start = (bf16[64,3072]{1,0:T(8,128)(2,1)S(1)}, bf16[64,3072]{1,0:T(8,128)(2,1)}, u32[]{:S(2)}) copy-start(bf16[64,3072]{1,0:T(8,128)(2,1)} %param.22) | copy-start | bytes 1179652
  73.7 4.7 %copy-start.1 = (bf16[3072,64]{0,1:T(8,128)(2,1)S(1)}, bf16[3072,64]{0,1:T(8,128)(2,1)}, u32[]{:S(2)}) copy-start(bf16[3072,64]{0,1:T(8,128)(2,1)} %param.21) | copy-start | bytes 1179652
  73.7 4.7 %copy-start.2 = (bf16[3072,64]{0,1:T(8,128)(2,1)S(1)}, bf16[3072,64]{0,1:T(8,128)(2,1)}, u32[]{:S(2)}) copy-start(bf16[3072,64]{0,1:T(8,128)(2,1)} %param.20) | copy-start | bytes 1179652
  79.7 29.7 %collective-permute-start = (bf16[3072,192]{0,1:T(8,128)(2,1)}, bf16[3072,192]{0,1:T(8,128)(2,1)S(1)}, u32[]{:S(2)}, u32[]{:S(2)}) collective-permute-start(bf16[3072,192]{0,1:T(8,128)(2,1)} %get-tuple-element.52), channel_id=1, source_target_pairs={{0,1},{1,2},{2,3},{3,0},{4,5},{5,6},{6,7},{7,4},{8,9},{9,10},{10,1... | collective-permute-start | bytes 3538952 | tf_op jit(solution)/shard_map/ppermute | solution.py:198
  81.3 54.5 %collective-permute-start.1 = (bf16[3072,192]{0,1:T(8,128)(2,1)}, bf16[3072,192]{0,1:T(8,128)(2,1)S(1)}, u32[]{:S(2)}, u32[]{:S(2)}) collective-permute-start(bf16[3072,192]{0,1:T(8,128)(2,1)} %get-tuple-element.52), channel_id=1, source_target_pairs={{0,2},{1,3},{2,0},{3,1},{4,6},{5,7},{6,4},{7,5},{8,10},{9,11},{10,... | collective-permute-start | bytes 3538952 | tf_op jit(solution)/shard_map/ppermute | solution.py:198
  84.2 51.6 %collective-permute-start.2 = (bf16[3072,192]{0,1:T(8,128)(2,1)}, bf16[3072,192]{0,1:T(8,128)(2,1)}, u32[]{:S(2)}, u32[]{:S(2)}) collective-permute-start(bf16[3072,192]{0,1:T(8,128)(2,1)} %get-tuple-element.52), channel_id=1, source_target_pairs={{0,3},{1,0},{2,1},{3,2},{4,7},{5,4},{6,5},{7,6},{8,11},{9,8},{10,9... | collective-permute-start | bytes 3538952 | tf_op jit(solution)/shard_map/ppermute | solution.py:198
  95.0 40.8 %copy-start.14 = (pred[2,2]{1,0:T(4,128)(4,1)}, pred[2,2]{1,0:T(4,128)(4,1)S(1)}, u32[]{:S(2)}) copy-start(pred[2,2]{1,0:T(4,128)(4,1)S(1)} %iota_compare_fusion.2) | copy-start | bytes 16
  139.4 1.9 copy-start.15
  139.4 2.5 copy-start.8
  165.8 3.3 %copy-start.9 = (bf16[32,768]{1,0:T(8,128)(2,1)S(1)}, bf16[32,768]{1,0:T(8,128)(2,1)}, u32[]{:S(2)}) copy-start(bf16[32,768]{1,0:T(8,128)(2,1)} %param.17) | copy-start | bytes 147460
  165.8 13.0 %copy-start.13 = (f32[3072]{0:T(1024)S(1)}, f32[3072]{0:T(1024)}, u32[]{:S(2)}) copy-start(f32[3072]{0:T(1024)} %param.19) | copy-start | bytes 36868
  169.2 6.2 %collective-permute-start.3 = (f32[8,3072]{1,0:T(8,128)S(1)}, f32[8,3072]{1,0:T(8,128)S(1)}, u32[]{:S(2)}, u32[]{:S(2)}) collective-permute-start(f32[8,3072]{1,0:T(8,128)S(1)} %get-tuple-element.61), channel_id=1, source_target_pairs={{0,1},{1,2},{2,3},{3,0},{4,5},{5,6},{6,7},{7,4},{8,9},{9,10},{10,1... | collective-permute-start | bytes 294920 | tf_op jit(solution)/shard_map/ppermute | solution.py:293
  170.9 7.8 %collective-permute-start.4 = (f32[8,3072]{1,0:T(8,128)S(1)}, f32[8,3072]{1,0:T(8,128)S(1)}, u32[]{:S(2)}, u32[]{:S(2)}) collective-permute-start(f32[8,3072]{1,0:T(8,128)S(1)} %get-tuple-element.63), channel_id=1, source_target_pairs={{0,2},{1,3},{2,0},{3,1},{4,6},{5,7},{6,4},{7,5},{8,10},{9,11},{10,... | collective-permute-start | bytes 294920 | tf_op jit(solution)/shard_map/ppermute | solution.py:293
  173.7 5.0 %collective-permute-start.5 = (f32[8,3072]{1,0:T(8,128)S(1)}, f32[8,3072]{1,0:T(8,128)S(1)}, u32[]{:S(2)}, u32[]{:S(2)}) collective-permute-start(f32[8,3072]{1,0:T(8,128)S(1)} %get-tuple-element.62), channel_id=1, source_target_pairs={{0,3},{1,0},{2,1},{3,2},{4,7},{5,4},{6,5},{7,6},{8,11},{9,8},{10,9... | collective-permute-start | bytes 294920 | tf_op jit(solution)/shard_map/ppermute | solution.py:293
  180.3 41.1 %all-to-all-start = ((bf16[32,8,3072]{2,1,0:T(8,128)(2,1)}), bf16[32,8,3072]{2,1,0:T(8,128)(2,1)S(1)}, u32[]{:S(2)}, u32[]{:S(2)}) async-start(bf16[32,8,3072]{2,1,0:T(8,128)(2,1)} %broadcast_in_dim.38), calls=%async_computation | async-start | bytes 3145728 | tf_op jit(solution)/shard_map/all_to_all | solution.py:300
  227.2 27.1 %all-to-all-start.1 = ((bf16[32,8,3072]{2,1,0:T(8,128)(2,1)}), bf16[32,8,3072]{2,1,0:T(8,128)(2,1)S(1)}, u32[]{:S(2)}, u32[]{:S(2)}) async-start(bf16[32,8,3072]{2,1,0:T(8,128)(2,1)} %fusion.1), calls=%async_computation.1 | async-start | bytes 3145728 | tf_op jit(solution)/shard_map/all_to_all | solution.py:316
  231.2 23.3 %copy-start.11 = (f32[3072]{0:T(1024)S(1)}, f32[3072]{0:T(1024)}, u32[]{:S(2)}) copy-start(f32[3072]{0:T(1024)} %param.24) | copy-start | bytes 36868
  231.2 23.3 %copy-start.12 = (f32[3072]{0:T(1024)S(1)}, f32[3072]{0:T(1024)}, u32[]{:S(2)}) copy-start(f32[3072]{0:T(1024)} %param.23) | copy-start | bytes 36868
  254.8 5.4 %collective-permute-start.6 = (f32[8,769]{1,0:T(8,128)S(1)}, f32[8,769]{1,0:T(8,128)S(1)}, u32[]{:S(2)}, u32[]{:S(2)}) collective-permute-start(f32[8,769]{1,0:T(8,128)S(1)} %get-tuple-element.72), channel_id=1, source_target_pairs={{0,1},{1,2},{2,3},{3,0},{4,5},{5,6},{6,7},{7,4},{8,9},{9,10},{10,1... | collective-permute-start | bytes 73832 | tf_op jit(solution)/shard_map/ppermute | solution.py:345
  255.9 5.4 %collective-permute-start.7 = (f32[8,769]{1,0:T(8,128)S(1)}, f32[8,769]{1,0:T(8,128)S(1)}, u32[]{:S(2)}, u32[]{:S(2)}) collective-permute-start(f32[8,769]{1,0:T(8,128)S(1)} %get-tuple-element.73), channel_id=1, source_target_pairs={{0,2},{1,3},{2,0},{3,1},{4,6},{5,7},{6,4},{7,5},{8,10},{9,11},{10,... | collective-permute-start | bytes 73832 | tf_op jit(solution)/shard_map/ppermute | solution.py:345
  258.9 3.9 %collective-permute-start.8 = (f32[8,769]{1,0:T(8,128)S(1)}, f32[8,769]{1,0:T(8,128)S(1)}, u32[]{:S(2)}, u32[]{:S(2)}) collective-permute-start(f32[8,769]{1,0:T(8,128)S(1)} %get-tuple-element.71), channel_id=1, source_target_pairs={{0,3},{1,0},{2,1},{3,2},{4,7},{5,4},{6,5},{7,6},{8,11},{9,8},{10,9... | collective-permute-start | bytes 73832 | tf_op jit(solution)/shard_map/ppermute | solution.py:345
  (5 other events, 6.5 us)
Sparse Core Ops, SparseCore 0:
  19.4 45.6 all-gather.3
  78.4 85.3 all-gather.5

commit v8 on v7

--- a/solution.py
+++ b/solution.py
@@ -181,15 +181,6 @@
     query = rotary(block[:, :, 0].astype(jnp.float32), position).astype(jnp.bfloat16)
     key_new = rotary(block[:, :, 1].astype(jnp.float32), position).astype(jnp.bfloat16)
     value_new = block[:, :, 2]
-    gathered = lax.all_gather(query.reshape(rows_here, width_here), "req", axis=0, tiled=True)
-    eye = jnp.eye(heads_here, dtype=jnp.bfloat16)
-    tail_diag = jnp.einsum("cthd,hg->chtgd", query, eye).reshape(
-        conts_here, heads_here * 2, width_here
-    )
-    tail_acc, tail_top, tail_sum = tail_attention(tail_diag, tail_cache, tail_here, score_scale)
-    gathered, tail_acc, tail_top, tail_sum = lax.optimization_barrier(
-        (gathered, tail_acc, tail_top, tail_sum)
-    )
     mlp_count = lax.axis_size("mlp")
     weights_cat = jnp.concatenate([w_gate, w_up, jnp.transpose(w_down)], axis=1)
     weights_all = jnp.stack(
@@ -200,6 +191,15 @@
             )
             for shift in range(1, mlp_count)
         ]
+    )
+    gathered = lax.all_gather(query.reshape(rows_here, width_here), "req", axis=0, tiled=True)
+    eye = jnp.eye(heads_here, dtype=jnp.bfloat16)
+    tail_diag = jnp.einsum("cthd,hg->chtgd", query, eye).reshape(
+        conts_here, heads_here * 2, width_here
+    )
+    tail_acc, tail_top, tail_sum = tail_attention(tail_diag, tail_cache, tail_here, score_scale)
+    gathered, tail_acc, tail_top, tail_sum, weights_all = lax.optimization_barrier(
+        (gathered, tail_acc, tail_top, tail_sum, weights_all)
     )
     slot_ids = jnp.arange(req_count, dtype=jnp.int32)
     slot_of = jnp.sum(
@@ -279,7 +279,6 @@
         + numer_tail * scale_tail[..., None]
     )
     attn = (row_numer / row_total[:, :, None]).astype(jnp.bfloat16).reshape(rows_here, width_here)
-    attn, weights_all = lax.optimization_barrier((attn, weights_all))
     partial = jnp.dot(attn, w_out, preferred_element_type=jnp.float32)
     col_start = mlp_index * width_here
     own_cols = lax.dynamic_slice_in_dim(partial, col_start, width_here, 1)

time: 272 us -> 272 us (level)
  Pallas kernels: 34.2 us -> 69.8 us
  waiting for transfers between devices: 124 us -> 110 us
  starting transfers between devices: 38.1 us -> 26.9 us
  local copies, waits for them, and re-layouts: 26.9 us -> 22.5 us
  other arithmetic: 14.5 us -> 10.7 us
    pallas_call x1, Pallas kernels: 3.41 us -> 39 us  [prompt_attention(): pl.pallas_call(functools.partial(prompt_kernel, block_len, score_scale),...]
    ppermute x3, waiting for transfers between devices: 40.1 us -> 17.4 us  [per_device(): lax.ppermute(weights_cat, 'mlp', [(m, (m + shift) % mlp_count) for m in r...]
    all_gather x1, waiting for transfers between devices: 21.1 us -> 43.6 us  [per_device(): packed_all = lax.all_gather(packed[None], 'req', axis=0, tiled=True)]
    all_to_all x1, starting transfers between devices: 17.9 us -> 5.1 us  [per_device(): lax.all_to_all(jnp.broadcast_to(normed_share[None], (req_count,) + normed...]
    all_gather x1, waiting for transfers between devices: 12.7 us -> 0.01 us  [per_device(): lax.all_gather(query.reshape(rows_here, width_here), 'req', axis=0, tiled...]
  transfers between devices with their start and end apart: 13 -> 13, of which waited for: 11 -> 9; matrix products, arithmetic and copies ran while one was open for 7% -> 5% of each run, Pallas kernels for 11% -> 11%
where the time goes in v8:
time: 272 us; the launch traced here: 271 us
  waiting for transfers between devices  110 us (40%)
  Pallas kernels  69.8 us (26%)
  starting transfers between devices  26.9 us (10%)
  local copies, waits for them, and re-layouts  22.5 us (8%)
  between operations  21.8 us (8%)
  other arithmetic  10.7 us (4%)
  matrix products  9.71 us (4%)
    all_gather x1, waiting for transfers between devices, per_device(): packed_all = lax.all_gather(packed[None], 'req', axis=0, tiled=True)  43.6 us
    pallas_call x1, Pallas kernels, prompt_attention(): pl.pallas_call(functools.partial(prompt_kernel, block_len, score_scale),...  39 us
    pallas_call x1, Pallas kernels, tail_attention(): pl.pallas_call(functools.partial(tail_kernel, score_scale), grid_spec=spe...  30.8 us
    all_to_all x1, waiting for transfers between devices, per_device(): lax.all_to_all(down_sum.astype(jnp.bfloat16).reshape(req_count, share, wi...  23.1 us
    all_to_all x1, waiting for transfers between devices, per_device(): lax.all_to_all(jnp.broadcast_to(normed_share[None], (req_count,) + normed...  19.8 us
    ppermute x3, waiting for transfers between devices, per_device(): lax.ppermute(weights_cat, 'mlp', [(m, (m + shift) % mlp_count) for m in r...  17.4 us
    ppermute x3, starting transfers between devices, per_device(): lax.ppermute(weights_cat, 'mlp', [(m, (m + shift) % mlp_count) for m in r...  6.59 us
    ppermute x3, starting transfers between devices, per_device(): lax.ppermute(lax.dynamic_slice_in_dim(partial, target * share, share, 0),...  5.85 us
  transfers between devices with their start and end apart: 13, of which 9 were waited for; matrix products, arithmetic and copies ran while one was open for 5% of the time, Pallas kernels for 11%

profile of v8, /device:TPU:0, one launch (start us, length us, event | category | flops | bytes accessed | tf_op | source)
XLA Modules:
  0.0 271.1 jit_solution(7574652854612457674)
XLA Ops:
  12.6 1.9 broadcast_add_fusion
  18.7 2.0 collective-permute-start
  20.7 3.6 %collective-permute-start.1 = (bf16[3072,192]{0,1:T(8,128)(2,1)}, bf16[3072,192]{0,1:T(8,128)(2,1)}, u32[]{:S(2)}, u32[]{:S(2)}) collective-permute-start(bf16[3072,192]{0,1:T(8,128)(2,1)} %get-tuple-element.50), channel_id=1, source_target_pairs={{0,2},{1,3},{2,0},{3,1},{4,6},{5,7},{6,4},{7,5},{8,10},{9,11},{10,... | collective-permute-start | bytes 3538952 | tf_op jit(solution)/shard_map/ppermute | solution.py:189
  27.4 30.8 %shard_map.149 = (f32[16,16,768]{2,1,0:T(8,128)}, f32[16,16,1]{2,1,0:T(8,128)}, f32[16,16,1]{2,1,0:T(8,128)}) custom-call(s32[16]{0:T(128)} %get-tuple-element.36.lens_ref, bf16[16,16,768]{2,1,0:T(8,128)(2,1)} %reshape.159.q_ref, bf16[16,256,2,768]{3,2,1,0:T(2,128)(2,1)} %cache_ref.2), custom_call_target="tpu_custom_call" | custom-call | flops 201326592 | bytes 13762560 | tf_op jit(solution)/shard_map/pallas_call | solution.py:135
  58.2 17.4 %collective-permute-done.1 = bf16[3072,192]{0,1:T(8,128)(2,1)} collective-permute-done((bf16[3072,192]{0,1:T(8,128)(2,1)}, bf16[3072,192]{0,1:T(8,128)(2,1)}, u32[]{:S(2)}, u32[]{:S(2)}) %collective-permute-start.1) | collective-permute-done | bytes 1179680 | tf_op jit(solution)/shard_map/ppermute | solution.py:189
  75.6 3.7 %pad_maximum_fusion = bf16[4,3072,192]{1,2,0:T(8,128)(2,1)} fusion(bf16[1,3072,192]{1,2,0:T(8,128)(2,1)} %bitcast.12, bf16[1,3072,192]{1,2,0:T(8,128)(2,1)} %bitcast.11, bf16[1,3072,192]{1,2,0:T(8,128)(2,1)S(1)} %bitcast.157, bf16[1,3072,192]{1,2,0:T(8,128)(2,1)S(1)} %get-tuple-element.49), kind=kLoop, calls=%fused_computation | loop fusion | flops 7077888 | bytes 9437184 | tf_op jit(solution)/shard_map/stack | solution.py:186
  80.6 1.8 reshape.162.q_ref
  82.3 39.0 %shard_map.150 = (f32[512,768]{1,0:T(8,128)}, f32[512,1]{1,0:T(8,128)}, f32[512,1]{1,0:T(8,128)}) custom-call(s32[1]{0:T(128)} %bitcast.2.valid_ref, bf16[512,768]{1,0:T(8,128)(2,1)} %reshape.162.q_ref, bf16[1,4096,2,768]{3,2,1,0:T(2,128)(2,1)} %cache_ref.3), custom_call_target="tpu_custom_call" | custom-call | flops 6442450944 | bytes 14942208 | tf_op jit(solution)/shard_map/pallas_call | solution.py:86
  121.3 2.4 reshape.163
  133.9 43.6 %all-gather.6.cloned.1.call-done = f32[2048,784]{1,0:T(8,128)} async-done(((f32[64,784]{1,0:T(8,128)}), f32[2048,784]{1,0:T(8,128)}) %all-gather.6.cloned.1.call-update) | async-done | bytes 6422544 | tf_op jit(solution)/shard_map/all_gather | solution.py:232
  179.4 3.2 %fusion.16 = f32[32,3072]{1,0:T(8,128)S(1)} fusion(bf16[768,3072]{1,0:T(8,128)(2,1)} %param.18, f32[32,768]{1,0:T(8,128)S(1)} %div.48, f32[32,768]{1,0:T(8,128)S(1)} %reshape.170, f32[32,768]{1,0:T(8,128)S(1)} %mul.263, f32[32,768]{1,0:T(8,128)S(1)} %mul.258, f32[32,784]{1,0:T(8,128)S(1)} %get-tuple-element.38, f32[32,768]{1,0:T(8,128)S(1)} %mul.255, ...), kind=kOutput, calls=%fused_computation.53 | convolution fusion | flops 151166976 | bytes 5799936 | tf_op jit(solution)/shard_map/dot_general | solution.py:282
  182.7 1.6 collective-permute-start.3
  184.3 2.9 %collective-permute-start.4 = (f32[8,3072]{1,0:T(8,128)S(1)}, f32[8,3072]{1,0:T(8,128)S(1)}, u32[]{:S(2)}, u32[]{:S(2)}) collective-permute-start(f32[8,3072]{1,0:T(8,128)S(1)} %get-tuple-element.61), channel_id=1, source_target_pairs={{0,2},{1,3},{2,0},{3,1},{4,6},{5,7},{6,4},{7,5},{8,10},{9,11},{10,... | collective-permute-start | bytes 294920 | tf_op jit(solution)/shard_map/ppermute | solution.py:292
  187.1 1.4 collective-permute-start.5
  188.9 3.3 %collective-permute-done.4 = f32[8,3072]{1,0:T(8,128)S(1)} collective-permute-done((f32[8,3072]{1,0:T(8,128)S(1)}, f32[8,3072]{1,0:T(8,128)S(1)}, u32[]{:S(2)}, u32[]{:S(2)}) %collective-permute-start.4) | collective-permute-done | bytes 98336 | tf_op jit(solution)/shard_map/ppermute | solution.py:292
  193.7 5.1 %all-to-all-start = ((bf16[32,8,3072]{2,1,0:T(8,128)(2,1)}), bf16[32,8,3072]{2,1,0:T(8,128)(2,1)S(1)}, u32[]{:S(2)}, u32[]{:S(2)}) async-start(bf16[32,8,3072]{2,1,0:T(8,128)(2,1)} %broadcast_in_dim.38), calls=%async_computation | async-start | bytes 3145728 | tf_op jit(solution)/shard_map/all_to_all | solution.py:299
  198.8 3.3 %fusion.39 = (bf16[4,3072,64]{1,2,0:T(8,128)(2,1)}, bf16[4,3072,64]{1,2,0:T(8,128)(2,1)S(1)}) fusion(bf16[4,3072,192]{1,2,0:T(8,128)(2,1)} %pad_maximum_fusion), kind=kLoop, calls=%fused_computation.121 | loop fusion | bytes 6291456 | tf_op jit(solution)/shard_map/slice | solution.py:307
  202.2 19.8 %all-to-all-done = bf16[32,8,3072]{2,1,0:T(8,128)(2,1)S(1)} async-done(((bf16[32,8,3072]{2,1,0:T(8,128)(2,1)}), bf16[32,8,3072]{2,1,0:T(8,128)(2,1)S(1)}, u32[]{:S(2)}, u32[]{:S(2)}) %all-to-all-start) | async-done | bytes 1572896 | tf_op jit(solution)/shard_map/all_to_all | solution.py:299
  222.0 2.0 fusion.4
  224.6 3.2 %fusion.1 = bf16[32,8,3072]{2,1,0:T(8,128)(2,1)} fusion(bf16[4,3072,192]{1,2,0:T(8,128)(2,1)} %pad_maximum_fusion, f32[256,4,64]{0,2,1:T(8,128)S(1)} %bitcast.163, f32[256,4,64]{0,2,1:T(8,128)S(1)} %bitcast.162), kind=kOutput, calls=%fused_computation.3 | convolution fusion | flops 403832832 | bytes 3670016 | tf_op jit(solution)/shard_map/rmj,mfj->rf/dot_general | solution.py:313
  227.8 4.0 %all-to-all-start.1 = ((bf16[32,8,3072]{2,1,0:T(8,128)(2,1)}), bf16[32,8,3072]{2,1,0:T(8,128)(2,1)S(1)}, u32[]{:S(2)}, u32[]{:S(2)}) async-start(bf16[32,8,3072]{2,1,0:T(8,128)(2,1)} %fusion.1), calls=%async_computation.1 | async-start | bytes 3145728 | tf_op jit(solution)/shard_map/all_to_all | solution.py:315
  231.9 23.1 %all-to-all-done.1 = bf16[32,8,3072]{2,1,0:T(8,128)(2,1)S(1)} async-done(((bf16[32,8,3072]{2,1,0:T(8,128)(2,1)}), bf16[32,8,3072]{2,1,0:T(8,128)(2,1)S(1)}, u32[]{:S(2)}, u32[]{:S(2)}) %all-to-all-start.1) | async-done | bytes 1572896 | tf_op jit(solution)/shard_map/all_to_all | solution.py:315
  256.7 2.4 collective-permute-start.7
  259.1 1.6 collective-permute-start.8
  (129 shorter events, 26.3 us)
Async XLA Ops:
  7.2 10.3 %copy-start.1 = (bf16[64,3072]{1,0:T(8,128)(2,1)S(1)}, bf16[64,3072]{1,0:T(8,128)(2,1)}, u32[]{:S(2)}) copy-start(bf16[64,3072]{1,0:T(8,128)(2,1)} %param.22) | copy-start | bytes 1179652
  7.2 10.3 %copy-start.3 = (bf16[3072,64]{0,1:T(8,128)(2,1)S(1)}, bf16[3072,64]{0,1:T(8,128)(2,1)}, u32[]{:S(2)}) copy-start(bf16[3072,64]{0,1:T(8,128)(2,1)} %param.20) | copy-start | bytes 1179652
  7.2 10.3 %copy-start.2 = (bf16[3072,64]{0,1:T(8,128)(2,1)S(1)}, bf16[3072,64]{0,1:T(8,128)(2,1)}, u32[]{:S(2)}) copy-start(bf16[3072,64]{0,1:T(8,128)(2,1)} %param.21) | copy-start | bytes 1179652
  7.2 72.1 %all-gather.4.cloned.1.call-start = ((), (), s32[]{:S(2)}) async-start(), calls=%async_computation.2 | async-start | bytes 1622016 | tf_op jit(solution)/shard_map/all_gather | solution.py:195
  17.4 160.1 %all-gather.6.cloned.1.call-start = ((), (), s32[]{:S(2)}) async-start(), calls=%async_computation.3 | async-start | bytes 7569408 | tf_op jit(solution)/shard_map/all_gather | solution.py:232
  18.7 39.5 %collective-permute-start = (bf16[3072,192]{0,1:T(8,128)(2,1)}, bf16[3072,192]{0,1:T(8,128)(2,1)S(1)}, u32[]{:S(2)}, u32[]{:S(2)}) collective-permute-start(bf16[3072,192]{0,1:T(8,128)(2,1)} %get-tuple-element.50), channel_id=1, source_target_pairs={{0,1},{1,2},{2,3},{3,0},{4,5},{5,6},{6,7},{7,4},{8,9},{9,10},{10,1... | collective-permute-start | bytes 3538952 | tf_op jit(solution)/shard_map/ppermute | solution.py:189
  20.7 54.9 %collective-permute-start.1 = (bf16[3072,192]{0,1:T(8,128)(2,1)}, bf16[3072,192]{0,1:T(8,128)(2,1)}, u32[]{:S(2)}, u32[]{:S(2)}) collective-permute-start(bf16[3072,192]{0,1:T(8,128)(2,1)} %get-tuple-element.50), channel_id=1, source_target_pairs={{0,2},{1,3},{2,0},{3,1},{4,6},{5,7},{6,4},{7,5},{8,10},{9,11},{10,... | collective-permute-start | bytes 3538952 | tf_op jit(solution)/shard_map/ppermute | solution.py:189
  24.3 51.3 %collective-permute-start.2 = (bf16[3072,192]{0,1:T(8,128)(2,1)}, bf16[3072,192]{0,1:T(8,128)(2,1)}, u32[]{:S(2)}, u32[]{:S(2)}) collective-permute-start(bf16[3072,192]{0,1:T(8,128)(2,1)} %get-tuple-element.50), channel_id=1, source_target_pairs={{0,3},{1,0},{2,1},{3,2},{4,7},{5,4},{6,5},{7,6},{8,11},{9,8},{10,9... | collective-permute-start | bytes 3538952 | tf_op jit(solution)/shard_map/ppermute | solution.py:189
  123.7 2.4 copy-start.12
  124.4 7.3 %copy-start = (f32[16,16,768]{2,1,0:T(8,128)S(1)}, f32[16,16,768]{2,1,0:T(8,128)}, u32[]{:S(2)}) copy-start(f32[16,16,768]{2,1,0:T(8,128)} %get-tuple-element.21) | copy-start | bytes 2359300
  129.5 2.7 %copy-start.7 = (f32[16,16,1]{2,1,0:T(8,128)S(1)}, f32[16,16,1]{2,1,0:T(8,128)}, u32[]{:S(2)}) copy-start(f32[16,16,1]{2,1,0:T(8,128)} %get-tuple-element.20) | copy-start | bytes 3076
  132.2 1.3 copy-start.6
  179.3 3.3 %copy-start.8 = (bf16[32,768]{1,0:T(8,128)(2,1)S(1)}, bf16[32,768]{1,0:T(8,128)(2,1)}, u32[]{:S(2)}) copy-start(bf16[32,768]{1,0:T(8,128)(2,1)} %param.17) | copy-start | bytes 147460
  179.3 13.0 %copy-start.11 = (f32[3072]{0:T(1024)S(1)}, f32[3072]{0:T(1024)}, u32[]{:S(2)}) copy-start(f32[3072]{0:T(1024)} %param.19) | copy-start | bytes 36868
  182.7 6.2 %collective-permute-start.3 = (f32[8,3072]{1,0:T(8,128)S(1)}, f32[8,3072]{1,0:T(8,128)S(1)}, u32[]{:S(2)}, u32[]{:S(2)}) collective-permute-start(f32[8,3072]{1,0:T(8,128)S(1)} %get-tuple-element.59), channel_id=1, source_target_pairs={{0,1},{1,2},{2,3},{3,0},{4,5},{5,6},{6,7},{7,4},{8,9},{9,10},{10,1... | collective-permute-start | bytes 294920 | tf_op jit(solution)/shard_map/ppermute | solution.py:292
  184.3 7.9 %collective-permute-start.4 = (f32[8,3072]{1,0:T(8,128)S(1)}, f32[8,3072]{1,0:T(8,128)S(1)}, u32[]{:S(2)}, u32[]{:S(2)}) collective-permute-start(f32[8,3072]{1,0:T(8,128)S(1)} %get-tuple-element.61), channel_id=1, source_target_pairs={{0,2},{1,3},{2,0},{3,1},{4,6},{5,7},{6,4},{7,5},{8,10},{9,11},{10,... | collective-permute-start | bytes 294920 | tf_op jit(solution)/shard_map/ppermute | solution.py:292
  187.1 5.0 %collective-permute-start.5 = (f32[8,3072]{1,0:T(8,128)S(1)}, f32[8,3072]{1,0:T(8,128)S(1)}, u32[]{:S(2)}, u32[]{:S(2)}) collective-permute-start(f32[8,3072]{1,0:T(8,128)S(1)} %get-tuple-element.60), channel_id=1, source_target_pairs={{0,3},{1,0},{2,1},{3,2},{4,7},{5,4},{6,5},{7,6},{8,11},{9,8},{10,9... | collective-permute-start | bytes 294920 | tf_op jit(solution)/shard_map/ppermute | solution.py:292
  193.7 28.2 %all-to-all-start = ((bf16[32,8,3072]{2,1,0:T(8,128)(2,1)}), bf16[32,8,3072]{2,1,0:T(8,128)(2,1)S(1)}, u32[]{:S(2)}, u32[]{:S(2)}) async-start(bf16[32,8,3072]{2,1,0:T(8,128)(2,1)} %broadcast_in_dim.38), calls=%async_computation | async-start | bytes 3145728 | tf_op jit(solution)/shard_map/all_to_all | solution.py:299
  227.8 27.1 %all-to-all-start.1 = ((bf16[32,8,3072]{2,1,0:T(8,128)(2,1)}), bf16[32,8,3072]{2,1,0:T(8,128)(2,1)S(1)}, u32[]{:S(2)}, u32[]{:S(2)}) async-start(bf16[32,8,3072]{2,1,0:T(8,128)(2,1)} %fusion.1), calls=%async_computation.1 | async-start | bytes 3145728 | tf_op jit(solution)/shard_map/all_to_all | solution.py:315
  231.8 23.3 %copy-start.9 = (f32[3072]{0:T(1024)S(1)}, f32[3072]{0:T(1024)}, u32[]{:S(2)}) copy-start(f32[3072]{0:T(1024)} %param.24) | copy-start | bytes 36868
  231.8 23.3 %copy-start.10 = (f32[3072]{0:T(1024)S(1)}, f32[3072]{0:T(1024)}, u32[]{:S(2)}) copy-start(f32[3072]{0:T(1024)} %param.23) | copy-start | bytes 36868
  255.4 5.5 %collective-permute-start.6 = (f32[8,769]{1,0:T(8,128)S(1)}, f32[8,769]{1,0:T(8,128)S(1)}, u32[]{:S(2)}, u32[]{:S(2)}) collective-permute-start(f32[8,769]{1,0:T(8,128)S(1)} %get-tuple-element.70), channel_id=1, source_target_pairs={{0,1},{1,2},{2,3},{3,0},{4,5},{5,6},{6,7},{7,4},{8,9},{9,10},{10,1... | collective-permute-start | bytes 73832 | tf_op jit(solution)/shard_map/ppermute | solution.py:344
  256.7 5.4 %collective-permute-start.7 = (f32[8,769]{1,0:T(8,128)S(1)}, f32[8,769]{1,0:T(8,128)S(1)}, u32[]{:S(2)}, u32[]{:S(2)}) collective-permute-start(f32[8,769]{1,0:T(8,128)S(1)} %get-tuple-element.71), channel_id=1, source_target_pairs={{0,2},{1,3},{2,0},{3,1},{4,6},{5,7},{6,4},{7,5},{8,10},{9,11},{10,... | collective-permute-start | bytes 73832 | tf_op jit(solution)/shard_map/ppermute | solution.py:344
  259.1 3.9 %collective-permute-start.8 = (f32[8,769]{1,0:T(8,128)S(1)}, f32[8,769]{1,0:T(8,128)S(1)}, u32[]{:S(2)}, u32[]{:S(2)}) collective-permute-start(f32[8,769]{1,0:T(8,128)S(1)} %get-tuple-element.69), channel_id=1, source_target_pairs={{0,3},{1,0},{2,1},{3,2},{4,7},{5,4},{6,5},{7,6},{8,11},{9,8},{10,9... | collective-permute-start | bytes 73832 | tf_op jit(solution)/shard_map/ppermute | solution.py:344
  (2 other events, 2.2 us)
Sparse Core Ops, SparseCore 0:
  17.5 45.5 all-gather.3
  126.2 51.1 all-gather.5

commit v9 on v8

--- a/solution.py
+++ b/solution.py
@@ -219,25 +219,26 @@
     prompt_acc, prompt_top, prompt_sum = prompt_attention(q_diag, prompt_cache, valid_count, score_scale)
     prompt_acc = prompt_acc.reshape(heads_here, owned_rows, heads_here, HD)
     owner_numer = jnp.stack([prompt_acc[h, :, h, :] for h in range(heads_here)], axis=1)
-    owner_total = prompt_sum.reshape(heads_here, owned_rows)
-    prefix_max = prompt_top.reshape(heads_here, owned_rows)
+    top_f = jnp.transpose(prompt_top.reshape(heads_here, owned_rows))
+    top_b = top_f.astype(jnp.bfloat16).astype(jnp.float32)
+    rebase = jnp.where(top_f > 0.5 * masked_value, jnp.exp(top_f - top_b), 0.0)
+    owner_total = jnp.transpose(prompt_sum.reshape(heads_here, owned_rows)) * rebase
+    owner_numer = owner_numer * rebase[:, :, None]
     packed = jnp.concatenate(
-        [
-            owner_numer.reshape(owned_rows, width_here),
-            jnp.transpose(owner_total),
-            jnp.transpose(prefix_max),
-        ],
-        axis=1,
-    )
-    packed_all = lax.all_gather(packed[None], "req", axis=0, tiled=True)
-    row_offset = req_index % 2 * rows_here
+        [owner_numer.reshape(owned_rows, width_here), owner_total, top_b], axis=1
+    ).astype(jnp.bfloat16)
+    outgoing = lax.dynamic_update_slice_in_dim(
+        jnp.zeros((req_count, rows_here, packed.shape[1]), jnp.bfloat16),
+        packed.reshape(2, rows_here, packed.shape[1]),
+        2 * owned_prompt,
+        0,
+    )
+    incoming = lax.all_to_all(outgoing, "req", split_axis=0, concat_axis=0, tiled=True)
     slot_first = lax.dynamic_index_in_dim(slot_of, 2 * own_prompt, 0, keepdims=False)
     slot_second = lax.dynamic_index_in_dim(slot_of, 2 * own_prompt + 1, 0, keepdims=False)
 
     def part_of(slot):
-        piece = lax.dynamic_slice_in_dim(
-            lax.dynamic_index_in_dim(packed_all, slot, 0, keepdims=False), row_offset, rows_here, 0
-        )
+        piece = lax.dynamic_index_in_dim(incoming, slot, 0, keepdims=False).astype(jnp.float32)
         numer = piece[:, :width_here].reshape(rows_here, heads_here, HD)
         total = piece[:, width_here : width_here + heads_here]
         top = piece[:, width_here + heads_here :]

time: 272 us -> 260 us (0.956)
  waiting for transfers between devices: 110 us -> 85.7 us
  starting transfers between devices: 26.9 us -> 36.4 us
  local copies, waits for them, and re-layouts: 22.5 us -> 27.5 us
  Pallas kernels: 69.8 us -> 65.5 us
    all_gather x1 -> x0, waiting for transfers between devices: 43.6 us -> none  [per_device(): packed_all = lax.all_gather(packed[None], 'req', axis=0, tiled=True)]
    all_to_all x0 -> x1, waiting for transfers between devices: none -> 24.6 us  [per_device(): lax.all_to_all(outgoing, 'req', split_axis=0, concat_axis=0, tiled=True)]
    all_to_all x0 -> x1, starting transfers between devices: none -> 12.1 us  [per_device(): lax.all_to_all(outgoing, 'req', split_axis=0, concat_axis=0, tiled=True)]
    ppermute x3, waiting for transfers between devices: 17.4 us -> 11.6 us  [per_device(): lax.ppermute(weights_cat, 'mlp', [(m, (m + shift) % mlp_count) for m in r...]
    pallas_call x1, Pallas kernels: 39 us -> 34.6 us  [prompt_attention(): pl.pallas_call(functools.partial(prompt_kernel, block_len, score_scale),...]
  transfers between devices with their start and end apart: 13 -> 13, of which waited for: 9 -> 10; matrix products, arithmetic and copies ran while one was open for 5% -> 5% of each run, Pallas kernels for 11% -> 12%
where the time goes in v9:
time: 260 us; the launch traced here: 259 us
  waiting for transfers between devices  85.7 us (33%)
  Pallas kernels  65.5 us (25%)
  starting transfers between devices  36.4 us (14%)
  local copies, waits for them, and re-layouts  27.5 us (11%)
  between operations  21.8 us (8%)
  other arithmetic  12.4 us (5%)
  matrix products  9.76 us (4%)
    pallas_call x1, Pallas kernels, prompt_attention(): pl.pallas_call(functools.partial(prompt_kernel, block_len, score_scale),...  34.6 us
    pallas_call x1, Pallas kernels, tail_attention(): pl.pallas_call(functools.partial(tail_kernel, score_scale), grid_spec=spe...  31 us
    all_to_all x1, waiting for transfers between devices, per_device(): lax.all_to_all(outgoing, 'req', split_axis=0, concat_axis=0, tiled=True)  24.6 us
    all_to_all x1, waiting for transfers between devices, per_device(): lax.all_to_all(down_sum.astype(jnp.bfloat16).reshape(req_count, share, wi...  23.1 us
    all_to_all x1, waiting for transfers between devices, per_device(): lax.all_to_all(jnp.broadcast_to(normed_share[None], (req_count,) + normed...  19.7 us
    all_to_all x1, starting transfers between devices, per_device(): lax.all_to_all(outgoing, 'req', split_axis=0, concat_axis=0, tiled=True)  12.1 us
    ppermute x3, waiting for transfers between devices, per_device(): lax.ppermute(weights_cat, 'mlp', [(m, (m + shift) % mlp_count) for m in r...  11.6 us
    ppermute x3, starting transfers between devices, per_device(): lax.ppermute(weights_cat, 'mlp', [(m, (m + shift) % mlp_count) for m in r...  6.59 us
  transfers between devices with their start and end apart: 13, of which 10 were waited for; matrix products, arithmetic and copies ran while one was open for 5% of the time, Pallas kernels for 12%

profile of v9, /device:TPU:0, one launch (start us, length us, event | category | flops | bytes accessed | tf_op | source)
XLA Modules:
  0.0 259.2 jit_solution(15569047011442414335)
XLA Ops:
  12.6 2.0 broadcast_add_fusion
  19.5 2.0 collective-permute-start
  21.5 3.6 %collective-permute-start.1 = (bf16[3072,192]{0,1:T(8,128)(2,1)}, bf16[3072,192]{0,1:T(8,128)(2,1)}, u32[]{:S(2)}, u32[]{:S(2)}) collective-permute-start(bf16[3072,192]{0,1:T(8,128)(2,1)} %get-tuple-element.53), channel_id=1, source_target_pairs={{0,2},{1,3},{2,0},{3,1},{4,6},{5,7},{6,4},{7,5},{8,10},{9,11},{10,... | collective-permute-start | bytes 3538952 | tf_op jit(solution)/shard_map/ppermute | solution.py:189
  33.7 31.0 %shard_map.149 = (f32[16,16,768]{2,1,0:T(8,128)}, f32[16,16,1]{2,1,0:T(8,128)}, f32[16,16,1]{2,1,0:T(8,128)}) custom-call(s32[16]{0:T(128)} %get-tuple-element.39.lens_ref, bf16[16,16,768]{2,1,0:T(8,128)(2,1)} %reshape.172.q_ref, bf16[16,256,2,768]{3,2,1,0:T(2,128)(2,1)} %cache_ref.2), custom_call_target="tpu_custom_call" | custom-call | flops 201326592 | bytes 13762560 | tf_op jit(solution)/shard_map/pallas_call | solution.py:135
  64.7 11.6 %collective-permute-done.1 = bf16[3072,192]{0,1:T(8,128)(2,1)} collective-permute-done((bf16[3072,192]{0,1:T(8,128)(2,1)}, bf16[3072,192]{0,1:T(8,128)(2,1)}, u32[]{:S(2)}, u32[]{:S(2)}) %collective-permute-start.1) | collective-permute-done | bytes 1179680 | tf_op jit(solution)/shard_map/ppermute | solution.py:189
  76.3 3.7 %pad_maximum_fusion = bf16[4,3072,192]{1,2,0:T(8,128)(2,1)} fusion(bf16[1,3072,192]{1,2,0:T(8,128)(2,1)} %bitcast.12, bf16[1,3072,192]{1,2,0:T(8,128)(2,1)} %bitcast.11, bf16[1,3072,192]{1,2,0:T(8,128)(2,1)S(1)} %bitcast.174, bf16[1,3072,192]{1,2,0:T(8,128)(2,1)S(1)} %get-tuple-element.52), kind=kLoop, calls=%fused_computation | loop fusion | flops 7077888 | bytes 9437184 | tf_op jit(solution)/shard_map/stack | solution.py:186
  80.0 1.6 reshape.181
  85.4 1.8 reshape.175.q_ref
  87.1 34.6 %shard_map.150 = (f32[512,768]{1,0:T(8,128)}, f32[512,1]{1,0:T(8,128)}, f32[512,1]{1,0:T(8,128)}) custom-call(s32[1]{0:T(128)} %bitcast.2.valid_ref, bf16[512,768]{1,0:T(8,128)(2,1)} %reshape.175.q_ref, bf16[1,4096,2,768]{3,2,1,0:T(2,128)(2,1)} %cache_ref.3), custom_call_target="tpu_custom_call" | custom-call | flops 6442450944 | bytes 14942208 | tf_op jit(solution)/shard_map/pallas_call | solution.py:86
  121.7 2.2 reshape.176
  130.1 12.1 %all-to-all-start = ((bf16[32,32,784]{2,1,0:T(8,128)(2,1)}), bf16[32,32,784]{2,1,0:T(8,128)(2,1)S(1)}, u32[]{:S(2)}, u32[]{:S(2)}) async-start(bf16[32,32,784]{2,1,0:T(8,128)(2,1)} %maximum_dynamic-update-slice_fusion), calls=%async_computation | async-start | bytes 3670016 | tf_op jit(solution)/shard_map/all_to_all | solution.py:236
  143.5 24.6 %all-to-all-done = bf16[32,32,784]{2,1,0:T(8,128)(2,1)S(1)} async-done(((bf16[32,32,784]{2,1,0:T(8,128)(2,1)}), bf16[32,32,784]{2,1,0:T(8,128)(2,1)S(1)}, u32[]{:S(2)}, u32[]{:S(2)}) %all-to-all-start) | async-done | bytes 1605664 | tf_op jit(solution)/shard_map/all_to_all | solution.py:236
  169.0 3.2 %fusion.16 = f32[32,3072]{1,0:T(8,128)S(1)} fusion(bf16[768,3072]{1,0:T(8,128)(2,1)} %param.18, f32[32,768]{1,0:T(8,128)S(1)} %div.48, f32[32,768]{1,0:T(8,128)S(1)} %reshape.182, f32[32,768]{1,0:T(8,128)S(1)} %mul.283, f32[32,768]{1,0:T(8,128)S(1)} %mul.278, f32[32,784]{1,0:T(8,128)S(1)} %get-tuple-element.51, f32[32,768]{1,0:T(8,128)S(1)} %mul.275, ...), kind=kOutput, calls=%fused_computation.54 | convolution fusion | flops 151166976 | bytes 5799936 | tf_op jit(solution)/shard_map/dot_general | solution.py:283
  173.5 2.4 collective-permute-start.4
  177.3 2.0 collective-permute-done.3
  182.4 4.0 %all-to-all-start.1 = ((bf16[32,8,3072]{2,1,0:T(8,128)(2,1)}), bf16[32,8,3072]{2,1,0:T(8,128)(2,1)S(1)}, u32[]{:S(2)}, u32[]{:S(2)}) async-start(bf16[32,8,3072]{2,1,0:T(8,128)(2,1)} %broadcast_in_dim.43), calls=%async_computation.1 | async-start | bytes 3145728 | tf_op jit(solution)/shard_map/all_to_all | solution.py:300
  186.4 3.4 %fusion.43 = (bf16[4,3072,64]{1,2,0:T(8,128)(2,1)}, bf16[4,3072,64]{1,2,0:T(8,128)(2,1)S(1)}) fusion(bf16[4,3072,192]{1,2,0:T(8,128)(2,1)} %pad_maximum_fusion), kind=kLoop, calls=%fused_computation.129 | loop fusion | bytes 6291456 | tf_op jit(solution)/shard_map/slice | solution.py:308
  189.8 19.7 %all-to-all-done.1 = bf16[32,8,3072]{2,1,0:T(8,128)(2,1)S(1)} async-done(((bf16[32,8,3072]{2,1,0:T(8,128)(2,1)}), bf16[32,8,3072]{2,1,0:T(8,128)(2,1)S(1)}, u32[]{:S(2)}, u32[]{:S(2)}) %all-to-all-start.1) | async-done | bytes 1572896 | tf_op jit(solution)/shard_map/all_to_all | solution.py:300
  209.5 2.0 fusion.4
  212.2 3.3 %fusion.1 = bf16[32,8,3072]{2,1,0:T(8,128)(2,1)} fusion(bf16[4,3072,192]{1,2,0:T(8,128)(2,1)} %pad_maximum_fusion, f32[256,4,64]{0,2,1:T(8,128)S(1)} %bitcast.180, f32[256,4,64]{0,2,1:T(8,128)S(1)} %bitcast.179), kind=kOutput, calls=%fused_computation.3 | convolution fusion | flops 403832832 | bytes 3670016 | tf_op jit(solution)/shard_map/rmj,mfj->rf/dot_general | solution.py:314
  215.4 4.0 %all-to-all-start.2 = ((bf16[32,8,3072]{2,1,0:T(8,128)(2,1)}), bf16[32,8,3072]{2,1,0:T(8,128)(2,1)S(1)}, u32[]{:S(2)}, u32[]{:S(2)}) async-start(bf16[32,8,3072]{2,1,0:T(8,128)(2,1)} %fusion.1), calls=%async_computation.2 | async-start | bytes 3145728 | tf_op jit(solution)/shard_map/all_to_all | solution.py:316
  219.5 23.1 %all-to-all-done.2 = bf16[32,8,3072]{2,1,0:T(8,128)(2,1)S(1)} async-done(((bf16[32,8,3072]{2,1,0:T(8,128)(2,1)}), bf16[32,8,3072]{2,1,0:T(8,128)(2,1)S(1)}, u32[]{:S(2)}, u32[]{:S(2)}) %all-to-all-start.2) | async-done | bytes 1572896 | tf_op jit(solution)/shard_map/all_to_all | solution.py:316
  244.6 2.6 collective-permute-start.7
  248.2 1.8 collective-permute-done.7
  (136 shorter events, 35.3 us)
Async XLA Ops:
  7.2 10.9 %copy-start = (bf16[64,3072]{1,0:T(8,128)(2,1)S(1)}, bf16[64,3072]{1,0:T(8,128)(2,1)}, u32[]{:S(2)}) copy-start(bf16[64,3072]{1,0:T(8,128)(2,1)} %param.22) | copy-start | bytes 1179652
  7.2 10.9 %copy-start.2 = (bf16[3072,64]{0,1:T(8,128)(2,1)S(1)}, bf16[3072,64]{0,1:T(8,128)(2,1)}, u32[]{:S(2)}) copy-start(bf16[3072,64]{0,1:T(8,128)(2,1)} %param.20) | copy-start | bytes 1179652
  7.2 10.9 %copy-start.1 = (bf16[3072,64]{0,1:T(8,128)(2,1)S(1)}, bf16[3072,64]{0,1:T(8,128)(2,1)}, u32[]{:S(2)}) copy-start(bf16[3072,64]{0,1:T(8,128)(2,1)} %param.21) | copy-start | bytes 1179652
  7.2 72.8 %all-gather.2.cloned.1.call-start = ((), (), s32[]{:S(2)}) async-start(), calls=%async_computation.3 | async-start | bytes 1622016 | tf_op jit(solution)/shard_map/all_gather | solution.py:195
  18.1 7.9 %copy-start.14 = (s32[32]{0:T(128)S(1)}, s32[32]{0:T(128)}, u32[]{:S(2)}) copy-start(s32[32]{0:T(128)} %param.25) | copy-start | bytes 388
  19.5 45.3 %collective-permute-start = (bf16[3072,192]{0,1:T(8,128)(2,1)}, bf16[3072,192]{0,1:T(8,128)(2,1)S(1)}, u32[]{:S(2)}, u32[]{:S(2)}) collective-permute-start(bf16[3072,192]{0,1:T(8,128)(2,1)} %get-tuple-element.53), channel_id=1, source_target_pairs={{0,1},{1,2},{2,3},{3,0},{4,5},{5,6},{6,7},{7,4},{8,9},{9,10},{10,1... | collective-permute-start | bytes 3538952 | tf_op jit(solution)/shard_map/ppermute | solution.py:189
  21.5 54.9 %collective-permute-start.1 = (bf16[3072,192]{0,1:T(8,128)(2,1)}, bf16[3072,192]{0,1:T(8,128)(2,1)}, u32[]{:S(2)}, u32[]{:S(2)}) collective-permute-start(bf16[3072,192]{0,1:T(8,128)(2,1)} %get-tuple-element.53), channel_id=1, source_target_pairs={{0,2},{1,3},{2,0},{3,1},{4,6},{5,7},{6,4},{7,5},{8,10},{9,11},{10,... | collective-permute-start | bytes 3538952 | tf_op jit(solution)/shard_map/ppermute | solution.py:189
  25.0 51.3 %collective-permute-start.2 = (bf16[3072,192]{0,1:T(8,128)(2,1)}, bf16[3072,192]{0,1:T(8,128)(2,1)}, u32[]{:S(2)}, u32[]{:S(2)}) collective-permute-start(bf16[3072,192]{0,1:T(8,128)(2,1)} %get-tuple-element.53), channel_id=1, source_target_pairs={{0,3},{1,0},{2,1},{3,2},{4,7},{5,4},{6,5},{7,6},{8,11},{9,8},{10,9... | collective-permute-start | bytes 3538952 | tf_op jit(solution)/shard_map/ppermute | solution.py:189
  121.7 4.2 %copy-start.3 = (f32[512,1]{1,0:T(8,128)S(1)}, f32[512,1]{1,0:T(8,128)}, u32[]{:S(2)}) copy-start(f32[512,1]{1,0:T(8,128)} %get-tuple-element.19) | copy-start | bytes 6148
  130.1 12.4 %copy-start.6 = (bf16[16,8,2,2]{3,2,1,0:T(2,128)(2,1)S(1)}, bf16[16,8,2,2]{3,2,1,0:T(2,128)(2,1)}, u32[]{:S(2)}) copy-start(bf16[16,8,2,2]{3,2,1,0:T(2,128)(2,1)} %copy.164) | copy-start | bytes 3076
  130.1 12.4 %copy-start.7 = (f32[16,2,8]{1,2,0:T(8,128)S(1)}, f32[16,2,8]{1,2,0:T(8,128)}, u32[]{:S(2)}) copy-start(f32[16,2,8]{1,2,0:T(8,128)} %copy.162) | copy-start | bytes 3076
  130.1 12.4 %copy-start.8 = (bf16[16,2,1,8,96]{4,3,1,0,2:T(8,128)(2,1)S(1)}, bf16[16,2,1,8,96]{4,3,1,0,2:T(8,128)(2,1)}, u32[]{:S(2)}) copy-start(bf16[16,2,1,8,96]{4,3,1,0,2:T(8,128)(2,1)} %get-tuple-element.65) | copy-start | bytes 147460
  130.1 37.9 %all-to-all-start = ((bf16[32,32,784]{2,1,0:T(8,128)(2,1)}), bf16[32,32,784]{2,1,0:T(8,128)(2,1)S(1)}, u32[]{:S(2)}, u32[]{:S(2)}) async-start(bf16[32,32,784]{2,1,0:T(8,128)(2,1)} %maximum_dynamic-update-slice_fusion), calls=%async_computation | async-start | bytes 3670016 | tf_op jit(solution)/shard_map/all_to_all | solution.py:236
  169.0 12.0 %copy-start.13 = (f32[3072]{0:T(1024)S(1)}, f32[3072]{0:T(1024)}, u32[]{:S(2)}) copy-start(f32[3072]{0:T(1024)} %param.19) | copy-start | bytes 36868
  172.3 7.0 %collective-permute-start.3 = (f32[8,3072]{1,0:T(8,128)S(1)}, f32[8,3072]{1,0:T(8,128)S(1)}, u32[]{:S(2)}, u32[]{:S(2)}) collective-permute-start(f32[8,3072]{1,0:T(8,128)S(1)} %get-tuple-element.62), channel_id=1, source_target_pairs={{0,1},{1,2},{2,3},{3,0},{4,5},{5,6},{6,7},{7,4},{8,9},{9,10},{10,1... | collective-permute-start | bytes 294920 | tf_op jit(solution)/shard_map/ppermute | solution.py:293
  173.5 6.9 %collective-permute-start.4 = (f32[8,3072]{1,0:T(8,128)S(1)}, f32[8,3072]{1,0:T(8,128)S(1)}, u32[]{:S(2)}, u32[]{:S(2)}) collective-permute-start(f32[8,3072]{1,0:T(8,128)S(1)} %get-tuple-element.64), channel_id=1, source_target_pairs={{0,2},{1,3},{2,0},{3,1},{4,6},{5,7},{6,4},{7,5},{8,10},{9,11},{10,... | collective-permute-start | bytes 294920 | tf_op jit(solution)/shard_map/ppermute | solution.py:293
  175.9 4.9 %collective-permute-start.5 = (f32[8,3072]{1,0:T(8,128)S(1)}, f32[8,3072]{1,0:T(8,128)S(1)}, u32[]{:S(2)}, u32[]{:S(2)}) collective-permute-start(f32[8,3072]{1,0:T(8,128)S(1)} %get-tuple-element.63), channel_id=1, source_target_pairs={{0,3},{1,0},{2,1},{3,2},{4,7},{5,4},{6,5},{7,6},{8,11},{9,8},{10,9... | collective-permute-start | bytes 294920 | tf_op jit(solution)/shard_map/ppermute | solution.py:293
  182.4 27.1 %all-to-all-start.1 = ((bf16[32,8,3072]{2,1,0:T(8,128)(2,1)}), bf16[32,8,3072]{2,1,0:T(8,128)(2,1)S(1)}, u32[]{:S(2)}, u32[]{:S(2)}) async-start(bf16[32,8,3072]{2,1,0:T(8,128)(2,1)} %broadcast_in_dim.43), calls=%async_computation.1 | async-start | bytes 3145728 | tf_op jit(solution)/shard_map/all_to_all | solution.py:300
  215.4 27.1 %all-to-all-start.2 = ((bf16[32,8,3072]{2,1,0:T(8,128)(2,1)}), bf16[32,8,3072]{2,1,0:T(8,128)(2,1)S(1)}, u32[]{:S(2)}, u32[]{:S(2)}) async-start(bf16[32,8,3072]{2,1,0:T(8,128)(2,1)} %fusion.1), calls=%async_computation.2 | async-start | bytes 3145728 | tf_op jit(solution)/shard_map/all_to_all | solution.py:316
  219.4 23.3 %copy-start.11 = (f32[3072]{0:T(1024)S(1)}, f32[3072]{0:T(1024)}, u32[]{:S(2)}) copy-start(f32[3072]{0:T(1024)} %param.24) | copy-start | bytes 36868
  219.4 23.3 %copy-start.12 = (f32[3072]{0:T(1024)S(1)}, f32[3072]{0:T(1024)}, u32[]{:S(2)}) copy-start(f32[3072]{0:T(1024)} %param.23) | copy-start | bytes 36868
  243.0 5.2 %collective-permute-start.6 = (f32[8,769]{1,0:T(8,128)S(1)}, f32[8,769]{1,0:T(8,128)S(1)}, u32[]{:S(2)}, u32[]{:S(2)}) collective-permute-start(f32[8,769]{1,0:T(8,128)S(1)} %get-tuple-element.73), channel_id=1, source_target_pairs={{0,1},{1,2},{2,3},{3,0},{4,5},{5,6},{6,7},{7,4},{8,9},{9,10},{10,1... | collective-permute-start | bytes 73832 | tf_op jit(solution)/shard_map/ppermute | solution.py:345
  244.6 5.4 %collective-permute-start.7 = (f32[8,769]{1,0:T(8,128)S(1)}, f32[8,769]{1,0:T(8,128)S(1)}, u32[]{:S(2)}, u32[]{:S(2)}) collective-permute-start(f32[8,769]{1,0:T(8,128)S(1)} %get-tuple-element.74), channel_id=1, source_target_pairs={{0,2},{1,3},{2,0},{3,1},{4,6},{5,7},{6,4},{7,5},{8,10},{9,11},{10,... | collective-permute-start | bytes 73832 | tf_op jit(solution)/shard_map/ppermute | solution.py:345
  247.2 3.9 %collective-permute-start.8 = (f32[8,769]{1,0:T(8,128)S(1)}, f32[8,769]{1,0:T(8,128)S(1)}, u32[]{:S(2)}, u32[]{:S(2)}) collective-permute-start(f32[8,769]{1,0:T(8,128)S(1)} %get-tuple-element.72), channel_id=1, source_target_pairs={{0,3},{1,0},{2,1},{3,2},{4,7},{5,4},{6,5},{7,6},{8,11},{9,8},{10,9... | collective-permute-start | bytes 73832 | tf_op jit(solution)/shard_map/ppermute | solution.py:345
  (4 other events, 6.9 us)
Sparse Core Ops, SparseCore 0:
  18.2 45.5 all-gather.1

commit v10 on v9

--- a/solution.py
+++ b/solution.py
@@ -62,7 +62,7 @@
 
 def prompt_attention(q_diag, cache, valid_count, score_scale):
     span = cache.shape[1]
-    block_len = min(512, span)
+    block_len = min(1024, span)
     lanes = cache.shape[3]
     rows = q_diag.shape[0]
 

time: 260 us -> 258 us (level)
  Pallas kernels: 65.5 us -> 34.5 us
  starting transfers between devices: 36.4 us -> 65 us
    pallas_call x1, Pallas kernels: 34.6 us -> 3.7 us  [prompt_attention(): pl.pallas_call(functools.partial(prompt_kernel, block_len, score_scale),...]
    all_to_all x1, starting transfers between devices: 12.1 us -> 40.7 us  [per_device(): lax.all_to_all(outgoing, 'req', split_axis=0, concat_axis=0, tiled=True)]
where the time goes in v10:
time: 258 us; the launch traced here: 257 us
  waiting for transfers between devices  85.9 us (33%)
  starting transfers between devices  65 us (25%)
  Pallas kernels  34.5 us (13%)
  local copies, waits for them, and re-layouts  27.5 us (11%)
  between operations  21.8 us (8%)
  other arithmetic  12.4 us (5%)
  matrix products  9.74 us (4%)
    all_to_all x1, starting transfers between devices, per_device(): lax.all_to_all(outgoing, 'req', split_axis=0, concat_axis=0, tiled=True)  40.7 us
    pallas_call x1, Pallas kernels, tail_attention(): pl.pallas_call(functools.partial(tail_kernel, score_scale), grid_spec=spe...  30.8 us
    all_to_all x1, waiting for transfers between devices, per_device(): lax.all_to_all(outgoing, 'req', split_axis=0, concat_axis=0, tiled=True)  24.6 us
    all_to_all x1, waiting for transfers between devices, per_device(): lax.all_to_all(down_sum.astype(jnp.bfloat16).reshape(req_count, share, wi...  23.1 us
    all_to_all x1, waiting for transfers between devices, per_device(): lax.all_to_all(jnp.broadcast_to(normed_share[None], (req_count,) + normed...  19.7 us
    ppermute x3, waiting for transfers between devices, per_device(): lax.ppermute(weights_cat, 'mlp', [(m, (m + shift) % mlp_count) for m in r...  11.8 us
    ppermute x3, starting transfers between devices, per_device(): lax.ppermute(weights_cat, 'mlp', [(m, (m + shift) % mlp_count) for m in r...  6.59 us
  transfers between devices with their start and end apart: 13, of which 10 were waited for; matrix products, arithmetic and copies ran while one was open for 5% of the time, Pallas kernels for 12%

profile of v10, /device:TPU:0, one launch (start us, length us, event | category | flops | bytes accessed | tf_op | source)
XLA Modules:
  0.0 256.9 jit_solution(12014500836119707468)
XLA Ops:
  12.6 2.0 broadcast_add_fusion
  19.5 2.0 collective-permute-start
  21.5 3.6 %collective-permute-start.1 = (bf16[3072,192]{0,1:T(8,128)(2,1)}, bf16[3072,192]{0,1:T(8,128)(2,1)}, u32[]{:S(2)}, u32[]{:S(2)}) collective-permute-start(bf16[3072,192]{0,1:T(8,128)(2,1)} %get-tuple-element.53), channel_id=1, source_target_pairs={{0,2},{1,3},{2,0},{3,1},{4,6},{5,7},{6,4},{7,5},{8,10},{9,11},{10,... | collective-permute-start | bytes 3538952 | tf_op jit(solution)/shard_map/ppermute | solution.py:189
  33.7 30.8 %shard_map.149 = (f32[16,16,768]{2,1,0:T(8,128)}, f32[16,16,1]{2,1,0:T(8,128)}, f32[16,16,1]{2,1,0:T(8,128)}) custom-call(s32[16]{0:T(128)} %get-tuple-element.39.lens_ref, bf16[16,16,768]{2,1,0:T(8,128)(2,1)} %reshape.172.q_ref, bf16[16,256,2,768]{3,2,1,0:T(2,128)(2,1)} %cache_ref.2), custom_call_target="tpu_custom_call" | custom-call | flops 201326592 | bytes 13762560 | tf_op jit(solution)/shard_map/pallas_call | solution.py:135
  64.5 11.8 %collective-permute-done.1 = bf16[3072,192]{0,1:T(8,128)(2,1)} collective-permute-done((bf16[3072,192]{0,1:T(8,128)(2,1)}, bf16[3072,192]{0,1:T(8,128)(2,1)}, u32[]{:S(2)}, u32[]{:S(2)}) %collective-permute-start.1) | collective-permute-done | bytes 1179680 | tf_op jit(solution)/shard_map/ppermute | solution.py:189
  76.3 3.7 %pad_maximum_fusion = bf16[4,3072,192]{1,2,0:T(8,128)(2,1)} fusion(bf16[1,3072,192]{1,2,0:T(8,128)(2,1)} %bitcast.12, bf16[1,3072,192]{1,2,0:T(8,128)(2,1)} %bitcast.11, bf16[1,3072,192]{1,2,0:T(8,128)(2,1)S(1)} %bitcast.174, bf16[1,3072,192]{1,2,0:T(8,128)(2,1)S(1)} %get-tuple-element.52), kind=kLoop, calls=%fused_computation | loop fusion | flops 7077888 | bytes 9437184 | tf_op jit(solution)/shard_map/stack | solution.py:186
  80.0 1.6 reshape.181
  85.4 1.8 reshape.175.q_ref
  87.1 3.7 %shard_map.150 = (f32[512,768]{1,0:T(8,128)}, f32[512,1]{1,0:T(8,128)}, f32[512,1]{1,0:T(8,128)}) custom-call(s32[1]{0:T(128)} %bitcast.2.valid_ref, bf16[512,768]{1,0:T(8,128)(2,1)} %reshape.175.q_ref, bf16[1,4096,2,768]{3,2,1,0:T(2,128)(2,1)} %cache_ref.3), custom_call_target="tpu_custom_call" | custom-call | flops 6442450944 | bytes 14942208 | tf_op jit(solution)/shard_map/pallas_call | solution.py:86
  90.8 2.2 reshape.176
  99.3 40.7 %all-to-all-start = ((bf16[32,32,784]{2,1,0:T(8,128)(2,1)}), bf16[32,32,784]{2,1,0:T(8,128)(2,1)S(1)}, u32[]{:S(2)}, u32[]{:S(2)}) async-start(bf16[32,32,784]{2,1,0:T(8,128)(2,1)} %maximum_dynamic-update-slice_fusion), calls=%async_computation | async-start | bytes 3670016 | tf_op jit(solution)/shard_map/all_to_all | solution.py:236
  141.2 24.6 %all-to-all-done = bf16[32,32,784]{2,1,0:T(8,128)(2,1)S(1)} async-done(((bf16[32,32,784]{2,1,0:T(8,128)(2,1)}), bf16[32,32,784]{2,1,0:T(8,128)(2,1)S(1)}, u32[]{:S(2)}, u32[]{:S(2)}) %all-to-all-start) | async-done | bytes 1605664 | tf_op jit(solution)/shard_map/all_to_all | solution.py:236
  166.7 3.2 %fusion.16 = f32[32,3072]{1,0:T(8,128)S(1)} fusion(bf16[768,3072]{1,0:T(8,128)(2,1)} %param.18, f32[32,768]{1,0:T(8,128)S(1)} %div.48, f32[32,768]{1,0:T(8,128)S(1)} %reshape.182, f32[32,768]{1,0:T(8,128)S(1)} %mul.283, f32[32,768]{1,0:T(8,128)S(1)} %mul.278, f32[32,784]{1,0:T(8,128)S(1)} %get-tuple-element.51, f32[32,768]{1,0:T(8,128)S(1)} %mul.275, ...), kind=kOutput, calls=%fused_computation.54 | convolution fusion | flops 151166976 | bytes 5799936 | tf_op jit(solution)/shard_map/dot_general | solution.py:283
  171.2 2.4 collective-permute-start.4
  175.0 2.0 collective-permute-done.3
  180.1 4.0 %all-to-all-start.1 = ((bf16[32,8,3072]{2,1,0:T(8,128)(2,1)}), bf16[32,8,3072]{2,1,0:T(8,128)(2,1)S(1)}, u32[]{:S(2)}, u32[]{:S(2)}) async-start(bf16[32,8,3072]{2,1,0:T(8,128)(2,1)} %broadcast_in_dim.43), calls=%async_computation.1 | async-start | bytes 3145728 | tf_op jit(solution)/shard_map/all_to_all | solution.py:300
  184.1 3.4 %fusion.43 = (bf16[4,3072,64]{1,2,0:T(8,128)(2,1)}, bf16[4,3072,64]{1,2,0:T(8,128)(2,1)S(1)}) fusion(bf16[4,3072,192]{1,2,0:T(8,128)(2,1)} %pad_maximum_fusion), kind=kLoop, calls=%fused_computation.129 | loop fusion | bytes 6291456 | tf_op jit(solution)/shard_map/slice | solution.py:308
  187.5 19.7 %all-to-all-done.1 = bf16[32,8,3072]{2,1,0:T(8,128)(2,1)S(1)} async-done(((bf16[32,8,3072]{2,1,0:T(8,128)(2,1)}), bf16[32,8,3072]{2,1,0:T(8,128)(2,1)S(1)}, u32[]{:S(2)}, u32[]{:S(2)}) %all-to-all-start.1) | async-done | bytes 1572896 | tf_op jit(solution)/shard_map/all_to_all | solution.py:300
  207.2 2.0 fusion.4
  209.9 3.3 %fusion.1 = bf16[32,8,3072]{2,1,0:T(8,128)(2,1)} fusion(bf16[4,3072,192]{1,2,0:T(8,128)(2,1)} %pad_maximum_fusion, f32[256,4,64]{0,2,1:T(8,128)S(1)} %bitcast.180, f32[256,4,64]{0,2,1:T(8,128)S(1)} %bitcast.179), kind=kOutput, calls=%fused_computation.3 | convolution fusion | flops 403832832 | bytes 3670016 | tf_op jit(solution)/shard_map/rmj,mfj->rf/dot_general | solution.py:314
  213.1 4.0 %all-to-all-start.2 = ((bf16[32,8,3072]{2,1,0:T(8,128)(2,1)}), bf16[32,8,3072]{2,1,0:T(8,128)(2,1)S(1)}, u32[]{:S(2)}, u32[]{:S(2)}) async-start(bf16[32,8,3072]{2,1,0:T(8,128)(2,1)} %fusion.1), calls=%async_computation.2 | async-start | bytes 3145728 | tf_op jit(solution)/shard_map/all_to_all | solution.py:316
  217.1 23.1 %all-to-all-done.2 = bf16[32,8,3072]{2,1,0:T(8,128)(2,1)S(1)} async-done(((bf16[32,8,3072]{2,1,0:T(8,128)(2,1)}), bf16[32,8,3072]{2,1,0:T(8,128)(2,1)S(1)}, u32[]{:S(2)}, u32[]{:S(2)}) %all-to-all-start.2) | async-done | bytes 1572896 | tf_op jit(solution)/shard_map/all_to_all | solution.py:316
  242.3 2.6 %collective-permute-start.7 = (f32[8,769]{1,0:T(8,128)S(1)}, f32[8,769]{1,0:T(8,128)S(1)}, u32[]{:S(2)}, u32[]{:S(2)}) collective-permute-start(f32[8,769]{1,0:T(8,128)S(1)} %get-tuple-element.74), channel_id=1, source_target_pairs={{0,2},{1,3},{2,0},{3,1},{4,6},{5,7},{6,4},{7,5},{8,10},{9,11},{10,... | collective-permute-start | bytes 73832 | tf_op jit(solution)/shard_map/ppermute | solution.py:345
  245.9 1.8 collective-permute-done.7
  (136 shorter events, 35.2 us)
Async XLA Ops:
  7.2 10.9 %copy-start = (bf16[64,3072]{1,0:T(8,128)(2,1)S(1)}, bf16[64,3072]{1,0:T(8,128)(2,1)}, u32[]{:S(2)}) copy-start(bf16[64,3072]{1,0:T(8,128)(2,1)} %param.22) | copy-start | bytes 1179652
  7.2 10.9 %copy-start.2 = (bf16[3072,64]{0,1:T(8,128)(2,1)S(1)}, bf16[3072,64]{0,1:T(8,128)(2,1)}, u32[]{:S(2)}) copy-start(bf16[3072,64]{0,1:T(8,128)(2,1)} %param.20) | copy-start | bytes 1179652
  7.2 10.9 %copy-start.1 = (bf16[3072,64]{0,1:T(8,128)(2,1)S(1)}, bf16[3072,64]{0,1:T(8,128)(2,1)}, u32[]{:S(2)}) copy-start(bf16[3072,64]{0,1:T(8,128)(2,1)} %param.21) | copy-start | bytes 1179652
  7.2 72.8 %all-gather.2.cloned.1.call-start = ((), (), s32[]{:S(2)}) async-start(), calls=%async_computation.3 | async-start | bytes 1622016 | tf_op jit(solution)/shard_map/all_gather | solution.py:195
  18.1 7.9 %copy-start.14 = (s32[32]{0:T(128)S(1)}, s32[32]{0:T(128)}, u32[]{:S(2)}) copy-start(s32[32]{0:T(128)} %param.25) | copy-start | bytes 388
  19.5 45.1 %collective-permute-start = (bf16[3072,192]{0,1:T(8,128)(2,1)}, bf16[3072,192]{0,1:T(8,128)(2,1)S(1)}, u32[]{:S(2)}, u32[]{:S(2)}) collective-permute-start(bf16[3072,192]{0,1:T(8,128)(2,1)} %get-tuple-element.53), channel_id=1, source_target_pairs={{0,1},{1,2},{2,3},{3,0},{4,5},{5,6},{6,7},{7,4},{8,9},{9,10},{10,1... | collective-permute-start | bytes 3538952 | tf_op jit(solution)/shard_map/ppermute | solution.py:189
  21.5 54.9 %collective-permute-start.1 = (bf16[3072,192]{0,1:T(8,128)(2,1)}, bf16[3072,192]{0,1:T(8,128)(2,1)}, u32[]{:S(2)}, u32[]{:S(2)}) collective-permute-start(bf16[3072,192]{0,1:T(8,128)(2,1)} %get-tuple-element.53), channel_id=1, source_target_pairs={{0,2},{1,3},{2,0},{3,1},{4,6},{5,7},{6,4},{7,5},{8,10},{9,11},{10,... | collective-permute-start | bytes 3538952 | tf_op jit(solution)/shard_map/ppermute | solution.py:189
  25.0 51.3 %collective-permute-start.2 = (bf16[3072,192]{0,1:T(8,128)(2,1)}, bf16[3072,192]{0,1:T(8,128)(2,1)}, u32[]{:S(2)}, u32[]{:S(2)}) collective-permute-start(bf16[3072,192]{0,1:T(8,128)(2,1)} %get-tuple-element.53), channel_id=1, source_target_pairs={{0,3},{1,0},{2,1},{3,2},{4,7},{5,4},{6,5},{7,6},{8,11},{9,8},{10,9... | collective-permute-start | bytes 3538952 | tf_op jit(solution)/shard_map/ppermute | solution.py:189
  90.8 4.2 %copy-start.3 = (f32[512,1]{1,0:T(8,128)S(1)}, f32[512,1]{1,0:T(8,128)}, u32[]{:S(2)}) copy-start(f32[512,1]{1,0:T(8,128)} %get-tuple-element.19) | copy-start | bytes 6148
  99.3 41.0 %copy-start.6 = (bf16[16,8,2,2]{3,2,1,0:T(2,128)(2,1)S(1)}, bf16[16,8,2,2]{3,2,1,0:T(2,128)(2,1)}, u32[]{:S(2)}) copy-start(bf16[16,8,2,2]{3,2,1,0:T(2,128)(2,1)} %copy.164) | copy-start | bytes 3076
  99.3 41.0 %copy-start.7 = (f32[16,2,8]{1,2,0:T(8,128)S(1)}, f32[16,2,8]{1,2,0:T(8,128)}, u32[]{:S(2)}) copy-start(f32[16,2,8]{1,2,0:T(8,128)} %copy.162) | copy-start | bytes 3076
  99.3 41.0 %copy-start.8 = (bf16[16,2,1,8,96]{4,3,1,0,2:T(8,128)(2,1)S(1)}, bf16[16,2,1,8,96]{4,3,1,0,2:T(8,128)(2,1)}, u32[]{:S(2)}) copy-start(bf16[16,2,1,8,96]{4,3,1,0,2:T(8,128)(2,1)} %get-tuple-element.65) | copy-start | bytes 147460
  99.3 66.5 %all-to-all-start = ((bf16[32,32,784]{2,1,0:T(8,128)(2,1)}), bf16[32,32,784]{2,1,0:T(8,128)(2,1)S(1)}, u32[]{:S(2)}, u32[]{:S(2)}) async-start(bf16[32,32,784]{2,1,0:T(8,128)(2,1)} %maximum_dynamic-update-slice_fusion), calls=%async_computation | async-start | bytes 3670016 | tf_op jit(solution)/shard_map/all_to_all | solution.py:236
  166.7 12.0 %copy-start.13 = (f32[3072]{0:T(1024)S(1)}, f32[3072]{0:T(1024)}, u32[]{:S(2)}) copy-start(f32[3072]{0:T(1024)} %param.19) | copy-start | bytes 36868
  170.0 7.0 %collective-permute-start.3 = (f32[8,3072]{1,0:T(8,128)S(1)}, f32[8,3072]{1,0:T(8,128)S(1)}, u32[]{:S(2)}, u32[]{:S(2)}) collective-permute-start(f32[8,3072]{1,0:T(8,128)S(1)} %get-tuple-element.62), channel_id=1, source_target_pairs={{0,1},{1,2},{2,3},{3,0},{4,5},{5,6},{6,7},{7,4},{8,9},{9,10},{10,1... | collective-permute-start | bytes 294920 | tf_op jit(solution)/shard_map/ppermute | solution.py:293
  171.2 6.9 %collective-permute-start.4 = (f32[8,3072]{1,0:T(8,128)S(1)}, f32[8,3072]{1,0:T(8,128)S(1)}, u32[]{:S(2)}, u32[]{:S(2)}) collective-permute-start(f32[8,3072]{1,0:T(8,128)S(1)} %get-tuple-element.64), channel_id=1, source_target_pairs={{0,2},{1,3},{2,0},{3,1},{4,6},{5,7},{6,4},{7,5},{8,10},{9,11},{10,... | collective-permute-start | bytes 294920 | tf_op jit(solution)/shard_map/ppermute | solution.py:293
  173.6 4.9 %collective-permute-start.5 = (f32[8,3072]{1,0:T(8,128)S(1)}, f32[8,3072]{1,0:T(8,128)S(1)}, u32[]{:S(2)}, u32[]{:S(2)}) collective-permute-start(f32[8,3072]{1,0:T(8,128)S(1)} %get-tuple-element.63), channel_id=1, source_target_pairs={{0,3},{1,0},{2,1},{3,2},{4,7},{5,4},{6,5},{7,6},{8,11},{9,8},{10,9... | collective-permute-start | bytes 294920 | tf_op jit(solution)/shard_map/ppermute | solution.py:293
  180.1 27.1 %all-to-all-start.1 = ((bf16[32,8,3072]{2,1,0:T(8,128)(2,1)}), bf16[32,8,3072]{2,1,0:T(8,128)(2,1)S(1)}, u32[]{:S(2)}, u32[]{:S(2)}) async-start(bf16[32,8,3072]{2,1,0:T(8,128)(2,1)} %broadcast_in_dim.43), calls=%async_computation.1 | async-start | bytes 3145728 | tf_op jit(solution)/shard_map/all_to_all | solution.py:300
  213.1 27.1 %all-to-all-start.2 = ((bf16[32,8,3072]{2,1,0:T(8,128)(2,1)}), bf16[32,8,3072]{2,1,0:T(8,128)(2,1)S(1)}, u32[]{:S(2)}, u32[]{:S(2)}) async-start(bf16[32,8,3072]{2,1,0:T(8,128)(2,1)} %fusion.1), calls=%async_computation.2 | async-start | bytes 3145728 | tf_op jit(solution)/shard_map/all_to_all | solution.py:316
  217.1 23.3 %copy-start.11 = (f32[3072]{0:T(1024)S(1)}, f32[3072]{0:T(1024)}, u32[]{:S(2)}) copy-start(f32[3072]{0:T(1024)} %param.24) | copy-start | bytes 36868
  217.1 23.3 %copy-start.12 = (f32[3072]{0:T(1024)S(1)}, f32[3072]{0:T(1024)}, u32[]{:S(2)}) copy-start(f32[3072]{0:T(1024)} %param.23) | copy-start | bytes 36868
  240.7 5.2 %collective-permute-start.6 = (f32[8,769]{1,0:T(8,128)S(1)}, f32[8,769]{1,0:T(8,128)S(1)}, u32[]{:S(2)}, u32[]{:S(2)}) collective-permute-start(f32[8,769]{1,0:T(8,128)S(1)} %get-tuple-element.73), channel_id=1, source_target_pairs={{0,1},{1,2},{2,3},{3,0},{4,5},{5,6},{6,7},{7,4},{8,9},{9,10},{10,1... | collective-permute-start | bytes 73832 | tf_op jit(solution)/shard_map/ppermute | solution.py:345
  242.3 5.4 %collective-permute-start.7 = (f32[8,769]{1,0:T(8,128)S(1)}, f32[8,769]{1,0:T(8,128)S(1)}, u32[]{:S(2)}, u32[]{:S(2)}) collective-permute-start(f32[8,769]{1,0:T(8,128)S(1)} %get-tuple-element.74), channel_id=1, source_target_pairs={{0,2},{1,3},{2,0},{3,1},{4,6},{5,7},{6,4},{7,5},{8,10},{9,11},{10,... | collective-permute-start | bytes 73832 | tf_op jit(solution)/shard_map/ppermute | solution.py:345
  244.9 3.9 %collective-permute-start.8 = (f32[8,769]{1,0:T(8,128)S(1)}, f32[8,769]{1,0:T(8,128)S(1)}, u32[]{:S(2)}, u32[]{:S(2)}) collective-permute-start(f32[8,769]{1,0:T(8,128)S(1)} %get-tuple-element.72), channel_id=1, source_target_pairs={{0,3},{1,0},{2,1},{3,2},{4,7},{5,4},{6,5},{7,6},{8,11},{9,8},{10,9... | collective-permute-start | bytes 73832 | tf_op jit(solution)/shard_map/ppermute | solution.py:345
  (4 other events, 6.9 us)
Sparse Core Ops, SparseCore 0:
  18.2 45.6 all-gather.1

commit v11 on v10

--- a/solution.py
+++ b/solution.py
@@ -30,6 +30,7 @@
 
 def prompt_kernel(block_len, score_scale, valid_ref, q_ref, cache_ref, acc_ref, top_ref, sum_ref):
     number = pl.program_id(0)
+    start = number * block_len
 
     @pl.when(number == 0)
     def _():
@@ -37,8 +38,7 @@
         top_ref[...] = jnp.full_like(top_ref, masked_value)
         sum_ref[...] = jnp.zeros_like(sum_ref)
 
-    @pl.when(number * block_len < valid_ref[0])
-    def _():
+    def step(masked):
         keys = cache_ref[:, 0, :]
         values = cache_ref[:, 1, :]
         scores = (
@@ -47,8 +47,9 @@
             )
             * score_scale
         )
-        places = number * block_len + lax.broadcasted_iota(jnp.int32, scores.shape, 1)
-        scores = jnp.where(places < valid_ref[0], scores, masked_value)
+        if masked:
+            places = start + lax.broadcasted_iota(jnp.int32, scores.shape, 1)
+            scores = jnp.where(places < valid_ref[0], scores, masked_value)
         top_old = top_ref[...]
         top_new = jnp.maximum(top_old, jnp.max(scores, axis=1, keepdims=True))
         shrink = jnp.exp(top_old - top_new)
@@ -58,6 +59,14 @@
             weights.astype(jnp.bfloat16), values, preferred_element_type=jnp.float32
         )
         top_ref[...] = top_new
+
+    @pl.when(start + block_len <= valid_ref[0])
+    def _():
+        step(False)
+
+    @pl.when(jnp.logical_and(start < valid_ref[0], start + block_len > valid_ref[0]))
+    def _():
+        step(True)
 
 
 def prompt_attention(q_diag, cache, valid_count, score_scale):

time: 258 us -> 258 us (level)
  starting transfers between devices: 65 us -> 31.5 us
  Pallas kernels: 34.5 us -> 67.7 us
    all_to_all x1, starting transfers between devices: 40.7 us -> 7.18 us  [per_device(): lax.all_to_all(outgoing, 'req', split_axis=0, concat_axis=0, tiled=True)]
    pallas_call x1, Pallas kernels: 3.7 us -> 36.9 us  [prompt_attention(): pl.pallas_call(functools.partial(prompt_kernel, block_len, score_scale),...]
where the time goes in v11:
time: 258 us; the launch traced here: 257 us
  waiting for transfers between devices  86.1 us (33%)
  Pallas kernels  67.7 us (26%)
  starting transfers between devices  31.5 us (12%)
  local copies, waits for them, and re-layouts  27.5 us (11%)
  between operations  21.8 us (8%)
  other arithmetic  12.4 us (5%)
  matrix products  9.75 us (4%)
    pallas_call x1, Pallas kernels, prompt_attention(): pl.pallas_call(functools.partial(prompt_kernel, block_len, score_scale),...  36.9 us
    pallas_call x1, Pallas kernels, tail_attention(): pl.pallas_call(functools.partial(tail_kernel, score_scale), grid_spec=spe...  30.8 us
    all_to_all x1, waiting for transfers between devices, per_device(): lax.all_to_all(outgoing, 'req', split_axis=0, concat_axis=0, tiled=True)  24.8 us
    all_to_all x1, waiting for transfers between devices, per_device(): lax.all_to_all(down_sum.astype(jnp.bfloat16).reshape(req_count, share, wi...  23.1 us
    all_to_all x1, waiting for transfers between devices, per_device(): lax.all_to_all(jnp.broadcast_to(normed_share[None], (req_count,) + normed...  19.7 us
    ppermute x3, waiting for transfers between devices, per_device(): lax.ppermute(weights_cat, 'mlp', [(m, (m + shift) % mlp_count) for m in r...  11.8 us
    all_to_all x1, starting transfers between devices, per_device(): lax.all_to_all(outgoing, 'req', split_axis=0, concat_axis=0, tiled=True)  7.18 us
    ppermute x3, starting transfers between devices, per_device(): lax.ppermute(weights_cat, 'mlp', [(m, (m + shift) % mlp_count) for m in r...  6.59 us
  transfers between devices with their start and end apart: 13, of which 10 were waited for; matrix products, arithmetic and copies ran while one was open for 5% of the time, Pallas kernels for 12%

profile of v11, /device:TPU:0, one launch (start us, length us, event | category | flops | bytes accessed | tf_op | source)
XLA Modules:
  0.0 256.8 jit_solution(9208758630797100608)
XLA Ops:
  12.6 2.0 broadcast_add_fusion
  19.5 2.0 collective-permute-start
  21.5 3.6 %collective-permute-start.1 = (bf16[3072,192]{0,1:T(8,128)(2,1)}, bf16[3072,192]{0,1:T(8,128)(2,1)}, u32[]{:S(2)}, u32[]{:S(2)}) collective-permute-start(bf16[3072,192]{0,1:T(8,128)(2,1)} %get-tuple-element.53), channel_id=1, source_target_pairs={{0,2},{1,3},{2,0},{3,1},{4,6},{5,7},{6,4},{7,5},{8,10},{9,11},{10,... | collective-permute-start | bytes 3538952 | tf_op jit(solution)/shard_map/ppermute | solution.py:198
  33.7 30.8 %shard_map.149 = (f32[16,16,768]{2,1,0:T(8,128)}, f32[16,16,1]{2,1,0:T(8,128)}, f32[16,16,1]{2,1,0:T(8,128)}) custom-call(s32[16]{0:T(128)} %get-tuple-element.39.lens_ref, bf16[16,16,768]{2,1,0:T(8,128)(2,1)} %reshape.172.q_ref, bf16[16,256,2,768]{3,2,1,0:T(2,128)(2,1)} %cache_ref.2), custom_call_target="tpu_custom_call" | custom-call | flops 201326592 | bytes 13762560 | tf_op jit(solution)/shard_map/pallas_call | solution.py:144
  64.5 11.8 %collective-permute-done.1 = bf16[3072,192]{0,1:T(8,128)(2,1)} collective-permute-done((bf16[3072,192]{0,1:T(8,128)(2,1)}, bf16[3072,192]{0,1:T(8,128)(2,1)}, u32[]{:S(2)}, u32[]{:S(2)}) %collective-permute-start.1) | collective-permute-done | bytes 1179680 | tf_op jit(solution)/shard_map/ppermute | solution.py:198
  76.3 3.7 %pad_maximum_fusion = bf16[4,3072,192]{1,2,0:T(8,128)(2,1)} fusion(bf16[1,3072,192]{1,2,0:T(8,128)(2,1)} %bitcast.12, bf16[1,3072,192]{1,2,0:T(8,128)(2,1)} %bitcast.11, bf16[1,3072,192]{1,2,0:T(8,128)(2,1)S(1)} %bitcast.174, bf16[1,3072,192]{1,2,0:T(8,128)(2,1)S(1)} %get-tuple-element.52), kind=kLoop, calls=%fused_computation | loop fusion | flops 7077888 | bytes 9437184 | tf_op jit(solution)/shard_map/stack | solution.py:195
  80.0 1.6 reshape.181
  85.4 1.8 reshape.175.q_ref
  87.1 36.9 %shard_map.150 = (f32[512,768]{1,0:T(8,128)}, f32[512,1]{1,0:T(8,128)}, f32[512,1]{1,0:T(8,128)}) custom-call(s32[1]{0:T(128)} %bitcast.2.valid_ref, bf16[512,768]{1,0:T(8,128)(2,1)} %reshape.175.q_ref, bf16[1,4096,2,768]{3,2,1,0:T(2,128)(2,1)} %cache_ref.3), custom_call_target="tpu_custom_call" | custom-call | flops 6442450944 | bytes 14942208 | tf_op jit(solution)/shard_map/pallas_call | solution.py:95
  124.1 2.2 reshape.176
  132.5 7.2 %all-to-all-start = ((bf16[32,32,784]{2,1,0:T(8,128)(2,1)}), bf16[32,32,784]{2,1,0:T(8,128)(2,1)S(1)}, u32[]{:S(2)}, u32[]{:S(2)}) async-start(bf16[32,32,784]{2,1,0:T(8,128)(2,1)} %maximum_dynamic-update-slice_fusion), calls=%async_computation | async-start | bytes 3670016 | tf_op jit(solution)/shard_map/all_to_all | solution.py:245
  140.9 24.8 %all-to-all-done = bf16[32,32,784]{2,1,0:T(8,128)(2,1)S(1)} async-done(((bf16[32,32,784]{2,1,0:T(8,128)(2,1)}), bf16[32,32,784]{2,1,0:T(8,128)(2,1)S(1)}, u32[]{:S(2)}, u32[]{:S(2)}) %all-to-all-start) | async-done | bytes 1605664 | tf_op jit(solution)/shard_map/all_to_all | solution.py:245
  166.7 3.2 %fusion.16 = f32[32,3072]{1,0:T(8,128)S(1)} fusion(bf16[768,3072]{1,0:T(8,128)(2,1)} %param.18, f32[32,768]{1,0:T(8,128)S(1)} %div.48, f32[32,768]{1,0:T(8,128)S(1)} %reshape.182, f32[32,768]{1,0:T(8,128)S(1)} %mul.283, f32[32,768]{1,0:T(8,128)S(1)} %mul.278, f32[32,784]{1,0:T(8,128)S(1)} %get-tuple-element.51, f32[32,768]{1,0:T(8,128)S(1)} %mul.275, ...), kind=kOutput, calls=%fused_computation.54 | convolution fusion | flops 151166976 | bytes 5799936 | tf_op jit(solution)/shard_map/dot_general | solution.py:292
  171.2 2.4 collective-permute-start.4
  174.9 2.0 collective-permute-done.3
  180.1 4.0 %all-to-all-start.1 = ((bf16[32,8,3072]{2,1,0:T(8,128)(2,1)}), bf16[32,8,3072]{2,1,0:T(8,128)(2,1)S(1)}, u32[]{:S(2)}, u32[]{:S(2)}) async-start(bf16[32,8,3072]{2,1,0:T(8,128)(2,1)} %broadcast_in_dim.43), calls=%async_computation.1 | async-start | bytes 3145728 | tf_op jit(solution)/shard_map/all_to_all | solution.py:309
  184.0 3.4 %fusion.43 = (bf16[4,3072,64]{1,2,0:T(8,128)(2,1)}, bf16[4,3072,64]{1,2,0:T(8,128)(2,1)S(1)}) fusion(bf16[4,3072,192]{1,2,0:T(8,128)(2,1)} %pad_maximum_fusion), kind=kLoop, calls=%fused_computation.129 | loop fusion | bytes 6291456 | tf_op jit(solution)/shard_map/slice | solution.py:317
  187.4 19.7 %all-to-all-done.1 = bf16[32,8,3072]{2,1,0:T(8,128)(2,1)S(1)} async-done(((bf16[32,8,3072]{2,1,0:T(8,128)(2,1)}), bf16[32,8,3072]{2,1,0:T(8,128)(2,1)S(1)}, u32[]{:S(2)}, u32[]{:S(2)}) %all-to-all-start.1) | async-done | bytes 1572896 | tf_op jit(solution)/shard_map/all_to_all | solution.py:309
  207.2 2.0 fusion.4
  209.8 3.3 %fusion.1 = bf16[32,8,3072]{2,1,0:T(8,128)(2,1)} fusion(bf16[4,3072,192]{1,2,0:T(8,128)(2,1)} %pad_maximum_fusion, f32[256,4,64]{0,2,1:T(8,128)S(1)} %bitcast.180, f32[256,4,64]{0,2,1:T(8,128)S(1)} %bitcast.179), kind=kOutput, calls=%fused_computation.3 | convolution fusion | flops 403832832 | bytes 3670016 | tf_op jit(solution)/shard_map/rmj,mfj->rf/dot_general | solution.py:323
  213.1 4.0 %all-to-all-start.2 = ((bf16[32,8,3072]{2,1,0:T(8,128)(2,1)}), bf16[32,8,3072]{2,1,0:T(8,128)(2,1)S(1)}, u32[]{:S(2)}, u32[]{:S(2)}) async-start(bf16[32,8,3072]{2,1,0:T(8,128)(2,1)} %fusion.1), calls=%async_computation.2 | async-start | bytes 3145728 | tf_op jit(solution)/shard_map/all_to_all | solution.py:325
  217.1 23.1 %all-to-all-done.2 = bf16[32,8,3072]{2,1,0:T(8,128)(2,1)S(1)} async-done(((bf16[32,8,3072]{2,1,0:T(8,128)(2,1)}), bf16[32,8,3072]{2,1,0:T(8,128)(2,1)S(1)}, u32[]{:S(2)}, u32[]{:S(2)}) %all-to-all-start.2) | async-done | bytes 1572896 | tf_op jit(solution)/shard_map/all_to_all | solution.py:325
  242.2 2.6 %collective-permute-start.7 = (f32[8,769]{1,0:T(8,128)S(1)}, f32[8,769]{1,0:T(8,128)S(1)}, u32[]{:S(2)}, u32[]{:S(2)}) collective-permute-start(f32[8,769]{1,0:T(8,128)S(1)} %get-tuple-element.74), channel_id=1, source_target_pairs={{0,2},{1,3},{2,0},{3,1},{4,6},{5,7},{6,4},{7,5},{8,10},{9,11},{10,... | collective-permute-start | bytes 73832 | tf_op jit(solution)/shard_map/ppermute | solution.py:354
  245.8 1.8 collective-permute-done.7
  (136 shorter events, 35.2 us)
Async XLA Ops:
  7.2 10.9 %copy-start = (bf16[64,3072]{1,0:T(8,128)(2,1)S(1)}, bf16[64,3072]{1,0:T(8,128)(2,1)}, u32[]{:S(2)}) copy-start(bf16[64,3072]{1,0:T(8,128)(2,1)} %param.22) | copy-start | bytes 1179652
  7.2 10.9 %copy-start.2 = (bf16[3072,64]{0,1:T(8,128)(2,1)S(1)}, bf16[3072,64]{0,1:T(8,128)(2,1)}, u32[]{:S(2)}) copy-start(bf16[3072,64]{0,1:T(8,128)(2,1)} %param.20) | copy-start | bytes 1179652
  7.2 10.9 %copy-start.1 = (bf16[3072,64]{0,1:T(8,128)(2,1)S(1)}, bf16[3072,64]{0,1:T(8,128)(2,1)}, u32[]{:S(2)}) copy-start(bf16[3072,64]{0,1:T(8,128)(2,1)} %param.21) | copy-start | bytes 1179652
  7.2 72.8 %all-gather.2.cloned.1.call-start = ((), (), s32[]{:S(2)}) async-start(), calls=%async_computation.3 | async-start | bytes 1622016 | tf_op jit(solution)/shard_map/all_gather | solution.py:204
  18.1 7.9 %copy-start.14 = (s32[32]{0:T(128)S(1)}, s32[32]{0:T(128)}, u32[]{:S(2)}) copy-start(s32[32]{0:T(128)} %param.25) | copy-start | bytes 388
  19.5 45.1 %collective-permute-start = (bf16[3072,192]{0,1:T(8,128)(2,1)}, bf16[3072,192]{0,1:T(8,128)(2,1)S(1)}, u32[]{:S(2)}, u32[]{:S(2)}) collective-permute-start(bf16[3072,192]{0,1:T(8,128)(2,1)} %get-tuple-element.53), channel_id=1, source_target_pairs={{0,1},{1,2},{2,3},{3,0},{4,5},{5,6},{6,7},{7,4},{8,9},{9,10},{10,1... | collective-permute-start | bytes 3538952 | tf_op jit(solution)/shard_map/ppermute | solution.py:198
  21.5 54.9 %collective-permute-start.1 = (bf16[3072,192]{0,1:T(8,128)(2,1)}, bf16[3072,192]{0,1:T(8,128)(2,1)}, u32[]{:S(2)}, u32[]{:S(2)}) collective-permute-start(bf16[3072,192]{0,1:T(8,128)(2,1)} %get-tuple-element.53), channel_id=1, source_target_pairs={{0,2},{1,3},{2,0},{3,1},{4,6},{5,7},{6,4},{7,5},{8,10},{9,11},{10,... | collective-permute-start | bytes 3538952 | tf_op jit(solution)/shard_map/ppermute | solution.py:198
  25.0 51.3 %collective-permute-start.2 = (bf16[3072,192]{0,1:T(8,128)(2,1)}, bf16[3072,192]{0,1:T(8,128)(2,1)}, u32[]{:S(2)}, u32[]{:S(2)}) collective-permute-start(bf16[3072,192]{0,1:T(8,128)(2,1)} %get-tuple-element.53), channel_id=1, source_target_pairs={{0,3},{1,0},{2,1},{3,2},{4,7},{5,4},{6,5},{7,6},{8,11},{9,8},{10,9... | collective-permute-start | bytes 3538952 | tf_op jit(solution)/shard_map/ppermute | solution.py:198
  124.1 4.2 %copy-start.3 = (f32[512,1]{1,0:T(8,128)S(1)}, f32[512,1]{1,0:T(8,128)}, u32[]{:S(2)}) copy-start(f32[512,1]{1,0:T(8,128)} %get-tuple-element.19) | copy-start | bytes 6148
  132.5 7.5 %copy-start.6 = (bf16[16,8,2,2]{3,2,1,0:T(2,128)(2,1)S(1)}, bf16[16,8,2,2]{3,2,1,0:T(2,128)(2,1)}, u32[]{:S(2)}) copy-start(bf16[16,8,2,2]{3,2,1,0:T(2,128)(2,1)} %copy.164) | copy-start | bytes 3076
  132.5 7.5 %copy-start.7 = (f32[16,2,8]{1,2,0:T(8,128)S(1)}, f32[16,2,8]{1,2,0:T(8,128)}, u32[]{:S(2)}) copy-start(f32[16,2,8]{1,2,0:T(8,128)} %copy.162) | copy-start | bytes 3076
  132.5 7.5 %copy-start.8 = (bf16[16,2,1,8,96]{4,3,1,0,2:T(8,128)(2,1)S(1)}, bf16[16,2,1,8,96]{4,3,1,0,2:T(8,128)(2,1)}, u32[]{:S(2)}) copy-start(bf16[16,2,1,8,96]{4,3,1,0,2:T(8,128)(2,1)} %get-tuple-element.65) | copy-start | bytes 147460
  132.5 33.2 %all-to-all-start = ((bf16[32,32,784]{2,1,0:T(8,128)(2,1)}), bf16[32,32,784]{2,1,0:T(8,128)(2,1)S(1)}, u32[]{:S(2)}, u32[]{:S(2)}) async-start(bf16[32,32,784]{2,1,0:T(8,128)(2,1)} %maximum_dynamic-update-slice_fusion), calls=%async_computation | async-start | bytes 3670016 | tf_op jit(solution)/shard_map/all_to_all | solution.py:245
  166.6 12.0 %copy-start.13 = (f32[3072]{0:T(1024)S(1)}, f32[3072]{0:T(1024)}, u32[]{:S(2)}) copy-start(f32[3072]{0:T(1024)} %param.19) | copy-start | bytes 36868
  170.0 7.0 %collective-permute-start.3 = (f32[8,3072]{1,0:T(8,128)S(1)}, f32[8,3072]{1,0:T(8,128)S(1)}, u32[]{:S(2)}, u32[]{:S(2)}) collective-permute-start(f32[8,3072]{1,0:T(8,128)S(1)} %get-tuple-element.62), channel_id=1, source_target_pairs={{0,1},{1,2},{2,3},{3,0},{4,5},{5,6},{6,7},{7,4},{8,9},{9,10},{10,1... | collective-permute-start | bytes 294920 | tf_op jit(solution)/shard_map/ppermute | solution.py:302
  171.2 6.9 %collective-permute-start.4 = (f32[8,3072]{1,0:T(8,128)S(1)}, f32[8,3072]{1,0:T(8,128)S(1)}, u32[]{:S(2)}, u32[]{:S(2)}) collective-permute-start(f32[8,3072]{1,0:T(8,128)S(1)} %get-tuple-element.64), channel_id=1, source_target_pairs={{0,2},{1,3},{2,0},{3,1},{4,6},{5,7},{6,4},{7,5},{8,10},{9,11},{10,... | collective-permute-start | bytes 294920 | tf_op jit(solution)/shard_map/ppermute | solution.py:302
  173.6 4.9 %collective-permute-start.5 = (f32[8,3072]{1,0:T(8,128)S(1)}, f32[8,3072]{1,0:T(8,128)S(1)}, u32[]{:S(2)}, u32[]{:S(2)}) collective-permute-start(f32[8,3072]{1,0:T(8,128)S(1)} %get-tuple-element.63), channel_id=1, source_target_pairs={{0,3},{1,0},{2,1},{3,2},{4,7},{5,4},{6,5},{7,6},{8,11},{9,8},{10,9... | collective-permute-start | bytes 294920 | tf_op jit(solution)/shard_map/ppermute | solution.py:302
  180.1 27.1 %all-to-all-start.1 = ((bf16[32,8,3072]{2,1,0:T(8,128)(2,1)}), bf16[32,8,3072]{2,1,0:T(8,128)(2,1)S(1)}, u32[]{:S(2)}, u32[]{:S(2)}) async-start(bf16[32,8,3072]{2,1,0:T(8,128)(2,1)} %broadcast_in_dim.43), calls=%async_computation.1 | async-start | bytes 3145728 | tf_op jit(solution)/shard_map/all_to_all | solution.py:309
  213.1 27.1 %all-to-all-start.2 = ((bf16[32,8,3072]{2,1,0:T(8,128)(2,1)}), bf16[32,8,3072]{2,1,0:T(8,128)(2,1)S(1)}, u32[]{:S(2)}, u32[]{:S(2)}) async-start(bf16[32,8,3072]{2,1,0:T(8,128)(2,1)} %fusion.1), calls=%async_computation.2 | async-start | bytes 3145728 | tf_op jit(solution)/shard_map/all_to_all | solution.py:325
  217.0 23.3 %copy-start.11 = (f32[3072]{0:T(1024)S(1)}, f32[3072]{0:T(1024)}, u32[]{:S(2)}) copy-start(f32[3072]{0:T(1024)} %param.24) | copy-start | bytes 36868
  217.0 23.3 %copy-start.12 = (f32[3072]{0:T(1024)S(1)}, f32[3072]{0:T(1024)}, u32[]{:S(2)}) copy-start(f32[3072]{0:T(1024)} %param.23) | copy-start | bytes 36868
  240.7 5.2 %collective-permute-start.6 = (f32[8,769]{1,0:T(8,128)S(1)}, f32[8,769]{1,0:T(8,128)S(1)}, u32[]{:S(2)}, u32[]{:S(2)}) collective-permute-start(f32[8,769]{1,0:T(8,128)S(1)} %get-tuple-element.73), channel_id=1, source_target_pairs={{0,1},{1,2},{2,3},{3,0},{4,5},{5,6},{6,7},{7,4},{8,9},{9,10},{10,1... | collective-permute-start | bytes 73832 | tf_op jit(solution)/shard_map/ppermute | solution.py:354
  242.2 5.4 %collective-permute-start.7 = (f32[8,769]{1,0:T(8,128)S(1)}, f32[8,769]{1,0:T(8,128)S(1)}, u32[]{:S(2)}, u32[]{:S(2)}) collective-permute-start(f32[8,769]{1,0:T(8,128)S(1)} %get-tuple-element.74), channel_id=1, source_target_pairs={{0,2},{1,3},{2,0},{3,1},{4,6},{5,7},{6,4},{7,5},{8,10},{9,11},{10,... | collective-permute-start | bytes 73832 | tf_op jit(solution)/shard_map/ppermute | solution.py:354
  244.8 3.9 %collective-permute-start.8 = (f32[8,769]{1,0:T(8,128)S(1)}, f32[8,769]{1,0:T(8,128)S(1)}, u32[]{:S(2)}, u32[]{:S(2)}) collective-permute-start(f32[8,769]{1,0:T(8,128)S(1)} %get-tuple-element.72), channel_id=1, source_target_pairs={{0,3},{1,0},{2,1},{3,2},{4,7},{5,4},{6,5},{7,6},{8,11},{9,8},{10,9... | collective-permute-start | bytes 73832 | tf_op jit(solution)/shard_map/ppermute | solution.py:354
  (4 other events, 6.9 us)
Sparse Core Ops, SparseCore 0:
  18.2 45.6 all-gather.1

commit v12 on v10

--- a/solution.py
+++ b/solution.py
@@ -30,6 +30,7 @@
 
 def prompt_kernel(block_len, score_scale, valid_ref, q_ref, cache_ref, acc_ref, top_ref, sum_ref):
     number = pl.program_id(0)
+    start = number * block_len
 
     @pl.when(number == 0)
     def _():
@@ -37,18 +38,19 @@
         top_ref[...] = jnp.full_like(top_ref, masked_value)
         sum_ref[...] = jnp.zeros_like(sum_ref)
 
-    @pl.when(number * block_len < valid_ref[0])
+    @pl.when(start < valid_ref[0])
     def _():
         keys = cache_ref[:, 0, :]
         values = cache_ref[:, 1, :]
+        places = start + lax.broadcasted_iota(jnp.int32, (1, block_len), 1)
+        bias = jnp.where(places < valid_ref[0], 0.0, masked_value)
         scores = (
             lax.dot_general(
                 q_ref[...], keys, (((1,), (1,)), ((), ())), preferred_element_type=jnp.float32
             )
             * score_scale
+            + bias
         )
-        places = number * block_len + lax.broadcasted_iota(jnp.int32, scores.shape, 1)
-        scores = jnp.where(places < valid_ref[0], scores, masked_value)
         top_old = top_ref[...]
         top_new = jnp.maximum(top_old, jnp.max(scores, axis=1, keepdims=True))
         shrink = jnp.exp(top_old - top_new)

time: 258 us -> 258 us (level)
  Pallas kernels: 34.5 us -> 51 us
  starting transfers between devices: 65 us -> 48.5 us
    pallas_call x1, Pallas kernels: 3.7 us -> 20.2 us  [prompt_attention(): pl.pallas_call(functools.partial(prompt_kernel, block_len, score_scale),...]
    all_to_all x1, starting transfers between devices: 40.7 us -> 24.2 us  [per_device(): lax.all_to_all(outgoing, 'req', split_axis=0, concat_axis=0, tiled=True)]
where the time goes in v12:
time: 258 us; the launch traced here: 257 us
  waiting for transfers between devices  85.9 us (33%)
  Pallas kernels  51 us (20%)
  starting transfers between devices  48.5 us (19%)
  local copies, waits for them, and re-layouts  27.5 us (11%)
  between operations  21.8 us (8%)
  other arithmetic  12.4 us (5%)
  matrix products  9.75 us (4%)
    pallas_call x1, Pallas kernels, tail_attention(): pl.pallas_call(functools.partial(tail_kernel, score_scale), grid_spec=spe...  30.8 us
    all_to_all x1, waiting for transfers between devices, per_device(): lax.all_to_all(outgoing, 'req', split_axis=0, concat_axis=0, tiled=True)  24.6 us
    all_to_all x1, starting transfers between devices, per_device(): lax.all_to_all(outgoing, 'req', split_axis=0, concat_axis=0, tiled=True)  24.2 us
    all_to_all x1, waiting for transfers between devices, per_device(): lax.all_to_all(down_sum.astype(jnp.bfloat16).reshape(req_count, share, wi...  23.1 us
    pallas_call x1, Pallas kernels, prompt_attention(): pl.pallas_call(functools.partial(prompt_kernel, block_len, score_scale),...  20.2 us
    all_to_all x1, waiting for transfers between devices, per_device(): lax.all_to_all(jnp.broadcast_to(normed_share[None], (req_count,) + normed...  19.7 us
    ppermute x3, waiting for transfers between devices, per_device(): lax.ppermute(weights_cat, 'mlp', [(m, (m + shift) % mlp_count) for m in r...  11.8 us
    ppermute x3, starting transfers between devices, per_device(): lax.ppermute(weights_cat, 'mlp', [(m, (m + shift) % mlp_count) for m in r...  6.59 us
  transfers between devices with their start and end apart: 13, of which 10 were waited for; matrix products, arithmetic and copies ran while one was open for 5% of the time, Pallas kernels for 12%

profile of v12, /device:TPU:0, one launch (start us, length us, event | category | flops | bytes accessed | tf_op | source)
XLA Modules:
  0.0 256.8 jit_solution(15801002588357492337)
XLA Ops:
  12.6 2.0 broadcast_add_fusion
  19.5 2.0 collective-permute-start
  21.5 3.6 %collective-permute-start.1 = (bf16[3072,192]{0,1:T(8,128)(2,1)}, bf16[3072,192]{0,1:T(8,128)(2,1)}, u32[]{:S(2)}, u32[]{:S(2)}) collective-permute-start(bf16[3072,192]{0,1:T(8,128)(2,1)} %get-tuple-element.53), channel_id=1, source_target_pairs={{0,2},{1,3},{2,0},{3,1},{4,6},{5,7},{6,4},{7,5},{8,10},{9,11},{10,... | collective-permute-start | bytes 3538952 | tf_op jit(solution)/shard_map/ppermute | solution.py:191
  33.7 30.8 %shard_map.149 = (f32[16,16,768]{2,1,0:T(8,128)}, f32[16,16,1]{2,1,0:T(8,128)}, f32[16,16,1]{2,1,0:T(8,128)}) custom-call(s32[16]{0:T(128)} %get-tuple-element.39.lens_ref, bf16[16,16,768]{2,1,0:T(8,128)(2,1)} %reshape.172.q_ref, bf16[16,256,2,768]{3,2,1,0:T(2,128)(2,1)} %cache_ref.2), custom_call_target="tpu_custom_call" | custom-call | flops 201326592 | bytes 13762560 | tf_op jit(solution)/shard_map/pallas_call | solution.py:137
  64.5 11.8 %collective-permute-done.1 = bf16[3072,192]{0,1:T(8,128)(2,1)} collective-permute-done((bf16[3072,192]{0,1:T(8,128)(2,1)}, bf16[3072,192]{0,1:T(8,128)(2,1)}, u32[]{:S(2)}, u32[]{:S(2)}) %collective-permute-start.1) | collective-permute-done | bytes 1179680 | tf_op jit(solution)/shard_map/ppermute | solution.py:191
  76.3 3.7 %pad_maximum_fusion = bf16[4,3072,192]{1,2,0:T(8,128)(2,1)} fusion(bf16[1,3072,192]{1,2,0:T(8,128)(2,1)} %bitcast.12, bf16[1,3072,192]{1,2,0:T(8,128)(2,1)} %bitcast.11, bf16[1,3072,192]{1,2,0:T(8,128)(2,1)S(1)} %bitcast.174, bf16[1,3072,192]{1,2,0:T(8,128)(2,1)S(1)} %get-tuple-element.52), kind=kLoop, calls=%fused_computation | loop fusion | flops 7077888 | bytes 9437184 | tf_op jit(solution)/shard_map/stack | solution.py:188
  80.0 1.6 reshape.181
  85.4 1.8 reshape.175.q_ref
  87.1 20.2 %shard_map.150 = (f32[512,768]{1,0:T(8,128)}, f32[512,1]{1,0:T(8,128)}, f32[512,1]{1,0:T(8,128)}) custom-call(s32[1]{0:T(128)} %bitcast.2.valid_ref, bf16[512,768]{1,0:T(8,128)(2,1)} %reshape.175.q_ref, bf16[1,4096,2,768]{3,2,1,0:T(2,128)(2,1)} %cache_ref.3), custom_call_target="tpu_custom_call" | custom-call | flops 6442450944 | bytes 14942208 | tf_op jit(solution)/shard_map/pallas_call | solution.py:88
  107.4 2.2 reshape.176
  115.8 24.2 %all-to-all-start = ((bf16[32,32,784]{2,1,0:T(8,128)(2,1)}), bf16[32,32,784]{2,1,0:T(8,128)(2,1)S(1)}, u32[]{:S(2)}, u32[]{:S(2)}) async-start(bf16[32,32,784]{2,1,0:T(8,128)(2,1)} %maximum_dynamic-update-slice_fusion), calls=%async_computation | async-start | bytes 3670016 | tf_op jit(solution)/shard_map/all_to_all | solution.py:238
  141.2 24.6 %all-to-all-done = bf16[32,32,784]{2,1,0:T(8,128)(2,1)S(1)} async-done(((bf16[32,32,784]{2,1,0:T(8,128)(2,1)}), bf16[32,32,784]{2,1,0:T(8,128)(2,1)S(1)}, u32[]{:S(2)}, u32[]{:S(2)}) %all-to-all-start) | async-done | bytes 1605664 | tf_op jit(solution)/shard_map/all_to_all | solution.py:238
  166.7 3.2 %fusion.16 = f32[32,3072]{1,0:T(8,128)S(1)} fusion(bf16[768,3072]{1,0:T(8,128)(2,1)} %param.18, f32[32,768]{1,0:T(8,128)S(1)} %div.48, f32[32,768]{1,0:T(8,128)S(1)} %reshape.182, f32[32,768]{1,0:T(8,128)S(1)} %mul.283, f32[32,768]{1,0:T(8,128)S(1)} %mul.278, f32[32,784]{1,0:T(8,128)S(1)} %get-tuple-element.51, f32[32,768]{1,0:T(8,128)S(1)} %mul.275, ...), kind=kOutput, calls=%fused_computation.54 | convolution fusion | flops 151166976 | bytes 5799936 | tf_op jit(solution)/shard_map/dot_general | solution.py:285
  171.2 2.4 collective-permute-start.4
  175.0 2.0 collective-permute-done.3
  180.1 4.0 %all-to-all-start.1 = ((bf16[32,8,3072]{2,1,0:T(8,128)(2,1)}), bf16[32,8,3072]{2,1,0:T(8,128)(2,1)S(1)}, u32[]{:S(2)}, u32[]{:S(2)}) async-start(bf16[32,8,3072]{2,1,0:T(8,128)(2,1)} %broadcast_in_dim.43), calls=%async_computation.1 | async-start | bytes 3145728 | tf_op jit(solution)/shard_map/all_to_all | solution.py:302
  184.1 3.4 %fusion.43 = (bf16[4,3072,64]{1,2,0:T(8,128)(2,1)}, bf16[4,3072,64]{1,2,0:T(8,128)(2,1)S(1)}) fusion(bf16[4,3072,192]{1,2,0:T(8,128)(2,1)} %pad_maximum_fusion), kind=kLoop, calls=%fused_computation.129 | loop fusion | bytes 6291456 | tf_op jit(solution)/shard_map/slice | solution.py:310
  187.5 19.7 %all-to-all-done.1 = bf16[32,8,3072]{2,1,0:T(8,128)(2,1)S(1)} async-done(((bf16[32,8,3072]{2,1,0:T(8,128)(2,1)}), bf16[32,8,3072]{2,1,0:T(8,128)(2,1)S(1)}, u32[]{:S(2)}, u32[]{:S(2)}) %all-to-all-start.1) | async-done | bytes 1572896 | tf_op jit(solution)/shard_map/all_to_all | solution.py:302
  207.2 2.0 fusion.4
  209.9 3.3 %fusion.1 = bf16[32,8,3072]{2,1,0:T(8,128)(2,1)} fusion(bf16[4,3072,192]{1,2,0:T(8,128)(2,1)} %pad_maximum_fusion, f32[256,4,64]{0,2,1:T(8,128)S(1)} %bitcast.180, f32[256,4,64]{0,2,1:T(8,128)S(1)} %bitcast.179), kind=kOutput, calls=%fused_computation.3 | convolution fusion | flops 403832832 | bytes 3670016 | tf_op jit(solution)/shard_map/rmj,mfj->rf/dot_general | solution.py:316
  213.1 4.0 %all-to-all-start.2 = ((bf16[32,8,3072]{2,1,0:T(8,128)(2,1)}), bf16[32,8,3072]{2,1,0:T(8,128)(2,1)S(1)}, u32[]{:S(2)}, u32[]{:S(2)}) async-start(bf16[32,8,3072]{2,1,0:T(8,128)(2,1)} %fusion.1), calls=%async_computation.2 | async-start | bytes 3145728 | tf_op jit(solution)/shard_map/all_to_all | solution.py:318
  217.1 23.1 %all-to-all-done.2 = bf16[32,8,3072]{2,1,0:T(8,128)(2,1)S(1)} async-done(((bf16[32,8,3072]{2,1,0:T(8,128)(2,1)}), bf16[32,8,3072]{2,1,0:T(8,128)(2,1)S(1)}, u32[]{:S(2)}, u32[]{:S(2)}) %all-to-all-start.2) | async-done | bytes 1572896 | tf_op jit(solution)/shard_map/all_to_all | solution.py:318
  242.3 2.6 %collective-permute-start.7 = (f32[8,769]{1,0:T(8,128)S(1)}, f32[8,769]{1,0:T(8,128)S(1)}, u32[]{:S(2)}, u32[]{:S(2)}) collective-permute-start(f32[8,769]{1,0:T(8,128)S(1)} %get-tuple-element.74), channel_id=1, source_target_pairs={{0,2},{1,3},{2,0},{3,1},{4,6},{5,7},{6,4},{7,5},{8,10},{9,11},{10,... | collective-permute-start | bytes 73832 | tf_op jit(solution)/shard_map/ppermute | solution.py:347
  245.9 1.8 collective-permute-done.7
  (136 shorter events, 35.2 us)
Async XLA Ops:
  7.2 10.9 %copy-start = (bf16[64,3072]{1,0:T(8,128)(2,1)S(1)}, bf16[64,3072]{1,0:T(8,128)(2,1)}, u32[]{:S(2)}) copy-start(bf16[64,3072]{1,0:T(8,128)(2,1)} %param.22) | copy-start | bytes 1179652
  7.2 10.9 %copy-start.2 = (bf16[3072,64]{0,1:T(8,128)(2,1)S(1)}, bf16[3072,64]{0,1:T(8,128)(2,1)}, u32[]{:S(2)}) copy-start(bf16[3072,64]{0,1:T(8,128)(2,1)} %param.20) | copy-start | bytes 1179652
  7.2 10.9 %copy-start.1 = (bf16[3072,64]{0,1:T(8,128)(2,1)S(1)}, bf16[3072,64]{0,1:T(8,128)(2,1)}, u32[]{:S(2)}) copy-start(bf16[3072,64]{0,1:T(8,128)(2,1)} %param.21) | copy-start | bytes 1179652
  7.2 72.8 %all-gather.2.cloned.1.call-start = ((), (), s32[]{:S(2)}) async-start(), calls=%async_computation.3 | async-start | bytes 1622016 | tf_op jit(solution)/shard_map/all_gather | solution.py:197
  18.1 7.9 %copy-start.14 = (s32[32]{0:T(128)S(1)}, s32[32]{0:T(128)}, u32[]{:S(2)}) copy-start(s32[32]{0:T(128)} %param.25) | copy-start | bytes 388
  19.5 45.1 %collective-permute-start = (bf16[3072,192]{0,1:T(8,128)(2,1)}, bf16[3072,192]{0,1:T(8,128)(2,1)S(1)}, u32[]{:S(2)}, u32[]{:S(2)}) collective-permute-start(bf16[3072,192]{0,1:T(8,128)(2,1)} %get-tuple-element.53), channel_id=1, source_target_pairs={{0,1},{1,2},{2,3},{3,0},{4,5},{5,6},{6,7},{7,4},{8,9},{9,10},{10,1... | collective-permute-start | bytes 3538952 | tf_op jit(solution)/shard_map/ppermute | solution.py:191
  21.5 54.9 %collective-permute-start.1 = (bf16[3072,192]{0,1:T(8,128)(2,1)}, bf16[3072,192]{0,1:T(8,128)(2,1)}, u32[]{:S(2)}, u32[]{:S(2)}) collective-permute-start(bf16[3072,192]{0,1:T(8,128)(2,1)} %get-tuple-element.53), channel_id=1, source_target_pairs={{0,2},{1,3},{2,0},{3,1},{4,6},{5,7},{6,4},{7,5},{8,10},{9,11},{10,... | collective-permute-start | bytes 3538952 | tf_op jit(solution)/shard_map/ppermute | solution.py:191
  25.0 51.3 %collective-permute-start.2 = (bf16[3072,192]{0,1:T(8,128)(2,1)}, bf16[3072,192]{0,1:T(8,128)(2,1)}, u32[]{:S(2)}, u32[]{:S(2)}) collective-permute-start(bf16[3072,192]{0,1:T(8,128)(2,1)} %get-tuple-element.53), channel_id=1, source_target_pairs={{0,3},{1,0},{2,1},{3,2},{4,7},{5,4},{6,5},{7,6},{8,11},{9,8},{10,9... | collective-permute-start | bytes 3538952 | tf_op jit(solution)/shard_map/ppermute | solution.py:191
  107.4 4.2 %copy-start.3 = (f32[512,1]{1,0:T(8,128)S(1)}, f32[512,1]{1,0:T(8,128)}, u32[]{:S(2)}) copy-start(f32[512,1]{1,0:T(8,128)} %get-tuple-element.19) | copy-start | bytes 6148
  115.8 24.5 %copy-start.6 = (bf16[16,8,2,2]{3,2,1,0:T(2,128)(2,1)S(1)}, bf16[16,8,2,2]{3,2,1,0:T(2,128)(2,1)}, u32[]{:S(2)}) copy-start(bf16[16,8,2,2]{3,2,1,0:T(2,128)(2,1)} %copy.164) | copy-start | bytes 3076
  115.8 24.5 %copy-start.7 = (f32[16,2,8]{1,2,0:T(8,128)S(1)}, f32[16,2,8]{1,2,0:T(8,128)}, u32[]{:S(2)}) copy-start(f32[16,2,8]{1,2,0:T(8,128)} %copy.162) | copy-start | bytes 3076
  115.8 24.5 %copy-start.8 = (bf16[16,2,1,8,96]{4,3,1,0,2:T(8,128)(2,1)S(1)}, bf16[16,2,1,8,96]{4,3,1,0,2:T(8,128)(2,1)}, u32[]{:S(2)}) copy-start(bf16[16,2,1,8,96]{4,3,1,0,2:T(8,128)(2,1)} %get-tuple-element.65) | copy-start | bytes 147460
  115.8 50.0 %all-to-all-start = ((bf16[32,32,784]{2,1,0:T(8,128)(2,1)}), bf16[32,32,784]{2,1,0:T(8,128)(2,1)S(1)}, u32[]{:S(2)}, u32[]{:S(2)}) async-start(bf16[32,32,784]{2,1,0:T(8,128)(2,1)} %maximum_dynamic-update-slice_fusion), calls=%async_computation | async-start | bytes 3670016 | tf_op jit(solution)/shard_map/all_to_all | solution.py:238
  166.7 12.0 %copy-start.13 = (f32[3072]{0:T(1024)S(1)}, f32[3072]{0:T(1024)}, u32[]{:S(2)}) copy-start(f32[3072]{0:T(1024)} %param.19) | copy-start | bytes 36868
  170.0 7.0 %collective-permute-start.3 = (f32[8,3072]{1,0:T(8,128)S(1)}, f32[8,3072]{1,0:T(8,128)S(1)}, u32[]{:S(2)}, u32[]{:S(2)}) collective-permute-start(f32[8,3072]{1,0:T(8,128)S(1)} %get-tuple-element.62), channel_id=1, source_target_pairs={{0,1},{1,2},{2,3},{3,0},{4,5},{5,6},{6,7},{7,4},{8,9},{9,10},{10,1... | collective-permute-start | bytes 294920 | tf_op jit(solution)/shard_map/ppermute | solution.py:295
  171.2 6.9 %collective-permute-start.4 = (f32[8,3072]{1,0:T(8,128)S(1)}, f32[8,3072]{1,0:T(8,128)S(1)}, u32[]{:S(2)}, u32[]{:S(2)}) collective-permute-start(f32[8,3072]{1,0:T(8,128)S(1)} %get-tuple-element.64), channel_id=1, source_target_pairs={{0,2},{1,3},{2,0},{3,1},{4,6},{5,7},{6,4},{7,5},{8,10},{9,11},{10,... | collective-permute-start | bytes 294920 | tf_op jit(solution)/shard_map/ppermute | solution.py:295
  173.6 4.9 %collective-permute-start.5 = (f32[8,3072]{1,0:T(8,128)S(1)}, f32[8,3072]{1,0:T(8,128)S(1)}, u32[]{:S(2)}, u32[]{:S(2)}) collective-permute-start(f32[8,3072]{1,0:T(8,128)S(1)} %get-tuple-element.63), channel_id=1, source_target_pairs={{0,3},{1,0},{2,1},{3,2},{4,7},{5,4},{6,5},{7,6},{8,11},{9,8},{10,9... | collective-permute-start | bytes 294920 | tf_op jit(solution)/shard_map/ppermute | solution.py:295
  180.1 27.1 %all-to-all-start.1 = ((bf16[32,8,3072]{2,1,0:T(8,128)(2,1)}), bf16[32,8,3072]{2,1,0:T(8,128)(2,1)S(1)}, u32[]{:S(2)}, u32[]{:S(2)}) async-start(bf16[32,8,3072]{2,1,0:T(8,128)(2,1)} %broadcast_in_dim.43), calls=%async_computation.1 | async-start | bytes 3145728 | tf_op jit(solution)/shard_map/all_to_all | solution.py:302
  213.1 27.1 %all-to-all-start.2 = ((bf16[32,8,3072]{2,1,0:T(8,128)(2,1)}), bf16[32,8,3072]{2,1,0:T(8,128)(2,1)S(1)}, u32[]{:S(2)}, u32[]{:S(2)}) async-start(bf16[32,8,3072]{2,1,0:T(8,128)(2,1)} %fusion.1), calls=%async_computation.2 | async-start | bytes 3145728 | tf_op jit(solution)/shard_map/all_to_all | solution.py:318
  217.1 23.3 %copy-start.11 = (f32[3072]{0:T(1024)S(1)}, f32[3072]{0:T(1024)}, u32[]{:S(2)}) copy-start(f32[3072]{0:T(1024)} %param.24) | copy-start | bytes 36868
  217.1 23.3 %copy-start.12 = (f32[3072]{0:T(1024)S(1)}, f32[3072]{0:T(1024)}, u32[]{:S(2)}) copy-start(f32[3072]{0:T(1024)} %param.23) | copy-start | bytes 36868
  240.7 5.2 %collective-permute-start.6 = (f32[8,769]{1,0:T(8,128)S(1)}, f32[8,769]{1,0:T(8,128)S(1)}, u32[]{:S(2)}, u32[]{:S(2)}) collective-permute-start(f32[8,769]{1,0:T(8,128)S(1)} %get-tuple-element.73), channel_id=1, source_target_pairs={{0,1},{1,2},{2,3},{3,0},{4,5},{5,6},{6,7},{7,4},{8,9},{9,10},{10,1... | collective-permute-start | bytes 73832 | tf_op jit(solution)/shard_map/ppermute | solution.py:347
  242.3 5.4 %collective-permute-start.7 = (f32[8,769]{1,0:T(8,128)S(1)}, f32[8,769]{1,0:T(8,128)S(1)}, u32[]{:S(2)}, u32[]{:S(2)}) collective-permute-start(f32[8,769]{1,0:T(8,128)S(1)} %get-tuple-element.74), channel_id=1, source_target_pairs={{0,2},{1,3},{2,0},{3,1},{4,6},{5,7},{6,4},{7,5},{8,10},{9,11},{10,... | collective-permute-start | bytes 73832 | tf_op jit(solution)/shard_map/ppermute | solution.py:347
  244.9 3.9 %collective-permute-start.8 = (f32[8,769]{1,0:T(8,128)S(1)}, f32[8,769]{1,0:T(8,128)S(1)}, u32[]{:S(2)}, u32[]{:S(2)}) collective-permute-start(f32[8,769]{1,0:T(8,128)S(1)} %get-tuple-element.72), channel_id=1, source_target_pairs={{0,3},{1,0},{2,1},{3,2},{4,7},{5,4},{6,5},{7,6},{8,11},{9,8},{10,9... | collective-permute-start | bytes 73832 | tf_op jit(solution)/shard_map/ppermute | solution.py:347
  (4 other events, 6.9 us)
Sparse Core Ops, SparseCore 0:
  18.2 45.6 all-gather.1

commit v13 on v11

--- a/solution.py
+++ b/solution.py
@@ -192,15 +192,19 @@
     value_new = block[:, :, 2]
     mlp_count = lax.axis_size("mlp")
     weights_cat = jnp.concatenate([w_gate, w_up, jnp.transpose(w_down)], axis=1)
-    weights_all = jnp.stack(
-        [weights_cat]
-        + [
-            lax.ppermute(
-                weights_cat, "mlp", [(m, (m + shift) % mlp_count) for m in range(mlp_count)]
-            )
-            for shift in range(1, mlp_count)
-        ]
-    )
+    ahead = [(m, (m + 1) % mlp_count) for m in range(mlp_count)]
+    behind = [(m, (m + mlp_count - 1) % mlp_count) for m in range(mlp_count)]
+    from_behind = lax.ppermute(weights_cat, "mlp", ahead)
+    from_ahead = lax.ppermute(weights_cat, "mlp", behind)
+    half = weights_cat.shape[1] // 2
+    far = jnp.concatenate(
+        [
+            lax.ppermute(from_behind[:, :half], "mlp", ahead),
+            lax.ppermute(from_ahead[:, half:], "mlp", behind),
+        ],
+        axis=1,
+    )
+    weights_all = jnp.stack([weights_cat, from_behind, far, from_ahead])
     gathered = lax.all_gather(query.reshape(rows_here, width_here), "req", axis=0, tiled=True)
     eye = jnp.eye(heads_here, dtype=jnp.bfloat16)
     tail_diag = jnp.einsum("cthd,hg->chtgd", query, eye).reshape(

time: 258 us -> 279 us (1.081)
  waiting for transfers between devices: 86.1 us -> 98.9 us
  local copies, waits for them, and re-layouts: 27.5 us -> 32.5 us
  other arithmetic: 12.4 us -> 16.9 us
  starting transfers between devices: 31.5 us -> 28.4 us
    ppermute x3 -> x4, waiting for transfers between devices: 11.8 us -> 22.3 us  [the longest x1 22.3 us: per_device(): from_behind = lax.ppermute(weights_cat, 'mlp', ahead)]
    another operation x6 -> x7, other arithmetic: 5.38 us -> 7.13 us  [the longest x3 5.1 us: per_device(): weights_all = jnp.stack([weights_cat, from_behind, far, from_ahead])]
    ppermute x3 -> x4, starting transfers between devices: 6.59 us -> 7.36 us  [the longest x1 3.23 us: per_device(): lax.ppermute(from_ahead[:, half:], 'mlp', behind)]
  transfers between devices with their start and end apart: 13 -> 14, of which waited for: 10 -> 9; matrix products, arithmetic and copies ran while one was open for 5% -> 8% of each run, Pallas kernels for 12% -> 11%
where the time goes in v13:
time: 279 us; the launch traced here: 278 us
  waiting for transfers between devices  98.9 us (35%)
  Pallas kernels  68 us (24%)
  local copies, waits for them, and re-layouts  32.5 us (12%)
  starting transfers between devices  28.4 us (10%)
  between operations  22 us (8%)
  other arithmetic  16.9 us (6%)
  matrix products  11.3 us (4%)
    pallas_call x1, Pallas kernels, prompt_attention(): pl.pallas_call(functools.partial(prompt_kernel, block_len, score_scale),...  37.2 us
    pallas_call x1, Pallas kernels, tail_attention(): pl.pallas_call(functools.partial(tail_kernel, score_scale), grid_spec=spe...  30.8 us
    all_to_all x1, waiting for transfers between devices, per_device(): lax.all_to_all(outgoing, 'req', split_axis=0, concat_axis=0, tiled=True)  24.8 us
    all_to_all x1, waiting for transfers between devices, per_device(): lax.all_to_all(down_sum.astype(jnp.bfloat16).reshape(req_count, share, wi...  23.1 us
    ppermute x1, waiting for transfers between devices, per_device(): from_behind = lax.ppermute(weights_cat, 'mlp', ahead)  22.3 us
    all_to_all x1, waiting for transfers between devices, per_device(): lax.all_to_all(jnp.broadcast_to(normed_share[None], (req_count,) + normed...  19.7 us
    all_to_all x1, starting transfers between devices, per_device(): lax.all_to_all(outgoing, 'req', split_axis=0, concat_axis=0, tiled=True)  5.91 us
  transfers between devices with their start and end apart: 14, of which 9 were waited for; matrix products, arithmetic and copies ran while one was open for 8% of the time, Pallas kernels for 11%

profile of v13, /device:TPU:0, one launch (start us, length us, event | category | flops | bytes accessed | tf_op | source)
XLA Modules:
  0.0 278.0 jit_solution(5690598605343989881)
XLA Ops:
  21.3 2.0 collective-permute-start
  23.3 2.1 collective-permute-start.2
  26.5 1.9 subtract_convert_fusion
  29.2 22.3 %collective-permute-done = bf16[3072,192]{0,1:T(8,128)(2,1)S(1)} collective-permute-done((bf16[3072,192]{0,1:T(8,128)(2,1)}, bf16[3072,192]{0,1:T(8,128)(2,1)S(1)}, u32[]{:S(2)}, u32[]{:S(2)}) %collective-permute-start) | collective-permute-done | bytes 1179680 | tf_op jit(solution)/shard_map/ppermute | solution.py:197
  53.3 3.2 %collective-permute-start.3 = (bf16[3072,96]{0,1:T(8,128)(2,1)}, bf16[3072,96]{0,1:T(8,128)(2,1)}, u32[]{:S(2)}, u32[]{:S(2)}) collective-permute-start(bf16[3072,96]{0,1:T(8,128)(2,1)} %slice.149), channel_id=1, source_target_pairs={{0,3},{1,0},{2,1},{3,2},{4,7},{5,4},{6,5},{7,6},{8,11},{9,8},{10,9... | collective-permute-start | bytes 1769480 | tf_op jit(solution)/shard_map/ppermute | solution.py:203
  60.0 2.3 reshape.172.q_ref
  62.3 1.9 fusion.15
  67.3 30.8 %shard_map.149 = (f32[16,16,768]{2,1,0:T(8,128)}, f32[16,16,1]{2,1,0:T(8,128)}, f32[16,16,1]{2,1,0:T(8,128)}) custom-call(s32[16]{0:T(128)} %get-tuple-element.39.lens_ref, bf16[16,16,768]{2,1,0:T(8,128)(2,1)} %reshape.172.q_ref, bf16[16,256,2,768]{3,2,1,0:T(2,128)(2,1)} %cache_ref.2), custom_call_target="tpu_custom_call" | custom-call | flops 201326592 | bytes 13762560 | tf_op jit(solution)/shard_map/pallas_call | solution.py:144
  100.1 2.5 pad_maximum_fusion
  109.8 37.2 %shard_map.150 = (f32[512,768]{1,0:T(8,128)}, f32[512,1]{1,0:T(8,128)}, f32[512,1]{1,0:T(8,128)}) custom-call(s32[1]{0:T(128)} %bitcast.2.valid_ref, bf16[512,768]{1,0:T(8,128)(2,1)} %reshape.175.q_ref, bf16[1,4096,2,768]{3,2,1,0:T(2,128)(2,1)} %cache_ref.3), custom_call_target="tpu_custom_call" | custom-call | flops 6442450944 | bytes 14942208 | tf_op jit(solution)/shard_map/pallas_call | solution.py:95
  146.9 2.2 reshape.176
  155.3 5.9 %all-to-all-start = ((bf16[32,32,784]{2,1,0:T(8,128)(2,1)}), bf16[32,32,784]{2,1,0:T(8,128)(2,1)S(1)}, u32[]{:S(2)}, u32[]{:S(2)}) async-start(bf16[32,32,784]{2,1,0:T(8,128)(2,1)} %maximum_dynamic-update-slice_fusion), calls=%async_computation | async-start | bytes 3670016 | tf_op jit(solution)/shard_map/all_to_all | solution.py:249
  162.5 24.8 %all-to-all-done = bf16[32,32,784]{2,1,0:T(8,128)(2,1)S(1)} async-done(((bf16[32,32,784]{2,1,0:T(8,128)(2,1)}), bf16[32,32,784]{2,1,0:T(8,128)(2,1)S(1)}, u32[]{:S(2)}, u32[]{:S(2)}) %all-to-all-start) | async-done | bytes 1605664 | tf_op jit(solution)/shard_map/all_to_all | solution.py:249
  188.2 3.2 %fusion.16 = f32[32,3072]{1,0:T(8,128)S(1)} fusion(bf16[768,3072]{1,0:T(8,128)(2,1)} %param.18, f32[32,768]{1,0:T(8,128)S(1)} %div.48, f32[32,768]{1,0:T(8,128)S(1)} %reshape.182, f32[32,768]{1,0:T(8,128)S(1)} %mul.283, f32[32,768]{1,0:T(8,128)S(1)} %mul.278, f32[32,784]{1,0:T(8,128)S(1)} %get-tuple-element.51, f32[32,768]{1,0:T(8,128)S(1)} %mul.275, ...), kind=kOutput, calls=%fused_computation.55 | convolution fusion | flops 151166976 | bytes 5799936 | tf_op jit(solution)/shard_map/dot_general | solution.py:296
  191.6 2.0 collective-permute-start.5
  194.9 4.5 %collective-permute-done.4 = f32[8,3072]{1,0:T(8,128)S(1)} collective-permute-done((f32[8,3072]{1,0:T(8,128)S(1)}, f32[8,3072]{1,0:T(8,128)S(1)}, u32[]{:S(2)}, u32[]{:S(2)}) %collective-permute-start.4) | collective-permute-done | bytes 98336 | tf_op jit(solution)/shard_map/ppermute | solution.py:306
  201.6 4.0 %all-to-all-start.1 = ((bf16[32,8,3072]{2,1,0:T(8,128)(2,1)}), bf16[32,8,3072]{2,1,0:T(8,128)(2,1)S(1)}, u32[]{:S(2)}, u32[]{:S(2)}) async-start(bf16[32,8,3072]{2,1,0:T(8,128)(2,1)} %broadcast_in_dim.43), calls=%async_computation.1 | async-start | bytes 3145728 | tf_op jit(solution)/shard_map/all_to_all | solution.py:313
  205.6 3.4 %fusion.43 = (bf16[4,3072,64]{1,2,0:T(8,128)(2,1)}, bf16[4,3072,64]{1,2,0:T(8,128)(2,1)S(1)}) fusion(bf16[4,3072,192]{1,2,0:T(8,128)(2,1)} %pad_maximum_fusion), kind=kLoop, calls=%fused_computation.130 | loop fusion | bytes 6291456 | tf_op jit(solution)/shard_map/slice | solution.py:321
  208.9 19.7 %all-to-all-done.1 = bf16[32,8,3072]{2,1,0:T(8,128)(2,1)S(1)} async-done(((bf16[32,8,3072]{2,1,0:T(8,128)(2,1)}), bf16[32,8,3072]{2,1,0:T(8,128)(2,1)S(1)}, u32[]{:S(2)}, u32[]{:S(2)}) %all-to-all-start.1) | async-done | bytes 1572896 | tf_op jit(solution)/shard_map/all_to_all | solution.py:313
  228.7 2.0 fusion.4
  231.3 3.3 %fusion.1 = bf16[32,8,3072]{2,1,0:T(8,128)(2,1)} fusion(bf16[4,3072,192]{1,2,0:T(8,128)(2,1)} %pad_maximum_fusion, f32[256,4,64]{0,2,1:T(8,128)S(1)} %bitcast.182, f32[256,4,64]{0,2,1:T(8,128)S(1)} %bitcast.181), kind=kOutput, calls=%fused_computation.3 | convolution fusion | flops 403832832 | bytes 3670016 | tf_op jit(solution)/shard_map/rmj,mfj->rf/dot_general | solution.py:327
  234.6 4.0 %all-to-all-start.2 = ((bf16[32,8,3072]{2,1,0:T(8,128)(2,1)}), bf16[32,8,3072]{2,1,0:T(8,128)(2,1)S(1)}, u32[]{:S(2)}, u32[]{:S(2)}) async-start(bf16[32,8,3072]{2,1,0:T(8,128)(2,1)} %fusion.1), calls=%async_computation.2 | async-start | bytes 3145728 | tf_op jit(solution)/shard_map/all_to_all | solution.py:329
  238.6 23.1 %all-to-all-done.2 = bf16[32,8,3072]{2,1,0:T(8,128)(2,1)S(1)} async-done(((bf16[32,8,3072]{2,1,0:T(8,128)(2,1)}), bf16[32,8,3072]{2,1,0:T(8,128)(2,1)S(1)}, u32[]{:S(2)}, u32[]{:S(2)}) %all-to-all-start.2) | async-done | bytes 1572896 | tf_op jit(solution)/shard_map/all_to_all | solution.py:329
  262.8 3.2 %collective-permute-start.8 = (f32[8,769]{1,0:T(8,128)S(1)}, f32[8,769]{1,0:T(8,128)S(1)}, u32[]{:S(2)}, u32[]{:S(2)}) collective-permute-start(f32[8,769]{1,0:T(8,128)S(1)} %get-tuple-element.74), channel_id=1, source_target_pairs={{0,2},{1,3},{2,0},{3,1},{4,6},{5,7},{6,4},{7,5},{8,10},{9,11},{10,... | collective-permute-start | bytes 73832 | tf_op jit(solution)/shard_map/ppermute | solution.py:358
  (167 shorter events, 44.6 us)
Async XLA Ops:
  7.2 12.8 %copy-start.2 = (bf16[64,3072]{1,0:T(8,128)(2,1)S(1)}, bf16[64,3072]{1,0:T(8,128)(2,1)}, u32[]{:S(2)}) copy-start(bf16[64,3072]{1,0:T(8,128)(2,1)} %param.22) | copy-start | bytes 1179652
  7.2 12.8 %copy-start.4 = (bf16[3072,64]{0,1:T(8,128)(2,1)S(1)}, bf16[3072,64]{0,1:T(8,128)(2,1)}, u32[]{:S(2)}) copy-start(bf16[3072,64]{0,1:T(8,128)(2,1)} %param.20) | copy-start | bytes 1179652
  7.2 12.8 %copy-start.3 = (bf16[3072,64]{0,1:T(8,128)(2,1)S(1)}, bf16[3072,64]{0,1:T(8,128)(2,1)}, u32[]{:S(2)}) copy-start(bf16[3072,64]{0,1:T(8,128)(2,1)} %param.21) | copy-start | bytes 1179652
  7.2 95.4 %all-gather.2.cloned.1.call-start = ((), (), s32[]{:S(2)}) async-start(), calls=%async_computation.3 | async-start | bytes 1622016 | tf_op jit(solution)/shard_map/all_gather | solution.py:208
  21.3 30.3 %collective-permute-start = (bf16[3072,192]{0,1:T(8,128)(2,1)}, bf16[3072,192]{0,1:T(8,128)(2,1)S(1)}, u32[]{:S(2)}, u32[]{:S(2)}) collective-permute-start(bf16[3072,192]{0,1:T(8,128)(2,1)} %get-tuple-element.53), channel_id=1, source_target_pairs={{0,1},{1,2},{2,3},{3,0},{4,5},{5,6},{6,7},{7,4},{8,9},{9,10},{10,1... | collective-permute-start | bytes 3538952 | tf_op jit(solution)/shard_map/ppermute | solution.py:197
  23.3 29.2 %collective-permute-start.2 = (bf16[3072,192]{0,1:T(8,128)(2,1)}, bf16[3072,192]{0,1:T(8,128)(2,1)S(1)}, u32[]{:S(2)}, u32[]{:S(2)}) collective-permute-start(bf16[3072,192]{0,1:T(8,128)(2,1)} %get-tuple-element.53), channel_id=1, source_target_pairs={{0,3},{1,0},{2,1},{3,2},{4,7},{5,4},{6,5},{7,6},{8,11},{9,8},{10,9... | collective-permute-start | bytes 3538952 | tf_op jit(solution)/shard_map/ppermute | solution.py:198
  25.4 27.9 %copy-start.20 = (bf16[8,8]{1,0:T(8,128)(2,1)}, bf16[8,8]{1,0:T(8,128)(2,1)S(1)}, u32[]{:S(2)}) copy-start(bf16[8,8]{1,0:T(8,128)(2,1)S(1)} %fusion.37) | copy-start | bytes 388
  28.3 28.2 %copy-start.27 = (s32[32]{0:T(128)S(1)}, s32[32]{0:T(128)}, u32[]{:S(2)}) copy-start(s32[32]{0:T(128)} %param.25) | copy-start | bytes 388
  52.4 46.3 %collective-permute-start.1 = (bf16[3072,96]{0,1:T(8,128)(2,1)}, bf16[3072,96]{0,1:T(8,128)(2,1)}, u32[]{:S(2)}, u32[]{:S(2)}) collective-permute-start(bf16[3072,96]{0,1:T(8,128)(2,1)} %slice.148), channel_id=1, source_target_pairs={{0,1},{1,2},{2,3},{3,0},{4,5},{5,6},{6,7},{7,4},{8,9},{9,10},{10,1... | collective-permute-start | bytes 1769480 | tf_op jit(solution)/shard_map/ppermute | solution.py:202
  53.3 45.5 %collective-permute-start.3 = (bf16[3072,96]{0,1:T(8,128)(2,1)}, bf16[3072,96]{0,1:T(8,128)(2,1)}, u32[]{:S(2)}, u32[]{:S(2)}) collective-permute-start(bf16[3072,96]{0,1:T(8,128)(2,1)} %slice.149), channel_id=1, source_target_pairs={{0,3},{1,0},{2,1},{3,2},{4,7},{5,4},{6,5},{7,6},{8,11},{9,8},{10,9... | collective-permute-start | bytes 1769480 | tf_op jit(solution)/shard_map/ppermute | solution.py:203
  155.3 6.2 %copy-start.15 = (f32[16,2,8]{1,2,0:T(8,128)S(1)}, f32[16,2,8]{1,2,0:T(8,128)}, u32[]{:S(2)}) copy-start(f32[16,2,8]{1,2,0:T(8,128)} %copy.162) | copy-start | bytes 3076
  155.3 6.2 %copy-start.16 = (bf16[16,2,1,8,96]{4,3,1,0,2:T(8,128)(2,1)S(1)}, bf16[16,2,1,8,96]{4,3,1,0,2:T(8,128)(2,1)}, u32[]{:S(2)}) copy-start(bf16[16,2,1,8,96]{4,3,1,0,2:T(8,128)(2,1)} %get-tuple-element.65) | copy-start | bytes 147460
  155.3 31.9 %all-to-all-start = ((bf16[32,32,784]{2,1,0:T(8,128)(2,1)}), bf16[32,32,784]{2,1,0:T(8,128)(2,1)S(1)}, u32[]{:S(2)}, u32[]{:S(2)}) async-start(bf16[32,32,784]{2,1,0:T(8,128)(2,1)} %maximum_dynamic-update-slice_fusion), calls=%async_computation | async-start | bytes 3670016 | tf_op jit(solution)/shard_map/all_to_all | solution.py:249
  188.2 11.9 %copy-start.24 = (f32[3072]{0:T(1024)S(1)}, f32[3072]{0:T(1024)}, u32[]{:S(2)}) copy-start(f32[3072]{0:T(1024)} %param.19) | copy-start | bytes 36868
  191.5 7.8 %collective-permute-start.4 = (f32[8,3072]{1,0:T(8,128)S(1)}, f32[8,3072]{1,0:T(8,128)S(1)}, u32[]{:S(2)}, u32[]{:S(2)}) collective-permute-start(f32[8,3072]{1,0:T(8,128)S(1)} %get-tuple-element.62), channel_id=1, source_target_pairs={{0,1},{1,2},{2,3},{3,0},{4,5},{5,6},{6,7},{7,4},{8,9},{9,10},{10,1... | collective-permute-start | bytes 294920 | tf_op jit(solution)/shard_map/ppermute | solution.py:306
  191.6 7.7 %collective-permute-start.5 = (f32[8,3072]{1,0:T(8,128)S(1)}, f32[8,3072]{1,0:T(8,128)S(1)}, u32[]{:S(2)}, u32[]{:S(2)}) collective-permute-start(f32[8,3072]{1,0:T(8,128)S(1)} %get-tuple-element.64), channel_id=1, source_target_pairs={{0,2},{1,3},{2,0},{3,1},{4,6},{5,7},{6,4},{7,5},{8,10},{9,11},{10,... | collective-permute-start | bytes 294920 | tf_op jit(solution)/shard_map/ppermute | solution.py:306
  193.6 6.4 %collective-permute-start.6 = (f32[8,3072]{1,0:T(8,128)S(1)}, f32[8,3072]{1,0:T(8,128)S(1)}, u32[]{:S(2)}, u32[]{:S(2)}) collective-permute-start(f32[8,3072]{1,0:T(8,128)S(1)} %get-tuple-element.63), channel_id=1, source_target_pairs={{0,3},{1,0},{2,1},{3,2},{4,7},{5,4},{6,5},{7,6},{8,11},{9,8},{10,9... | collective-permute-start | bytes 294920 | tf_op jit(solution)/shard_map/ppermute | solution.py:306
  201.6 27.1 %all-to-all-start.1 = ((bf16[32,8,3072]{2,1,0:T(8,128)(2,1)}), bf16[32,8,3072]{2,1,0:T(8,128)(2,1)S(1)}, u32[]{:S(2)}, u32[]{:S(2)}) async-start(bf16[32,8,3072]{2,1,0:T(8,128)(2,1)} %broadcast_in_dim.43), calls=%async_computation.1 | async-start | bytes 3145728 | tf_op jit(solution)/shard_map/all_to_all | solution.py:313
  234.6 27.1 %all-to-all-start.2 = ((bf16[32,8,3072]{2,1,0:T(8,128)(2,1)}), bf16[32,8,3072]{2,1,0:T(8,128)(2,1)S(1)}, u32[]{:S(2)}, u32[]{:S(2)}) async-start(bf16[32,8,3072]{2,1,0:T(8,128)(2,1)} %fusion.1), calls=%async_computation.2 | async-start | bytes 3145728 | tf_op jit(solution)/shard_map/all_to_all | solution.py:329
  238.6 23.3 %copy-start.22 = (f32[3072]{0:T(1024)S(1)}, f32[3072]{0:T(1024)}, u32[]{:S(2)}) copy-start(f32[3072]{0:T(1024)} %param.24) | copy-start | bytes 36868
  238.6 23.3 %copy-start.23 = (f32[3072]{0:T(1024)S(1)}, f32[3072]{0:T(1024)}, u32[]{:S(2)}) copy-start(f32[3072]{0:T(1024)} %param.23) | copy-start | bytes 36868
  262.2 5.2 %collective-permute-start.7 = (f32[8,769]{1,0:T(8,128)S(1)}, f32[8,769]{1,0:T(8,128)S(1)}, u32[]{:S(2)}, u32[]{:S(2)}) collective-permute-start(f32[8,769]{1,0:T(8,128)S(1)} %get-tuple-element.73), channel_id=1, source_target_pairs={{0,1},{1,2},{2,3},{3,0},{4,5},{5,6},{6,7},{7,4},{8,9},{9,10},{10,1... | collective-permute-start | bytes 73832 | tf_op jit(solution)/shard_map/ppermute | solution.py:358
  262.8 5.4 %collective-permute-start.8 = (f32[8,769]{1,0:T(8,128)S(1)}, f32[8,769]{1,0:T(8,128)S(1)}, u32[]{:S(2)}, u32[]{:S(2)}) collective-permute-start(f32[8,769]{1,0:T(8,128)S(1)} %get-tuple-element.74), channel_id=1, source_target_pairs={{0,2},{1,3},{2,0},{3,1},{4,6},{5,7},{6,4},{7,5},{8,10},{9,11},{10,... | collective-permute-start | bytes 73832 | tf_op jit(solution)/shard_map/ppermute | solution.py:358
  266.1 3.9 %collective-permute-start.9 = (f32[8,769]{1,0:T(8,128)S(1)}, f32[8,769]{1,0:T(8,128)S(1)}, u32[]{:S(2)}, u32[]{:S(2)}) collective-permute-start(f32[8,769]{1,0:T(8,128)S(1)} %get-tuple-element.72), channel_id=1, source_target_pairs={{0,3},{1,0},{2,1},{3,2},{4,7},{5,4},{6,5},{7,6},{8,11},{9,8},{10,9... | collective-permute-start | bytes 73832 | tf_op jit(solution)/shard_map/ppermute | solution.py:358
  (18 other events, 45.2 us)
Sparse Core Ops, SparseCore 0:
  20.0 45.5 all-gather.1

commit v14 on v11

--- a/solution.py
+++ b/solution.py
@@ -191,16 +191,10 @@
     key_new = rotary(block[:, :, 1].astype(jnp.float32), position).astype(jnp.bfloat16)
     value_new = block[:, :, 2]
     mlp_count = lax.axis_size("mlp")
-    weights_cat = jnp.concatenate([w_gate, w_up, jnp.transpose(w_down)], axis=1)
-    weights_all = jnp.stack(
-        [weights_cat]
-        + [
-            lax.ppermute(
-                weights_cat, "mlp", [(m, (m + shift) % mlp_count) for m in range(mlp_count)]
-            )
-            for shift in range(1, mlp_count)
-        ]
-    )
+    weights_cat = jnp.concatenate([w_gate, w_up], axis=1)
+    rings = [[(m, (m + shift) % mlp_count) for m in range(mlp_count)] for shift in range(1, mlp_count)]
+    weights_all = jnp.stack([weights_cat] + [lax.ppermute(weights_cat, "mlp", ring) for ring in rings])
+    down_w = jnp.stack([w_down] + [lax.ppermute(w_down, "mlp", ring) for ring in rings])
     gathered = lax.all_gather(query.reshape(rows_here, width_here), "req", axis=0, tiled=True)
     eye = jnp.eye(heads_here, dtype=jnp.bfloat16)
     tail_diag = jnp.einsum("cthd,hg->chtgd", query, eye).reshape(
@@ -316,11 +310,10 @@
     hidden_here = w_gate.shape[1]
     gate_w = weights_all[:, :, :hidden_here]
     up_w = weights_all[:, :, hidden_here : 2 * hidden_here]
-    down_w = weights_all[:, :, 2 * hidden_here :]
     gate = jnp.einsum("rk,mkj->rmj", piece, gate_w, preferred_element_type=jnp.float32)
     upper = jnp.einsum("rk,mkj->rmj", piece, up_w, preferred_element_type=jnp.float32)
     hidden_all = (jax.nn.silu(gate) * upper).astype(jnp.bfloat16)
-    down_sum = jnp.einsum("rmj,mfj->rf", hidden_all, down_w, preferred_element_type=jnp.float32)
+    down_sum = jnp.einsum("rmj,mjf->rf", hidden_all, down_w, preferred_element_type=jnp.float32)
     row_sums = jnp.sum(
         lax.all_to_all(
             down_sum.astype(jnp.bfloat16).reshape(req_count, share, width),

time: 258 us -> 242 us (0.938)
  waiting for transfers between devices: 86.1 us -> 71.6 us
    ppermute x3 -> x6, waiting for transfers between devices: 11.8 us -> 0.02 us  [the longest x3 0.01 us: per_device(): lax.ppermute(weights_cat, 'mlp', ring)]
    all_to_all x1, waiting for transfers between devices: 19.7 us -> 15.5 us  [per_device(): lax.all_to_all(jnp.broadcast_to(normed_share[None], (req_count,) + normed...]
    ppermute x3 -> x6, starting transfers between devices: 6.59 us -> 10.3 us  [the longest x3 6.06 us: per_device(): lax.ppermute(weights_cat, 'mlp', ring)]
    another operation x6 -> x5, other arithmetic: 5.38 us -> 3.2 us  [the longest x1 2.83 us: per_device(): jnp.stack([weights_cat] + [lax.ppermute(weights_cat, 'mlp', ring) for rin...]
  transfers between devices with their start and end apart: 13 -> 16, of which waited for: 10 -> 9; matrix products, arithmetic and copies ran while one was open for 5% -> 5% of each run, Pallas kernels for 12% -> 13%
where the time goes in v14:
time: 242 us; the launch traced here: 241 us
  waiting for transfers between devices  71.6 us (30%)
  Pallas kernels  67.7 us (28%)
  starting transfers between devices  32.6 us (13%)
  local copies, waits for them, and re-layouts  27.4 us (11%)
  between operations  21.6 us (9%)
  other arithmetic  10.2 us (4%)
  matrix products  9.7 us (4%)
    pallas_call x1, Pallas kernels, prompt_attention(): pl.pallas_call(functools.partial(prompt_kernel, block_len, score_scale),...  36.9 us
    pallas_call x1, Pallas kernels, tail_attention(): pl.pallas_call(functools.partial(tail_kernel, score_scale), grid_spec=spe...  30.8 us
    all_to_all x1, waiting for transfers between devices, per_device(): lax.all_to_all(outgoing, 'req', split_axis=0, concat_axis=0, tiled=True)  24.8 us
    all_to_all x1, waiting for transfers between devices, per_device(): lax.all_to_all(down_sum.astype(jnp.bfloat16).reshape(req_count, share, wi...  23.1 us
    all_to_all x1, waiting for transfers between devices, per_device(): lax.all_to_all(jnp.broadcast_to(normed_share[None], (req_count,) + normed...  15.5 us
    ppermute x3, starting transfers between devices, per_device(): lax.ppermute(weights_cat, 'mlp', ring)  6.06 us
    all_to_all x1, starting transfers between devices, per_device(): lax.all_to_all(outgoing, 'req', split_axis=0, concat_axis=0, tiled=True)  6.05 us
  transfers between devices with their start and end apart: 16, of which 9 were waited for; matrix products, arithmetic and copies ran while one was open for 5% of the time, Pallas kernels for 13%

profile of v14, /device:TPU:0, one launch (start us, length us, event | category | flops | bytes accessed | tf_op | source)
XLA Modules:
  0.0 240.7 jit_solution(6482706172532986059)
XLA Ops:
  11.2 1.4 fusion.53
  12.6 1.9 broadcast_add_fusion
  18.1 4.0 %collective-permute-start.1 = (bf16[3072,128]{0,1:T(8,128)(2,1)S(1)}, bf16[3072,128]{0,1:T(8,128)(2,1)S(1)}, u32[]{:S(2)}, u32[]{:S(2)}) collective-permute-start(bf16[3072,128]{0,1:T(8,128)(2,1)S(1)} %constant_dynamic-update-slice_fusion), channel_id=1, source_target_pairs={{0,2},{1,3},{2,0},{3,1},{4,6},{5,7},{6,4},{7,5},{8,10},{9,11},{10,... | collective-permute-start | bytes 2359304 | tf_op jit(solution)/shard_map/ppermute | solution.py:196
  31.5 30.8 %shard_map.149 = (f32[16,16,768]{2,1,0:T(8,128)}, f32[16,16,1]{2,1,0:T(8,128)}, f32[16,16,1]{2,1,0:T(8,128)}) custom-call(s32[16]{0:T(128)} %get-tuple-element.39.lens_ref, bf16[16,16,768]{2,1,0:T(8,128)(2,1)} %reshape.172.q_ref, bf16[16,256,2,768]{3,2,1,0:T(2,128)(2,1)} %cache_ref.2), custom_call_target="tpu_custom_call" | custom-call | flops 201326592 | bytes 13762560 | tf_op jit(solution)/shard_map/pallas_call | solution.py:144
  62.4 2.8 %pad_maximum_fusion = bf16[4,3072,128]{1,2,0:T(8,128)(2,1)} fusion(bf16[1,3072,128]{1,2,0:T(8,128)(2,1)S(1)} %bitcast.180, bf16[1,3072,128]{1,2,0:T(8,128)(2,1)S(1)} %bitcast.179, bf16[1,3072,128]{1,2,0:T(8,128)(2,1)} %bitcast.9, bf16[1,3072,128]{1,2,0:T(8,128)(2,1)S(1)} %bitcast.176), kind=kLoop, calls=%fused_computation.3 | loop fusion | flops 4718592 | bytes 6291456 | tf_op jit(solution)/shard_map/stack | solution.py:196
  65.2 1.6 reshape.181
  70.6 1.8 reshape.175.q_ref
  72.3 36.9 %shard_map.150 = (f32[512,768]{1,0:T(8,128)}, f32[512,1]{1,0:T(8,128)}, f32[512,1]{1,0:T(8,128)}) custom-call(s32[1]{0:T(128)} %bitcast.2.valid_ref, bf16[512,768]{1,0:T(8,128)(2,1)} %reshape.175.q_ref, bf16[1,4096,2,768]{3,2,1,0:T(2,128)(2,1)} %cache_ref.3), custom_call_target="tpu_custom_call" | custom-call | flops 6442450944 | bytes 14942208 | tf_op jit(solution)/shard_map/pallas_call | solution.py:95
  109.3 2.2 reshape.176
  117.6 6.1 %all-to-all-start = ((bf16[32,32,784]{2,1,0:T(8,128)(2,1)}), bf16[32,32,784]{2,1,0:T(8,128)(2,1)S(1)}, u32[]{:S(2)}, u32[]{:S(2)}) async-start(bf16[32,32,784]{2,1,0:T(8,128)(2,1)} %maximum_dynamic-update-slice_fusion), calls=%async_computation | async-start | bytes 3670016 | tf_op jit(solution)/shard_map/all_to_all | solution.py:239
  125.0 24.8 %all-to-all-done = bf16[32,32,784]{2,1,0:T(8,128)(2,1)S(1)} async-done(((bf16[32,32,784]{2,1,0:T(8,128)(2,1)}), bf16[32,32,784]{2,1,0:T(8,128)(2,1)S(1)}, u32[]{:S(2)}, u32[]{:S(2)}) %all-to-all-start) | async-done | bytes 1605664 | tf_op jit(solution)/shard_map/all_to_all | solution.py:239
  150.7 3.2 %fusion.22 = f32[32,3072]{1,0:T(8,128)S(1)} fusion(bf16[768,3072]{1,0:T(8,128)(2,1)} %param.18, f32[32,768]{1,0:T(8,128)S(1)} %div.48, f32[32,768]{1,0:T(8,128)S(1)} %reshape.182, f32[32,768]{1,0:T(8,128)S(1)} %mul.283, f32[32,768]{1,0:T(8,128)S(1)} %mul.278, f32[32,784]{1,0:T(8,128)S(1)} %get-tuple-element.51, f32[32,768]{1,0:T(8,128)S(1)} %mul.275, ...), kind=kOutput, calls=%fused_computation.59 | convolution fusion | flops 151166976 | bytes 5799936 | tf_op jit(solution)/shard_map/dot_general | solution.py:286
  155.1 2.4 collective-permute-start.4
  158.0 2.9 %collective-permute-done.3 = f32[8,3072]{1,0:T(8,128)S(1)} collective-permute-done((f32[8,3072]{1,0:T(8,128)S(1)}, f32[8,3072]{1,0:T(8,128)S(1)}, u32[]{:S(2)}, u32[]{:S(2)}) %collective-permute-start.3) | collective-permute-done | bytes 98336 | tf_op jit(solution)/shard_map/ppermute | solution.py:296
  164.0 4.0 %all-to-all-start.1 = ((bf16[32,8,3072]{2,1,0:T(8,128)(2,1)}), bf16[32,8,3072]{2,1,0:T(8,128)(2,1)S(1)}, u32[]{:S(2)}, u32[]{:S(2)}) async-start(bf16[32,8,3072]{2,1,0:T(8,128)(2,1)} %broadcast_in_dim.43), calls=%async_computation.1 | async-start | bytes 3145728 | tf_op jit(solution)/shard_map/all_to_all | solution.py:303
  168.9 3.3 %collective-permute-start.7 = (bf16[64,3072]{1,0:T(8,128)(2,1)}, bf16[64,3072]{1,0:T(8,128)(2,1)}, u32[]{:S(2)}, u32[]{:S(2)}) collective-permute-start(bf16[64,3072]{1,0:T(8,128)(2,1)} %param.22), channel_id=1, source_target_pairs={{0,2},{1,3},{2,0},{3,1},{4,6},{5,7},{6,4},{7,5},{8,10},{9,11},{10,... | collective-permute-start | bytes 1179656 | tf_op jit(solution)/shard_map/ppermute | solution.py:197
  172.2 3.4 %fusion.49 = (bf16[4,3072,64]{1,2,0:T(8,128)(2,1)}, bf16[4,3072,64]{1,2,0:T(8,128)(2,1)S(1)}) fusion(bf16[4,3072,128]{1,2,0:T(8,128)(2,1)} %pad_maximum_fusion), kind=kLoop, calls=%fused_computation.136 | loop fusion | bytes 6291456 | tf_op jit(solution)/shard_map/slice | solution.py:311
  175.5 15.5 %all-to-all-done.1 = bf16[32,8,3072]{2,1,0:T(8,128)(2,1)S(1)} async-done(((bf16[32,8,3072]{2,1,0:T(8,128)(2,1)}), bf16[32,8,3072]{2,1,0:T(8,128)(2,1)S(1)}, u32[]{:S(2)}, u32[]{:S(2)}) %all-to-all-start.1) | async-done | bytes 1572896 | tf_op jit(solution)/shard_map/all_to_all | solution.py:303
  191.1 2.0 fusion.11
  193.8 3.2 %fusion.1 = bf16[32,8,3072]{2,1,0:T(8,128)(2,1)} fusion(bf16[1,64,3072]{2,1,0:T(8,128)(2,1)} %bitcast.61, bf16[1,64,3072]{2,1,0:T(8,128)(2,1)} %bitcast.60, bf16[1,64,3072]{2,1,0:T(8,128)(2,1)} %bitcast.59, bf16[1,64,3072]{2,1,0:T(8,128)(2,1)} %bitcast.58, f32[256,4,64]{0,2,1:T(8,128)S(1)} %bitcast.183, f32[256,4,64]{0,2,1:T(8,128)S(1)} %bitcast.182), kind=kOutput, calls=%fused_computation.2 | convolution fusion | flops 406192128 | bytes 3670016 | tf_op jit(solution)/shard_map/rmj,mjf->rf/dot_general | solution.py:316
  197.0 4.0 %all-to-all-start.2 = ((bf16[32,8,3072]{2,1,0:T(8,128)(2,1)}), bf16[32,8,3072]{2,1,0:T(8,128)(2,1)S(1)}, u32[]{:S(2)}, u32[]{:S(2)}) async-start(bf16[32,8,3072]{2,1,0:T(8,128)(2,1)} %fusion.1), calls=%async_computation.2 | async-start | bytes 3145728 | tf_op jit(solution)/shard_map/all_to_all | solution.py:318
  201.0 23.1 %all-to-all-done.2 = bf16[32,8,3072]{2,1,0:T(8,128)(2,1)S(1)} async-done(((bf16[32,8,3072]{2,1,0:T(8,128)(2,1)}), bf16[32,8,3072]{2,1,0:T(8,128)(2,1)S(1)}, u32[]{:S(2)}, u32[]{:S(2)}) %all-to-all-start.2) | async-done | bytes 1572896 | tf_op jit(solution)/shard_map/all_to_all | solution.py:318
  225.5 3.3 %collective-permute-start.10 = (f32[8,769]{1,0:T(8,128)S(1)}, f32[8,769]{1,0:T(8,128)S(1)}, u32[]{:S(2)}, u32[]{:S(2)}) collective-permute-start(f32[8,769]{1,0:T(8,128)S(1)} %get-tuple-element.72), channel_id=1, source_target_pairs={{0,2},{1,3},{2,0},{3,1},{4,6},{5,7},{6,4},{7,5},{8,10},{9,11},{10,... | collective-permute-start | bytes 73832 | tf_op jit(solution)/shard_map/ppermute | solution.py:347
  230.9 1.7 collective-permute-done.11
  (141 shorter events, 32.8 us)
Async XLA Ops:
  7.2 10.9 %copy-start = (bf16[3072,64]{0,1:T(8,128)(2,1)S(1)}, bf16[3072,64]{0,1:T(8,128)(2,1)}, u32[]{:S(2)}) copy-start(bf16[3072,64]{0,1:T(8,128)(2,1)} %param.20) | copy-start | bytes 1179652
  7.2 10.9 %copy-start.1 = (bf16[3072,64]{0,1:T(8,128)(2,1)S(1)}, bf16[3072,64]{0,1:T(8,128)(2,1)}, u32[]{:S(2)}) copy-start(bf16[3072,64]{0,1:T(8,128)(2,1)} %param.21) | copy-start | bytes 1179652
  7.2 58.0 %all-gather.2.cloned.1.call-start = ((), (), s32[]{:S(2)}) async-start(), calls=%async_computation.3 | async-start | bytes 1622016 | tf_op jit(solution)/shard_map/all_gather | solution.py:198
  16.8 7.7 %copy-start.13 = (s32[32]{0:T(128)S(1)}, s32[32]{0:T(128)}, u32[]{:S(2)}) copy-start(s32[32]{0:T(128)} %param.25) | copy-start | bytes 388
  18.1 44.2 %collective-permute-start.1 = (bf16[3072,128]{0,1:T(8,128)(2,1)S(1)}, bf16[3072,128]{0,1:T(8,128)(2,1)S(1)}, u32[]{:S(2)}, u32[]{:S(2)}) collective-permute-start(bf16[3072,128]{0,1:T(8,128)(2,1)S(1)} %constant_dynamic-update-slice_fusion), channel_id=1, source_target_pairs={{0,2},{1,3},{2,0},{3,1},{4,6},{5,7},{6,4},{7,5},{8,10},{9,11},{10,... | collective-permute-start | bytes 2359304 | tf_op jit(solution)/shard_map/ppermute | solution.py:196
  22.2 40.2 %collective-permute-start.2 = (bf16[3072,128]{0,1:T(8,128)(2,1)S(1)}, bf16[3072,128]{0,1:T(8,128)(2,1)S(1)}, u32[]{:S(2)}, u32[]{:S(2)}) collective-permute-start(bf16[3072,128]{0,1:T(8,128)(2,1)S(1)} %constant_dynamic-update-slice_fusion), channel_id=1, source_target_pairs={{0,3},{1,0},{2,1},{3,2},{4,7},{5,4},{6,5},{7,6},{8,11},{9,8},{10,9... | collective-permute-start | bytes 2359304 | tf_op jit(solution)/shard_map/ppermute | solution.py:196
  22.9 39.5 %collective-permute-start = (bf16[3072,128]{0,1:T(8,128)(2,1)S(1)}, bf16[3072,128]{0,1:T(8,128)(2,1)}, u32[]{:S(2)}, u32[]{:S(2)}) collective-permute-start(bf16[3072,128]{0,1:T(8,128)(2,1)S(1)} %constant_dynamic-update-slice_fusion), channel_id=1, source_target_pairs={{0,1},{1,2},{2,3},{3,0},{4,5},{5,6},{6,7},{7,4},{8,9},{9,10},{10,1... | collective-permute-start | bytes 2359304 | tf_op jit(solution)/shard_map/ppermute | solution.py:196
  117.6 6.4 %copy-start.6 = (f32[16,2,8]{1,2,0:T(8,128)S(1)}, f32[16,2,8]{1,2,0:T(8,128)}, u32[]{:S(2)}) copy-start(f32[16,2,8]{1,2,0:T(8,128)} %copy.162) | copy-start | bytes 3076
  117.6 6.4 %copy-start.7 = (bf16[16,2,1,8,96]{4,3,1,0,2:T(8,128)(2,1)S(1)}, bf16[16,2,1,8,96]{4,3,1,0,2:T(8,128)(2,1)}, u32[]{:S(2)}) copy-start(bf16[16,2,1,8,96]{4,3,1,0,2:T(8,128)(2,1)} %get-tuple-element.63) | copy-start | bytes 147460
  117.6 32.1 %all-to-all-start = ((bf16[32,32,784]{2,1,0:T(8,128)(2,1)}), bf16[32,32,784]{2,1,0:T(8,128)(2,1)S(1)}, u32[]{:S(2)}, u32[]{:S(2)}) async-start(bf16[32,32,784]{2,1,0:T(8,128)(2,1)} %maximum_dynamic-update-slice_fusion), calls=%async_computation | async-start | bytes 3670016 | tf_op jit(solution)/shard_map/all_to_all | solution.py:239
  150.7 11.9 %copy-start.12 = (f32[3072]{0:T(1024)S(1)}, f32[3072]{0:T(1024)}, u32[]{:S(2)}) copy-start(f32[3072]{0:T(1024)} %param.19) | copy-start | bytes 36868
  154.0 6.9 %collective-permute-start.3 = (f32[8,3072]{1,0:T(8,128)S(1)}, f32[8,3072]{1,0:T(8,128)S(1)}, u32[]{:S(2)}, u32[]{:S(2)}) collective-permute-start(f32[8,3072]{1,0:T(8,128)S(1)} %get-tuple-element.60), channel_id=1, source_target_pairs={{0,1},{1,2},{2,3},{3,0},{4,5},{5,6},{6,7},{7,4},{8,9},{9,10},{10,1... | collective-permute-start | bytes 294920 | tf_op jit(solution)/shard_map/ppermute | solution.py:296
  155.1 6.9 %collective-permute-start.4 = (f32[8,3072]{1,0:T(8,128)S(1)}, f32[8,3072]{1,0:T(8,128)S(1)}, u32[]{:S(2)}, u32[]{:S(2)}) collective-permute-start(f32[8,3072]{1,0:T(8,128)S(1)} %get-tuple-element.62), channel_id=1, source_target_pairs={{0,2},{1,3},{2,0},{3,1},{4,6},{5,7},{6,4},{7,5},{8,10},{9,11},{10,... | collective-permute-start | bytes 294920 | tf_op jit(solution)/shard_map/ppermute | solution.py:296
  157.4 4.9 %collective-permute-start.5 = (f32[8,3072]{1,0:T(8,128)S(1)}, f32[8,3072]{1,0:T(8,128)S(1)}, u32[]{:S(2)}, u32[]{:S(2)}) collective-permute-start(f32[8,3072]{1,0:T(8,128)S(1)} %get-tuple-element.61), channel_id=1, source_target_pairs={{0,3},{1,0},{2,1},{3,2},{4,7},{5,4},{6,5},{7,6},{8,11},{9,8},{10,9... | collective-permute-start | bytes 294920 | tf_op jit(solution)/shard_map/ppermute | solution.py:296
  164.0 27.1 %all-to-all-start.1 = ((bf16[32,8,3072]{2,1,0:T(8,128)(2,1)}), bf16[32,8,3072]{2,1,0:T(8,128)(2,1)S(1)}, u32[]{:S(2)}, u32[]{:S(2)}) async-start(bf16[32,8,3072]{2,1,0:T(8,128)(2,1)} %broadcast_in_dim.43), calls=%async_computation.1 | async-start | bytes 3145728 | tf_op jit(solution)/shard_map/all_to_all | solution.py:303
  168.0 25.7 %collective-permute-start.6 = (bf16[64,3072]{1,0:T(8,128)(2,1)}, bf16[64,3072]{1,0:T(8,128)(2,1)}, u32[]{:S(2)}, u32[]{:S(2)}) collective-permute-start(bf16[64,3072]{1,0:T(8,128)(2,1)} %param.22), channel_id=1, source_target_pairs={{0,1},{1,2},{2,3},{3,0},{4,5},{5,6},{6,7},{7,4},{8,9},{9,10},{10,1... | collective-permute-start | bytes 1179656 | tf_op jit(solution)/shard_map/ppermute | solution.py:197
  168.9 24.9 %collective-permute-start.7 = (bf16[64,3072]{1,0:T(8,128)(2,1)}, bf16[64,3072]{1,0:T(8,128)(2,1)}, u32[]{:S(2)}, u32[]{:S(2)}) collective-permute-start(bf16[64,3072]{1,0:T(8,128)(2,1)} %param.22), channel_id=1, source_target_pairs={{0,2},{1,3},{2,0},{3,1},{4,6},{5,7},{6,4},{7,5},{8,10},{9,11},{10,... | collective-permute-start | bytes 1179656 | tf_op jit(solution)/shard_map/ppermute | solution.py:197
  172.2 21.6 %collective-permute-start.8 = (bf16[64,3072]{1,0:T(8,128)(2,1)}, bf16[64,3072]{1,0:T(8,128)(2,1)}, u32[]{:S(2)}, u32[]{:S(2)}) collective-permute-start(bf16[64,3072]{1,0:T(8,128)(2,1)} %param.22), channel_id=1, source_target_pairs={{0,3},{1,0},{2,1},{3,2},{4,7},{5,4},{6,5},{7,6},{8,11},{9,8},{10,9... | collective-permute-start | bytes 1179656 | tf_op jit(solution)/shard_map/ppermute | solution.py:197
  197.0 27.1 %all-to-all-start.2 = ((bf16[32,8,3072]{2,1,0:T(8,128)(2,1)}), bf16[32,8,3072]{2,1,0:T(8,128)(2,1)S(1)}, u32[]{:S(2)}, u32[]{:S(2)}) async-start(bf16[32,8,3072]{2,1,0:T(8,128)(2,1)} %fusion.1), calls=%async_computation.2 | async-start | bytes 3145728 | tf_op jit(solution)/shard_map/all_to_all | solution.py:318
  200.9 23.3 %copy-start.10 = (f32[3072]{0:T(1024)S(1)}, f32[3072]{0:T(1024)}, u32[]{:S(2)}) copy-start(f32[3072]{0:T(1024)} %param.24) | copy-start | bytes 36868
  201.0 23.3 %copy-start.11 = (f32[3072]{0:T(1024)S(1)}, f32[3072]{0:T(1024)}, u32[]{:S(2)}) copy-start(f32[3072]{0:T(1024)} %param.23) | copy-start | bytes 36868
  224.6 5.5 %collective-permute-start.9 = (f32[8,769]{1,0:T(8,128)S(1)}, f32[8,769]{1,0:T(8,128)S(1)}, u32[]{:S(2)}, u32[]{:S(2)}) collective-permute-start(f32[8,769]{1,0:T(8,128)S(1)} %get-tuple-element.71), channel_id=1, source_target_pairs={{0,1},{1,2},{2,3},{3,0},{4,5},{5,6},{6,7},{7,4},{8,9},{9,10},{10,1... | collective-permute-start | bytes 73832 | tf_op jit(solution)/shard_map/ppermute | solution.py:347
  225.5 5.5 %collective-permute-start.10 = (f32[8,769]{1,0:T(8,128)S(1)}, f32[8,769]{1,0:T(8,128)S(1)}, u32[]{:S(2)}, u32[]{:S(2)}) collective-permute-start(f32[8,769]{1,0:T(8,128)S(1)} %get-tuple-element.72), channel_id=1, source_target_pairs={{0,2},{1,3},{2,0},{3,1},{4,6},{5,7},{6,4},{7,5},{8,10},{9,11},{10,... | collective-permute-start | bytes 73832 | tf_op jit(solution)/shard_map/ppermute | solution.py:347
  228.8 3.9 %collective-permute-start.11 = (f32[8,769]{1,0:T(8,128)S(1)}, f32[8,769]{1,0:T(8,128)S(1)}, u32[]{:S(2)}, u32[]{:S(2)}) collective-permute-start(f32[8,769]{1,0:T(8,128)S(1)} %get-tuple-element.70), channel_id=1, source_target_pairs={{0,3},{1,0},{2,1},{3,2},{4,7},{5,4},{6,5},{7,6},{8,11},{9,8},{10,9... | collective-permute-start | bytes 73832 | tf_op jit(solution)/shard_map/ppermute | solution.py:347
  (6 other events, 17.5 us)
Sparse Core Ops, SparseCore 0:
  18.1 45.6 all-gather.1

commit v15 on v14

--- a/solution.py
+++ b/solution.py
@@ -38,18 +38,19 @@
         top_ref[...] = jnp.full_like(top_ref, masked_value)
         sum_ref[...] = jnp.zeros_like(sum_ref)
 
-    def step(masked):
+    @pl.when(start < valid_ref[0])
+    def _():
         keys = cache_ref[:, 0, :]
         values = cache_ref[:, 1, :]
+        places = start + lax.broadcasted_iota(jnp.int32, (1, block_len), 1)
+        bias = jnp.where(places < valid_ref[0], 0.0, masked_value)
         scores = (
             lax.dot_general(
                 q_ref[...], keys, (((1,), (1,)), ((), ())), preferred_element_type=jnp.float32
             )
             * score_scale
+            + bias
         )
-        if masked:
-            places = start + lax.broadcasted_iota(jnp.int32, scores.shape, 1)
-            scores = jnp.where(places < valid_ref[0], scores, masked_value)
         top_old = top_ref[...]
         top_new = jnp.maximum(top_old, jnp.max(scores, axis=1, keepdims=True))
         shrink = jnp.exp(top_old - top_new)
@@ -59,14 +60,6 @@
             weights.astype(jnp.bfloat16), values, preferred_element_type=jnp.float32
         )
         top_ref[...] = top_new
-
-    @pl.when(start + block_len <= valid_ref[0])
-    def _():
-        step(False)
-
-    @pl.when(jnp.logical_and(start < valid_ref[0], start + block_len > valid_ref[0]))
-    def _():
-        step(True)
 
 
 def prompt_attention(q_diag, cache, valid_count, score_scale):

time: 242 us -> 241 us (level)
  no operation moved by 1% of the time
where the time goes in v15:
time: 241 us; the launch traced here: 240 us
  waiting for transfers between devices  71.4 us (30%)
  Pallas kernels  67.5 us (28%)
  starting transfers between devices  32.3 us (13%)
  local copies, waits for them, and re-layouts  27.4 us (11%)
  between operations  21.6 us (9%)
  other arithmetic  10.2 us (4%)
  matrix products  9.7 us (4%)
    pallas_call x1, Pallas kernels, prompt_attention(): pl.pallas_call(functools.partial(prompt_kernel, block_len, score_scale),...  36.7 us
    pallas_call x1, Pallas kernels, tail_attention(): pl.pallas_call(functools.partial(tail_kernel, score_scale), grid_spec=spe...  30.8 us
    all_to_all x1, waiting for transfers between devices, per_device(): lax.all_to_all(outgoing, 'req', split_axis=0, concat_axis=0, tiled=True)  24.6 us
    all_to_all x1, waiting for transfers between devices, per_device(): lax.all_to_all(down_sum.astype(jnp.bfloat16).reshape(req_count, share, wi...  23.1 us
    all_to_all x1, waiting for transfers between devices, per_device(): lax.all_to_all(jnp.broadcast_to(normed_share[None], (req_count,) + normed...  15.5 us
    ppermute x3, starting transfers between devices, per_device(): lax.ppermute(weights_cat, 'mlp', ring)  6.06 us
    all_to_all x1, starting transfers between devices, per_device(): lax.all_to_all(outgoing, 'req', split_axis=0, concat_axis=0, tiled=True)  5.79 us
  transfers between devices with their start and end apart: 16, of which 9 were waited for; matrix products, arithmetic and copies ran while one was open for 5% of the time, Pallas kernels for 13%

profile of v15, /device:TPU:0, one launch (start us, length us, event | category | flops | bytes accessed | tf_op | source)
XLA Modules:
  0.0 240.1 jit_solution(17197905252425324272)
XLA Ops:
  11.2 1.4 fusion.53
  12.6 1.9 broadcast_add_fusion
  18.1 4.0 %collective-permute-start.1 = (bf16[3072,128]{0,1:T(8,128)(2,1)S(1)}, bf16[3072,128]{0,1:T(8,128)(2,1)S(1)}, u32[]{:S(2)}, u32[]{:S(2)}) collective-permute-start(bf16[3072,128]{0,1:T(8,128)(2,1)S(1)} %constant_dynamic-update-slice_fusion), channel_id=1, source_target_pairs={{0,2},{1,3},{2,0},{3,1},{4,6},{5,7},{6,4},{7,5},{8,10},{9,11},{10,... | collective-permute-start | bytes 2359304 | tf_op jit(solution)/shard_map/ppermute | solution.py:189
  31.5 30.8 %shard_map.149 = (f32[16,16,768]{2,1,0:T(8,128)}, f32[16,16,1]{2,1,0:T(8,128)}, f32[16,16,1]{2,1,0:T(8,128)}) custom-call(s32[16]{0:T(128)} %get-tuple-element.39.lens_ref, bf16[16,16,768]{2,1,0:T(8,128)(2,1)} %reshape.172.q_ref, bf16[16,256,2,768]{3,2,1,0:T(2,128)(2,1)} %cache_ref.2), custom_call_target="tpu_custom_call" | custom-call | flops 201326592 | bytes 13762560 | tf_op jit(solution)/shard_map/pallas_call | solution.py:137
  62.4 2.8 %pad_maximum_fusion = bf16[4,3072,128]{1,2,0:T(8,128)(2,1)} fusion(bf16[1,3072,128]{1,2,0:T(8,128)(2,1)S(1)} %bitcast.180, bf16[1,3072,128]{1,2,0:T(8,128)(2,1)S(1)} %bitcast.179, bf16[1,3072,128]{1,2,0:T(8,128)(2,1)} %bitcast.9, bf16[1,3072,128]{1,2,0:T(8,128)(2,1)S(1)} %bitcast.176), kind=kLoop, calls=%fused_computation.3 | loop fusion | flops 4718592 | bytes 6291456 | tf_op jit(solution)/shard_map/stack | solution.py:189
  65.2 1.6 reshape.181
  70.6 1.8 reshape.175.q_ref
  72.3 36.7 %shard_map.150 = (f32[512,768]{1,0:T(8,128)}, f32[512,1]{1,0:T(8,128)}, f32[512,1]{1,0:T(8,128)}) custom-call(s32[1]{0:T(128)} %bitcast.2.valid_ref, bf16[512,768]{1,0:T(8,128)(2,1)} %reshape.175.q_ref, bf16[1,4096,2,768]{3,2,1,0:T(2,128)(2,1)} %cache_ref.3), custom_call_target="tpu_custom_call" | custom-call | flops 6442450944 | bytes 14942208 | tf_op jit(solution)/shard_map/pallas_call | solution.py:88
  109.1 2.2 reshape.176
  117.5 5.8 %all-to-all-start = ((bf16[32,32,784]{2,1,0:T(8,128)(2,1)}), bf16[32,32,784]{2,1,0:T(8,128)(2,1)S(1)}, u32[]{:S(2)}, u32[]{:S(2)}) async-start(bf16[32,32,784]{2,1,0:T(8,128)(2,1)} %maximum_dynamic-update-slice_fusion), calls=%async_computation | async-start | bytes 3670016 | tf_op jit(solution)/shard_map/all_to_all | solution.py:232
  124.5 24.6 %all-to-all-done = bf16[32,32,784]{2,1,0:T(8,128)(2,1)S(1)} async-done(((bf16[32,32,784]{2,1,0:T(8,128)(2,1)}), bf16[32,32,784]{2,1,0:T(8,128)(2,1)S(1)}, u32[]{:S(2)}, u32[]{:S(2)}) %all-to-all-start) | async-done | bytes 1605664 | tf_op jit(solution)/shard_map/all_to_all | solution.py:232
  150.0 3.2 %fusion.22 = f32[32,3072]{1,0:T(8,128)S(1)} fusion(bf16[768,3072]{1,0:T(8,128)(2,1)} %param.18, f32[32,768]{1,0:T(8,128)S(1)} %div.48, f32[32,768]{1,0:T(8,128)S(1)} %reshape.182, f32[32,768]{1,0:T(8,128)S(1)} %mul.283, f32[32,768]{1,0:T(8,128)S(1)} %mul.278, f32[32,784]{1,0:T(8,128)S(1)} %get-tuple-element.51, f32[32,768]{1,0:T(8,128)S(1)} %mul.275, ...), kind=kOutput, calls=%fused_computation.59 | convolution fusion | flops 151166976 | bytes 5799936 | tf_op jit(solution)/shard_map/dot_general | solution.py:279
  154.4 2.4 collective-permute-start.4
  157.4 2.9 %collective-permute-done.3 = f32[8,3072]{1,0:T(8,128)S(1)} collective-permute-done((f32[8,3072]{1,0:T(8,128)S(1)}, f32[8,3072]{1,0:T(8,128)S(1)}, u32[]{:S(2)}, u32[]{:S(2)}) %collective-permute-start.3) | collective-permute-done | bytes 98336 | tf_op jit(solution)/shard_map/ppermute | solution.py:289
  163.3 4.0 %all-to-all-start.1 = ((bf16[32,8,3072]{2,1,0:T(8,128)(2,1)}), bf16[32,8,3072]{2,1,0:T(8,128)(2,1)S(1)}, u32[]{:S(2)}, u32[]{:S(2)}) async-start(bf16[32,8,3072]{2,1,0:T(8,128)(2,1)} %broadcast_in_dim.43), calls=%async_computation.1 | async-start | bytes 3145728 | tf_op jit(solution)/shard_map/all_to_all | solution.py:296
  168.2 3.3 %collective-permute-start.7 = (bf16[64,3072]{1,0:T(8,128)(2,1)}, bf16[64,3072]{1,0:T(8,128)(2,1)}, u32[]{:S(2)}, u32[]{:S(2)}) collective-permute-start(bf16[64,3072]{1,0:T(8,128)(2,1)} %param.22), channel_id=1, source_target_pairs={{0,2},{1,3},{2,0},{3,1},{4,6},{5,7},{6,4},{7,5},{8,10},{9,11},{10,... | collective-permute-start | bytes 1179656 | tf_op jit(solution)/shard_map/ppermute | solution.py:190
  171.5 3.4 %fusion.49 = (bf16[4,3072,64]{1,2,0:T(8,128)(2,1)}, bf16[4,3072,64]{1,2,0:T(8,128)(2,1)S(1)}) fusion(bf16[4,3072,128]{1,2,0:T(8,128)(2,1)} %pad_maximum_fusion), kind=kLoop, calls=%fused_computation.136 | loop fusion | bytes 6291456 | tf_op jit(solution)/shard_map/slice | solution.py:304
  174.9 15.5 %all-to-all-done.1 = bf16[32,8,3072]{2,1,0:T(8,128)(2,1)S(1)} async-done(((bf16[32,8,3072]{2,1,0:T(8,128)(2,1)}), bf16[32,8,3072]{2,1,0:T(8,128)(2,1)S(1)}, u32[]{:S(2)}, u32[]{:S(2)}) %all-to-all-start.1) | async-done | bytes 1572896 | tf_op jit(solution)/shard_map/all_to_all | solution.py:296
  190.4 2.0 fusion.11
  193.1 3.2 %fusion.1 = bf16[32,8,3072]{2,1,0:T(8,128)(2,1)} fusion(bf16[1,64,3072]{2,1,0:T(8,128)(2,1)} %bitcast.61, bf16[1,64,3072]{2,1,0:T(8,128)(2,1)} %bitcast.60, bf16[1,64,3072]{2,1,0:T(8,128)(2,1)} %bitcast.59, bf16[1,64,3072]{2,1,0:T(8,128)(2,1)} %bitcast.58, f32[256,4,64]{0,2,1:T(8,128)S(1)} %bitcast.183, f32[256,4,64]{0,2,1:T(8,128)S(1)} %bitcast.182), kind=kOutput, calls=%fused_computation.2 | convolution fusion | flops 406192128 | bytes 3670016 | tf_op jit(solution)/shard_map/rmj,mjf->rf/dot_general | solution.py:309
  196.3 4.0 %all-to-all-start.2 = ((bf16[32,8,3072]{2,1,0:T(8,128)(2,1)}), bf16[32,8,3072]{2,1,0:T(8,128)(2,1)S(1)}, u32[]{:S(2)}, u32[]{:S(2)}) async-start(bf16[32,8,3072]{2,1,0:T(8,128)(2,1)} %fusion.1), calls=%async_computation.2 | async-start | bytes 3145728 | tf_op jit(solution)/shard_map/all_to_all | solution.py:311
  200.3 23.1 %all-to-all-done.2 = bf16[32,8,3072]{2,1,0:T(8,128)(2,1)S(1)} async-done(((bf16[32,8,3072]{2,1,0:T(8,128)(2,1)}), bf16[32,8,3072]{2,1,0:T(8,128)(2,1)S(1)}, u32[]{:S(2)}, u32[]{:S(2)}) %all-to-all-start.2) | async-done | bytes 1572896 | tf_op jit(solution)/shard_map/all_to_all | solution.py:311
  224.8 3.3 %collective-permute-start.10 = (f32[8,769]{1,0:T(8,128)S(1)}, f32[8,769]{1,0:T(8,128)S(1)}, u32[]{:S(2)}, u32[]{:S(2)}) collective-permute-start(f32[8,769]{1,0:T(8,128)S(1)} %get-tuple-element.72), channel_id=1, source_target_pairs={{0,2},{1,3},{2,0},{3,1},{4,6},{5,7},{6,4},{7,5},{8,10},{9,11},{10,... | collective-permute-start | bytes 73832 | tf_op jit(solution)/shard_map/ppermute | solution.py:340
  230.3 1.7 collective-permute-done.11
  (141 shorter events, 32.8 us)
Async XLA Ops:
  7.2 10.9 %copy-start = (bf16[3072,64]{0,1:T(8,128)(2,1)S(1)}, bf16[3072,64]{0,1:T(8,128)(2,1)}, u32[]{:S(2)}) copy-start(bf16[3072,64]{0,1:T(8,128)(2,1)} %param.20) | copy-start | bytes 1179652
  7.2 10.9 %copy-start.1 = (bf16[3072,64]{0,1:T(8,128)(2,1)S(1)}, bf16[3072,64]{0,1:T(8,128)(2,1)}, u32[]{:S(2)}) copy-start(bf16[3072,64]{0,1:T(8,128)(2,1)} %param.21) | copy-start | bytes 1179652
  7.2 58.0 %all-gather.2.cloned.1.call-start = ((), (), s32[]{:S(2)}) async-start(), calls=%async_computation.3 | async-start | bytes 1622016 | tf_op jit(solution)/shard_map/all_gather | solution.py:191
  16.8 7.7 %copy-start.13 = (s32[32]{0:T(128)S(1)}, s32[32]{0:T(128)}, u32[]{:S(2)}) copy-start(s32[32]{0:T(128)} %param.25) | copy-start | bytes 388
  18.1 44.2 %collective-permute-start.1 = (bf16[3072,128]{0,1:T(8,128)(2,1)S(1)}, bf16[3072,128]{0,1:T(8,128)(2,1)S(1)}, u32[]{:S(2)}, u32[]{:S(2)}) collective-permute-start(bf16[3072,128]{0,1:T(8,128)(2,1)S(1)} %constant_dynamic-update-slice_fusion), channel_id=1, source_target_pairs={{0,2},{1,3},{2,0},{3,1},{4,6},{5,7},{6,4},{7,5},{8,10},{9,11},{10,... | collective-permute-start | bytes 2359304 | tf_op jit(solution)/shard_map/ppermute | solution.py:189
  22.2 40.2 %collective-permute-start.2 = (bf16[3072,128]{0,1:T(8,128)(2,1)S(1)}, bf16[3072,128]{0,1:T(8,128)(2,1)S(1)}, u32[]{:S(2)}, u32[]{:S(2)}) collective-permute-start(bf16[3072,128]{0,1:T(8,128)(2,1)S(1)} %constant_dynamic-update-slice_fusion), channel_id=1, source_target_pairs={{0,3},{1,0},{2,1},{3,2},{4,7},{5,4},{6,5},{7,6},{8,11},{9,8},{10,9... | collective-permute-start | bytes 2359304 | tf_op jit(solution)/shard_map/ppermute | solution.py:189
  22.9 39.5 %collective-permute-start = (bf16[3072,128]{0,1:T(8,128)(2,1)S(1)}, bf16[3072,128]{0,1:T(8,128)(2,1)}, u32[]{:S(2)}, u32[]{:S(2)}) collective-permute-start(bf16[3072,128]{0,1:T(8,128)(2,1)S(1)} %constant_dynamic-update-slice_fusion), channel_id=1, source_target_pairs={{0,1},{1,2},{2,3},{3,0},{4,5},{5,6},{6,7},{7,4},{8,9},{9,10},{10,1... | collective-permute-start | bytes 2359304 | tf_op jit(solution)/shard_map/ppermute | solution.py:189
  117.5 6.1 %copy-start.6 = (f32[16,2,8]{1,2,0:T(8,128)S(1)}, f32[16,2,8]{1,2,0:T(8,128)}, u32[]{:S(2)}) copy-start(f32[16,2,8]{1,2,0:T(8,128)} %copy.162) | copy-start | bytes 3076
  117.5 6.1 %copy-start.7 = (bf16[16,2,1,8,96]{4,3,1,0,2:T(8,128)(2,1)S(1)}, bf16[16,2,1,8,96]{4,3,1,0,2:T(8,128)(2,1)}, u32[]{:S(2)}) copy-start(bf16[16,2,1,8,96]{4,3,1,0,2:T(8,128)(2,1)} %get-tuple-element.63) | copy-start | bytes 147460
  117.5 31.6 %all-to-all-start = ((bf16[32,32,784]{2,1,0:T(8,128)(2,1)}), bf16[32,32,784]{2,1,0:T(8,128)(2,1)S(1)}, u32[]{:S(2)}, u32[]{:S(2)}) async-start(bf16[32,32,784]{2,1,0:T(8,128)(2,1)} %maximum_dynamic-update-slice_fusion), calls=%async_computation | async-start | bytes 3670016 | tf_op jit(solution)/shard_map/all_to_all | solution.py:232
  150.0 11.9 %copy-start.12 = (f32[3072]{0:T(1024)S(1)}, f32[3072]{0:T(1024)}, u32[]{:S(2)}) copy-start(f32[3072]{0:T(1024)} %param.19) | copy-start | bytes 36868
  153.3 6.9 %collective-permute-start.3 = (f32[8,3072]{1,0:T(8,128)S(1)}, f32[8,3072]{1,0:T(8,128)S(1)}, u32[]{:S(2)}, u32[]{:S(2)}) collective-permute-start(f32[8,3072]{1,0:T(8,128)S(1)} %get-tuple-element.60), channel_id=1, source_target_pairs={{0,1},{1,2},{2,3},{3,0},{4,5},{5,6},{6,7},{7,4},{8,9},{9,10},{10,1... | collective-permute-start | bytes 294920 | tf_op jit(solution)/shard_map/ppermute | solution.py:289
  154.4 6.9 %collective-permute-start.4 = (f32[8,3072]{1,0:T(8,128)S(1)}, f32[8,3072]{1,0:T(8,128)S(1)}, u32[]{:S(2)}, u32[]{:S(2)}) collective-permute-start(f32[8,3072]{1,0:T(8,128)S(1)} %get-tuple-element.62), channel_id=1, source_target_pairs={{0,2},{1,3},{2,0},{3,1},{4,6},{5,7},{6,4},{7,5},{8,10},{9,11},{10,... | collective-permute-start | bytes 294920 | tf_op jit(solution)/shard_map/ppermute | solution.py:289
  156.8 4.9 %collective-permute-start.5 = (f32[8,3072]{1,0:T(8,128)S(1)}, f32[8,3072]{1,0:T(8,128)S(1)}, u32[]{:S(2)}, u32[]{:S(2)}) collective-permute-start(f32[8,3072]{1,0:T(8,128)S(1)} %get-tuple-element.61), channel_id=1, source_target_pairs={{0,3},{1,0},{2,1},{3,2},{4,7},{5,4},{6,5},{7,6},{8,11},{9,8},{10,9... | collective-permute-start | bytes 294920 | tf_op jit(solution)/shard_map/ppermute | solution.py:289
  163.3 27.1 %all-to-all-start.1 = ((bf16[32,8,3072]{2,1,0:T(8,128)(2,1)}), bf16[32,8,3072]{2,1,0:T(8,128)(2,1)S(1)}, u32[]{:S(2)}, u32[]{:S(2)}) async-start(bf16[32,8,3072]{2,1,0:T(8,128)(2,1)} %broadcast_in_dim.43), calls=%async_computation.1 | async-start | bytes 3145728 | tf_op jit(solution)/shard_map/all_to_all | solution.py:296
  167.3 25.7 %collective-permute-start.6 = (bf16[64,3072]{1,0:T(8,128)(2,1)}, bf16[64,3072]{1,0:T(8,128)(2,1)}, u32[]{:S(2)}, u32[]{:S(2)}) collective-permute-start(bf16[64,3072]{1,0:T(8,128)(2,1)} %param.22), channel_id=1, source_target_pairs={{0,1},{1,2},{2,3},{3,0},{4,5},{5,6},{6,7},{7,4},{8,9},{9,10},{10,1... | collective-permute-start | bytes 1179656 | tf_op jit(solution)/shard_map/ppermute | solution.py:190
  168.2 24.9 %collective-permute-start.7 = (bf16[64,3072]{1,0:T(8,128)(2,1)}, bf16[64,3072]{1,0:T(8,128)(2,1)}, u32[]{:S(2)}, u32[]{:S(2)}) collective-permute-start(bf16[64,3072]{1,0:T(8,128)(2,1)} %param.22), channel_id=1, source_target_pairs={{0,2},{1,3},{2,0},{3,1},{4,6},{5,7},{6,4},{7,5},{8,10},{9,11},{10,... | collective-permute-start | bytes 1179656 | tf_op jit(solution)/shard_map/ppermute | solution.py:190
  171.5 21.6 %collective-permute-start.8 = (bf16[64,3072]{1,0:T(8,128)(2,1)}, bf16[64,3072]{1,0:T(8,128)(2,1)}, u32[]{:S(2)}, u32[]{:S(2)}) collective-permute-start(bf16[64,3072]{1,0:T(8,128)(2,1)} %param.22), channel_id=1, source_target_pairs={{0,3},{1,0},{2,1},{3,2},{4,7},{5,4},{6,5},{7,6},{8,11},{9,8},{10,9... | collective-permute-start | bytes 1179656 | tf_op jit(solution)/shard_map/ppermute | solution.py:190
  196.3 27.1 %all-to-all-start.2 = ((bf16[32,8,3072]{2,1,0:T(8,128)(2,1)}), bf16[32,8,3072]{2,1,0:T(8,128)(2,1)S(1)}, u32[]{:S(2)}, u32[]{:S(2)}) async-start(bf16[32,8,3072]{2,1,0:T(8,128)(2,1)} %fusion.1), calls=%async_computation.2 | async-start | bytes 3145728 | tf_op jit(solution)/shard_map/all_to_all | solution.py:311
  200.3 23.3 %copy-start.10 = (f32[3072]{0:T(1024)S(1)}, f32[3072]{0:T(1024)}, u32[]{:S(2)}) copy-start(f32[3072]{0:T(1024)} %param.24) | copy-start | bytes 36868
  200.3 23.3 %copy-start.11 = (f32[3072]{0:T(1024)S(1)}, f32[3072]{0:T(1024)}, u32[]{:S(2)}) copy-start(f32[3072]{0:T(1024)} %param.23) | copy-start | bytes 36868
  223.9 5.5 %collective-permute-start.9 = (f32[8,769]{1,0:T(8,128)S(1)}, f32[8,769]{1,0:T(8,128)S(1)}, u32[]{:S(2)}, u32[]{:S(2)}) collective-permute-start(f32[8,769]{1,0:T(8,128)S(1)} %get-tuple-element.71), channel_id=1, source_target_pairs={{0,1},{1,2},{2,3},{3,0},{4,5},{5,6},{6,7},{7,4},{8,9},{9,10},{10,1... | collective-permute-start | bytes 73832 | tf_op jit(solution)/shard_map/ppermute | solution.py:340
  224.8 5.4 %collective-permute-start.10 = (f32[8,769]{1,0:T(8,128)S(1)}, f32[8,769]{1,0:T(8,128)S(1)}, u32[]{:S(2)}, u32[]{:S(2)}) collective-permute-start(f32[8,769]{1,0:T(8,128)S(1)} %get-tuple-element.72), channel_id=1, source_target_pairs={{0,2},{1,3},{2,0},{3,1},{4,6},{5,7},{6,4},{7,5},{8,10},{9,11},{10,... | collective-permute-start | bytes 73832 | tf_op jit(solution)/shard_map/ppermute | solution.py:340
  228.1 3.9 %collective-permute-start.11 = (f32[8,769]{1,0:T(8,128)S(1)}, f32[8,769]{1,0:T(8,128)S(1)}, u32[]{:S(2)}, u32[]{:S(2)}) collective-permute-start(f32[8,769]{1,0:T(8,128)S(1)} %get-tuple-element.70), channel_id=1, source_target_pairs={{0,3},{1,0},{2,1},{3,2},{4,7},{5,4},{6,5},{7,6},{8,11},{9,8},{10,9... | collective-permute-start | bytes 73832 | tf_op jit(solution)/shard_map/ppermute | solution.py:340
  (6 other events, 17.2 us)
Sparse Core Ops, SparseCore 0:
  18.1 45.6 all-gather.1

commit v16 on v15

--- a/solution.py
+++ b/solution.py
@@ -184,10 +184,11 @@
     key_new = rotary(block[:, :, 1].astype(jnp.float32), position).astype(jnp.bfloat16)
     value_new = block[:, :, 2]
     mlp_count = lax.axis_size("mlp")
-    weights_cat = jnp.concatenate([w_gate, w_up], axis=1)
+    weights_cat = w_gate
     rings = [[(m, (m + shift) % mlp_count) for m in range(mlp_count)] for shift in range(1, mlp_count)]
     weights_all = jnp.stack([weights_cat] + [lax.ppermute(weights_cat, "mlp", ring) for ring in rings])
     down_w = jnp.stack([w_down] + [lax.ppermute(w_down, "mlp", ring) for ring in rings])
+    up_w = jnp.stack([w_up] + [lax.ppermute(w_up, "mlp", ring) for ring in rings])
     gathered = lax.all_gather(query.reshape(rows_here, width_here), "req", axis=0, tiled=True)
     eye = jnp.eye(heads_here, dtype=jnp.bfloat16)
     tail_diag = jnp.einsum("cthd,hg->chtgd", query, eye).reshape(
@@ -302,7 +303,6 @@
     ).reshape(req_count * share, width)
     hidden_here = w_gate.shape[1]
     gate_w = weights_all[:, :, :hidden_here]
-    up_w = weights_all[:, :, hidden_here : 2 * hidden_here]
     gate = jnp.einsum("rk,mkj->rmj", piece, gate_w, preferred_element_type=jnp.float32)
     upper = jnp.einsum("rk,mkj->rmj", piece, up_w, preferred_element_type=jnp.float32)
     hidden_all = (jax.nn.silu(gate) * upper).astype(jnp.bfloat16)

time: 241 us -> 259 us (1.075)
  starting transfers between devices: 32.3 us -> 39.8 us
  waiting for transfers between devices: 71.4 us -> 78.5 us
  local copies, waits for them, and re-layouts: 27.4 us -> 30.4 us
    ppermute x0 -> x3, waiting for transfers between devices: none -> 15.6 us  [per_device(): lax.ppermute(w_up, 'mlp', ring)]
    all_to_all x1, waiting for transfers between devices: 15.5 us -> 0.01 us  [per_device(): lax.all_to_all(jnp.broadcast_to(normed_share[None], (req_count,) + normed...]
    ppermute x3, waiting for transfers between devices: 0.01 us -> 11.8 us  [per_device(): lax.ppermute(w_down, 'mlp', ring)]
    all_to_all x1, waiting for transfers between devices: 24.6 us -> 19.7 us  [per_device(): lax.all_to_all(outgoing, 'req', split_axis=0, concat_axis=0, tiled=True)]
    ppermute x0 -> x3, starting transfers between devices: none -> 4.21 us  [per_device(): lax.ppermute(w_up, 'mlp', ring)]
    all_to_all x1, starting transfers between devices: 3.97 us -> 7.37 us  [per_device(): lax.all_to_all(down_sum.astype(jnp.bfloat16).reshape(req_count, share, wi...]
    slice x1 -> x0, local copies, waits for them, and re-layouts: 3.35 us -> none  [per_device(): gate_w = weights_all[:, :, :hidden_here]]
  transfers between devices with their start and end apart: 16 -> 19, of which waited for: 9 -> 12; matrix products, arithmetic and copies ran while one was open for 5% -> 6% of each run, Pallas kernels for 13% -> 12%
where the time goes in v16:
time: 259 us
  waiting for transfers between devices  78.5 us (30%)
  Pallas kernels  67.5 us (26%)
  starting transfers between devices  39.8 us (15%)
  local copies, waits for them, and re-layouts  30.4 us (12%)
  between operations  21.8 us (8%)
  other arithmetic  12 us (5%)
  matrix products  9.08 us (4%)
    pallas_call x1, Pallas kernels, prompt_attention(): pl.pallas_call(functools.partial(prompt_kernel, block_len, score_scale),...  36.7 us
    pallas_call x1, Pallas kernels, tail_attention(): pl.pallas_call(functools.partial(tail_kernel, score_scale), grid_spec=spe...  30.8 us
    all_to_all x1, waiting for transfers between devices, per_device(): lax.all_to_all(down_sum.astype(jnp.bfloat16).reshape(req_count, share, wi...  23.1 us
    all_to_all x1, waiting for transfers between devices, per_device(): lax.all_to_all(outgoing, 'req', split_axis=0, concat_axis=0, tiled=True)  19.7 us
    ppermute x3, waiting for transfers between devices, per_device(): lax.ppermute(w_up, 'mlp', ring)  15.6 us
    ppermute x3, waiting for transfers between devices, per_device(): lax.ppermute(w_down, 'mlp', ring)  11.8 us
    all_to_all x1, starting transfers between devices, per_device(): lax.all_to_all(down_sum.astype(jnp.bfloat16).reshape(req_count, share, wi...  7.37 us
    all_to_all x1, starting transfers between devices, per_device(): lax.all_to_all(outgoing, 'req', split_axis=0, concat_axis=0, tiled=True)  7.33 us
  transfers between devices with their start and end apart: 19, of which 12 were waited for; matrix products, arithmetic and copies ran while one was open for 6% of the time, Pallas kernels for 12%

profile of v16, /device:TPU:0, one launch (start us, length us, event | category | flops | bytes accessed | tf_op | source)
XLA Modules:
  0.0 259.1 jit_solution(17830393469960678396)
XLA Ops:
  12.5 1.9 broadcast_add_fusion
  18.0 4.0 %collective-permute-start.1 = (bf16[3072,64]{0,1:T(8,128)(2,1)S(1)}, bf16[3072,64]{0,1:T(8,128)(2,1)S(1)}, u32[]{:S(2)}, u32[]{:S(2)}) collective-permute-start(bf16[3072,64]{0,1:T(8,128)(2,1)S(1)} %copy-done.4), channel_id=1, source_target_pairs={{0,2},{1,3},{2,0},{3,1},{4,6},{5,7},{6,4},{7,5},{8,10},{9,11},{10,... | collective-permute-start | bytes 1179656 | tf_op jit(solution)/shard_map/ppermute | solution.py:189
  31.6 30.8 %shard_map.149 = (f32[16,16,768]{2,1,0:T(8,128)}, f32[16,16,1]{2,1,0:T(8,128)}, f32[16,16,1]{2,1,0:T(8,128)}) custom-call(s32[16]{0:T(128)} %get-tuple-element.39.lens_ref, bf16[16,16,768]{2,1,0:T(8,128)(2,1)} %reshape.172.q_ref, bf16[16,256,2,768]{3,2,1,0:T(2,128)(2,1)} %cache_ref.2), custom_call_target="tpu_custom_call" | custom-call | flops 201326592 | bytes 13762560 | tf_op jit(solution)/shard_map/pallas_call | solution.py:137
  70.4 1.8 reshape.175.q_ref
  72.1 36.7 %shard_map.150 = (f32[512,768]{1,0:T(8,128)}, f32[512,1]{1,0:T(8,128)}, f32[512,1]{1,0:T(8,128)}) custom-call(s32[1]{0:T(128)} %bitcast.2.valid_ref, bf16[512,768]{1,0:T(8,128)(2,1)} %reshape.175.q_ref, bf16[1,4096,2,768]{3,2,1,0:T(2,128)(2,1)} %cache_ref.3), custom_call_target="tpu_custom_call" | custom-call | flops 6442450944 | bytes 14942208 | tf_op jit(solution)/shard_map/pallas_call | solution.py:88
  108.9 3.1 %reshape.176 = f32[8,64,8,96]{3,2,1,0:T(8,128)} reshape(f32[512,768]{1,0:T(8,128)} %get-tuple-element.17) | data formatting | bytes 3145728 | tf_op jit(solution)/shard_map/reshape | solution.py:217
  112.0 1.7 slice_bitcast_fusion
  117.3 7.3 %all-to-all-start = ((bf16[32,32,784]{2,1,0:T(8,128)(2,1)}), bf16[32,32,784]{2,1,0:T(8,128)(2,1)S(1)}, u32[]{:S(2)}, u32[]{:S(2)}) async-start(bf16[32,32,784]{2,1,0:T(8,128)(2,1)} %maximum_dynamic-update-slice_fusion), calls=%async_computation | async-start | bytes 3670016 | tf_op jit(solution)/shard_map/all_to_all | solution.py:233
  130.7 19.7 %all-to-all-done = bf16[32,32,784]{2,1,0:T(8,128)(2,1)S(1)} async-done(((bf16[32,32,784]{2,1,0:T(8,128)(2,1)}), bf16[32,32,784]{2,1,0:T(8,128)(2,1)S(1)}, u32[]{:S(2)}, u32[]{:S(2)}) %all-to-all-start) | async-done | bytes 1605664 | tf_op jit(solution)/shard_map/all_to_all | solution.py:233
  152.8 3.2 %fusion.22 = f32[32,3072]{1,0:T(8,128)S(1)} fusion(bf16[768,3072]{1,0:T(8,128)(2,1)} %param.18, f32[32,768]{1,0:T(8,128)S(1)} %div.48, f32[32,768]{1,0:T(8,128)S(1)} %copy-done.6, f32[32,768]{1,0:T(8,128)S(1)} %mul.283, f32[32,768]{1,0:T(8,128)S(1)} %mul.278, f32[32,784]{1,0:T(8,128)S(1)} %copy-done.3, f32[32,768]{1,0:T(8,128)S(1)} %mul.275, ...), kind=kOutput, calls=%fused_computation.60 | convolution fusion | flops 151166976 | bytes 5799936 | tf_op jit(solution)/shard_map/dot_general | solution.py:280
  157.2 2.4 collective-permute-start.4
  160.0 3.0 %collective-permute-done.3 = f32[8,3072]{1,0:T(8,128)S(1)} collective-permute-done((f32[8,3072]{1,0:T(8,128)S(1)}, f32[8,3072]{1,0:T(8,128)S(1)}, u32[]{:S(2)}, u32[]{:S(2)}) %collective-permute-start.3) | collective-permute-done | bytes 98336 | tf_op jit(solution)/shard_map/ppermute | solution.py:290
  166.1 4.0 %all-to-all-start.1 = ((bf16[32,8,3072]{2,1,0:T(8,128)(2,1)}), bf16[32,8,3072]{2,1,0:T(8,128)(2,1)S(1)}, u32[]{:S(2)}, u32[]{:S(2)}) async-start(bf16[32,8,3072]{2,1,0:T(8,128)(2,1)} %broadcast_in_dim.43), calls=%async_computation.1 | async-start | bytes 3145728 | tf_op jit(solution)/shard_map/all_to_all | solution.py:297
  171.0 3.3 %collective-permute-start.7 = (bf16[3072,64]{0,1:T(8,128)(2,1)}, bf16[3072,64]{0,1:T(8,128)(2,1)S(1)}, u32[]{:S(2)}, u32[]{:S(2)}) collective-permute-start(bf16[3072,64]{0,1:T(8,128)(2,1)} %param.21), channel_id=1, source_target_pairs={{0,2},{1,3},{2,0},{3,1},{4,6},{5,7},{6,4},{7,5},{8,10},{9,11},{10,... | collective-permute-start | bytes 1179656 | tf_op jit(solution)/shard_map/ppermute | solution.py:191
  174.3 2.0 collective-permute-start.9
  176.6 7.6 %collective-permute-done.6 = bf16[3072,64]{0,1:T(8,128)(2,1)S(1)} collective-permute-done((bf16[3072,64]{0,1:T(8,128)(2,1)}, bf16[3072,64]{0,1:T(8,128)(2,1)S(1)}, u32[]{:S(2)}, u32[]{:S(2)}) %collective-permute-start.6) | collective-permute-done | bytes 393248 | tf_op jit(solution)/shard_map/ppermute | solution.py:191
  185.0 7.9 %collective-permute-done.7 = bf16[3072,64]{0,1:T(8,128)(2,1)S(1)} collective-permute-done((bf16[3072,64]{0,1:T(8,128)(2,1)}, bf16[3072,64]{0,1:T(8,128)(2,1)S(1)}, u32[]{:S(2)}, u32[]{:S(2)}) %collective-permute-start.7) | collective-permute-done | bytes 393248 | tf_op jit(solution)/shard_map/ppermute | solution.py:191
  192.9 2.3 pad_maximum_fusion.1
  197.3 2.4 collective-permute-done.9
  199.8 9.4 %collective-permute-done.10 = bf16[64,3072]{1,0:T(8,128)(2,1)} collective-permute-done((bf16[64,3072]{1,0:T(8,128)(2,1)}, bf16[64,3072]{1,0:T(8,128)(2,1)}, u32[]{:S(2)}, u32[]{:S(2)}) %collective-permute-start.10) | collective-permute-done | bytes 393248 | tf_op jit(solution)/shard_map/ppermute | solution.py:190
  209.1 3.1 %fusion.1 = bf16[32,8,3072]{2,1,0:T(8,128)(2,1)} fusion(bf16[1,64,3072]{2,1,0:T(8,128)(2,1)} %bitcast.65, bf16[1,64,3072]{2,1,0:T(8,128)(2,1)} %bitcast.64, bf16[1,64,3072]{2,1,0:T(8,128)(2,1)} %bitcast.63, bf16[1,64,3072]{2,1,0:T(8,128)(2,1)S(1)} %bitcast.209, f32[256,4,64]{0,2,1:T(8,128)S(1)} %bitcast.192, f32[256,4,64]{0,2,1:T(8,128)S(1)} %bitcast.191), kind=kOutput, calls=%fused_computation.2 | convolution fusion | flops 406192128 | bytes 3670016 | tf_op jit(solution)/shard_map/rmj,mjf->rf/dot_general | solution.py:309
  212.2 7.4 %all-to-all-start.2 = ((bf16[32,8,3072]{2,1,0:T(8,128)(2,1)}), bf16[32,8,3072]{2,1,0:T(8,128)(2,1)S(1)}, u32[]{:S(2)}, u32[]{:S(2)}) async-start(bf16[32,8,3072]{2,1,0:T(8,128)(2,1)} %fusion.1), calls=%async_computation.2 | async-start | bytes 3145728 | tf_op jit(solution)/shard_map/all_to_all | solution.py:311
  219.7 23.1 %all-to-all-done.2 = bf16[32,8,3072]{2,1,0:T(8,128)(2,1)S(1)} async-done(((bf16[32,8,3072]{2,1,0:T(8,128)(2,1)}), bf16[32,8,3072]{2,1,0:T(8,128)(2,1)S(1)}, u32[]{:S(2)}, u32[]{:S(2)}) %all-to-all-start.2) | async-done | bytes 1572896 | tf_op jit(solution)/shard_map/all_to_all | solution.py:311
  243.8 3.3 %collective-permute-start.13 = (f32[8,769]{1,0:T(8,128)S(1)}, f32[8,769]{1,0:T(8,128)S(1)}, u32[]{:S(2)}, u32[]{:S(2)}) collective-permute-start(f32[8,769]{1,0:T(8,128)S(1)} %get-tuple-element.70), channel_id=1, source_target_pairs={{0,2},{1,3},{2,0},{3,1},{4,6},{5,7},{6,4},{7,5},{8,10},{9,11},{10,... | collective-permute-start | bytes 73832 | tf_op jit(solution)/shard_map/ppermute | solution.py:340
  (167 shorter events, 45.7 us)
Async XLA Ops:
  7.2 16.9 %copy-start.24 = (s32[32]{0:T(128)S(1)}, s32[32]{0:T(128)}, u32[]{:S(2)}) copy-start(s32[32]{0:T(128)} %param.25) | copy-start | bytes 388
  7.2 58.0 %all-gather.2.cloned.1.call-start = ((), (), s32[]{:S(2)}) async-start(), calls=%async_computation.3 | async-start | bytes 1622016 | tf_op jit(solution)/shard_map/all_gather | solution.py:192
  18.0 45.1 %collective-permute-start.1 = (bf16[3072,64]{0,1:T(8,128)(2,1)S(1)}, bf16[3072,64]{0,1:T(8,128)(2,1)S(1)}, u32[]{:S(2)}, u32[]{:S(2)}) collective-permute-start(bf16[3072,64]{0,1:T(8,128)(2,1)S(1)} %copy-done.4), channel_id=1, source_target_pairs={{0,2},{1,3},{2,0},{3,1},{4,6},{5,7},{6,4},{7,5},{8,10},{9,11},{10,... | collective-permute-start | bytes 1179656 | tf_op jit(solution)/shard_map/ppermute | solution.py:189
  22.0 41.0 %collective-permute-start.2 = (bf16[3072,64]{0,1:T(8,128)(2,1)S(1)}, bf16[3072,64]{0,1:T(8,128)(2,1)S(1)}, u32[]{:S(2)}, u32[]{:S(2)}) collective-permute-start(bf16[3072,64]{0,1:T(8,128)(2,1)S(1)} %copy-done.4), channel_id=1, source_target_pairs={{0,3},{1,0},{2,1},{3,2},{4,7},{5,4},{6,5},{7,6},{8,11},{9,8},{10,9... | collective-permute-start | bytes 1179656 | tf_op jit(solution)/shard_map/ppermute | solution.py:189
  22.7 40.3 %collective-permute-start = (bf16[3072,64]{0,1:T(8,128)(2,1)S(1)}, bf16[3072,64]{0,1:T(8,128)(2,1)S(1)}, u32[]{:S(2)}, u32[]{:S(2)}) collective-permute-start(bf16[3072,64]{0,1:T(8,128)(2,1)S(1)} %copy-done.4), channel_id=1, source_target_pairs={{0,1},{1,2},{2,3},{3,0},{4,5},{5,6},{6,7},{7,4},{8,9},{9,10},{10,1... | collective-permute-start | bytes 1179656 | tf_op jit(solution)/shard_map/ppermute | solution.py:189
  27.4 34.9 %copy-start.16 = (bf16[8,8]{1,0:T(8,128)(2,1)}, bf16[8,8]{1,0:T(8,128)(2,1)S(1)}, u32[]{:S(2)}) copy-start(bf16[8,8]{1,0:T(8,128)(2,1)S(1)} %fusion.43) | copy-start | bytes 388
  117.3 33.1 %all-to-all-start = ((bf16[32,32,784]{2,1,0:T(8,128)(2,1)}), bf16[32,32,784]{2,1,0:T(8,128)(2,1)S(1)}, u32[]{:S(2)}, u32[]{:S(2)}) async-start(bf16[32,32,784]{2,1,0:T(8,128)(2,1)} %maximum_dynamic-update-slice_fusion), calls=%async_computation | async-start | bytes 3670016 | tf_op jit(solution)/shard_map/all_to_all | solution.py:233
  156.1 6.9 %collective-permute-start.3 = (f32[8,3072]{1,0:T(8,128)S(1)}, f32[8,3072]{1,0:T(8,128)S(1)}, u32[]{:S(2)}, u32[]{:S(2)}) collective-permute-start(f32[8,3072]{1,0:T(8,128)S(1)} %get-tuple-element.58), channel_id=1, source_target_pairs={{0,1},{1,2},{2,3},{3,0},{4,5},{5,6},{6,7},{7,4},{8,9},{9,10},{10,1... | collective-permute-start | bytes 294920 | tf_op jit(solution)/shard_map/ppermute | solution.py:290
  157.2 6.9 %collective-permute-start.4 = (f32[8,3072]{1,0:T(8,128)S(1)}, f32[8,3072]{1,0:T(8,128)S(1)}, u32[]{:S(2)}, u32[]{:S(2)}) collective-permute-start(f32[8,3072]{1,0:T(8,128)S(1)} %get-tuple-element.60), channel_id=1, source_target_pairs={{0,2},{1,3},{2,0},{3,1},{4,6},{5,7},{6,4},{7,5},{8,10},{9,11},{10,... | collective-permute-start | bytes 294920 | tf_op jit(solution)/shard_map/ppermute | solution.py:290
  159.6 4.9 %collective-permute-start.5 = (f32[8,3072]{1,0:T(8,128)S(1)}, f32[8,3072]{1,0:T(8,128)S(1)}, u32[]{:S(2)}, u32[]{:S(2)}) collective-permute-start(f32[8,3072]{1,0:T(8,128)S(1)} %get-tuple-element.59), channel_id=1, source_target_pairs={{0,3},{1,0},{2,1},{3,2},{4,7},{5,4},{6,5},{7,6},{8,11},{9,8},{10,9... | collective-permute-start | bytes 294920 | tf_op jit(solution)/shard_map/ppermute | solution.py:290
  166.1 29.1 %all-to-all-start.1 = ((bf16[32,8,3072]{2,1,0:T(8,128)(2,1)}), bf16[32,8,3072]{2,1,0:T(8,128)(2,1)S(1)}, u32[]{:S(2)}, u32[]{:S(2)}) async-start(bf16[32,8,3072]{2,1,0:T(8,128)(2,1)} %broadcast_in_dim.43), calls=%async_computation.1 | async-start | bytes 3145728 | tf_op jit(solution)/shard_map/all_to_all | solution.py:297
  170.1 14.1 %collective-permute-start.6 = (bf16[3072,64]{0,1:T(8,128)(2,1)}, bf16[3072,64]{0,1:T(8,128)(2,1)S(1)}, u32[]{:S(2)}, u32[]{:S(2)}) collective-permute-start(bf16[3072,64]{0,1:T(8,128)(2,1)} %param.21), channel_id=1, source_target_pairs={{0,1},{1,2},{2,3},{3,0},{4,5},{5,6},{6,7},{7,4},{8,9},{9,10},{10,1... | collective-permute-start | bytes 1179656 | tf_op jit(solution)/shard_map/ppermute | solution.py:191
  171.0 21.9 %collective-permute-start.7 = (bf16[3072,64]{0,1:T(8,128)(2,1)}, bf16[3072,64]{0,1:T(8,128)(2,1)S(1)}, u32[]{:S(2)}, u32[]{:S(2)}) collective-permute-start(bf16[3072,64]{0,1:T(8,128)(2,1)} %param.21), channel_id=1, source_target_pairs={{0,2},{1,3},{2,0},{3,1},{4,6},{5,7},{6,4},{7,5},{8,10},{9,11},{10,... | collective-permute-start | bytes 1179656 | tf_op jit(solution)/shard_map/ppermute | solution.py:191
  174.3 18.6 %collective-permute-start.8 = (bf16[3072,64]{0,1:T(8,128)(2,1)}, bf16[3072,64]{0,1:T(8,128)(2,1)S(1)}, u32[]{:S(2)}, u32[]{:S(2)}) collective-permute-start(bf16[3072,64]{0,1:T(8,128)(2,1)} %param.21), channel_id=1, source_target_pairs={{0,3},{1,0},{2,1},{3,2},{4,7},{5,4},{6,5},{7,6},{8,11},{9,8},{10,9... | collective-permute-start | bytes 1179656 | tf_op jit(solution)/shard_map/ppermute | solution.py:191
  174.3 25.4 %collective-permute-start.9 = (bf16[64,3072]{1,0:T(8,128)(2,1)}, bf16[64,3072]{1,0:T(8,128)(2,1)}, u32[]{:S(2)}, u32[]{:S(2)}) collective-permute-start(bf16[64,3072]{1,0:T(8,128)(2,1)} %param.22), channel_id=1, source_target_pairs={{0,1},{1,2},{2,3},{3,0},{4,5},{5,6},{6,7},{7,4},{8,9},{9,10},{10,1... | collective-permute-start | bytes 1179656 | tf_op jit(solution)/shard_map/ppermute | solution.py:190
  176.4 32.8 %collective-permute-start.10 = (bf16[64,3072]{1,0:T(8,128)(2,1)}, bf16[64,3072]{1,0:T(8,128)(2,1)}, u32[]{:S(2)}, u32[]{:S(2)}) collective-permute-start(bf16[64,3072]{1,0:T(8,128)(2,1)} %param.22), channel_id=1, source_target_pairs={{0,2},{1,3},{2,0},{3,1},{4,6},{5,7},{6,4},{7,5},{8,10},{9,11},{10,... | collective-permute-start | bytes 1179656 | tf_op jit(solution)/shard_map/ppermute | solution.py:190
  184.2 24.9 %collective-permute-start.11 = (bf16[64,3072]{1,0:T(8,128)(2,1)}, bf16[64,3072]{1,0:T(8,128)(2,1)}, u32[]{:S(2)}, u32[]{:S(2)}) collective-permute-start(bf16[64,3072]{1,0:T(8,128)(2,1)} %param.22), channel_id=1, source_target_pairs={{0,3},{1,0},{2,1},{3,2},{4,7},{5,4},{6,5},{7,6},{8,11},{9,8},{10,9... | collective-permute-start | bytes 1179656 | tf_op jit(solution)/shard_map/ppermute | solution.py:190
  196.7 12.4 %copy-start.23 = (bf16[64,3072]{1,0:T(8,128)(2,1)S(1)}, bf16[64,3072]{1,0:T(8,128)(2,1)}, u32[]{:S(2)}) copy-start(bf16[64,3072]{1,0:T(8,128)(2,1)} %param.22) | copy-start | bytes 1179652
  212.2 30.5 %all-to-all-start.2 = ((bf16[32,8,3072]{2,1,0:T(8,128)(2,1)}), bf16[32,8,3072]{2,1,0:T(8,128)(2,1)S(1)}, u32[]{:S(2)}, u32[]{:S(2)}) async-start(bf16[32,8,3072]{2,1,0:T(8,128)(2,1)} %fusion.1), calls=%async_computation.2 | async-start | bytes 3145728 | tf_op jit(solution)/shard_map/all_to_all | solution.py:311
  219.6 23.4 %copy-start.18 = (f32[3072]{0:T(1024)S(1)}, f32[3072]{0:T(1024)}, u32[]{:S(2)}) copy-start(f32[3072]{0:T(1024)} %param.24) | copy-start | bytes 36868
  219.6 23.3 %copy-start.19 = (f32[3072]{0:T(1024)S(1)}, f32[3072]{0:T(1024)}, u32[]{:S(2)}) copy-start(f32[3072]{0:T(1024)} %param.23) | copy-start | bytes 36868
  243.3 5.2 %collective-permute-start.12 = (f32[8,769]{1,0:T(8,128)S(1)}, f32[8,769]{1,0:T(8,128)S(1)}, u32[]{:S(2)}, u32[]{:S(2)}) collective-permute-start(f32[8,769]{1,0:T(8,128)S(1)} %get-tuple-element.69), channel_id=1, source_target_pairs={{0,1},{1,2},{2,3},{3,0},{4,5},{5,6},{6,7},{7,4},{8,9},{9,10},{10,1... | collective-permute-start | bytes 73832 | tf_op jit(solution)/shard_map/ppermute | solution.py:340
  243.8 5.4 %collective-permute-start.13 = (f32[8,769]{1,0:T(8,128)S(1)}, f32[8,769]{1,0:T(8,128)S(1)}, u32[]{:S(2)}, u32[]{:S(2)}) collective-permute-start(f32[8,769]{1,0:T(8,128)S(1)} %get-tuple-element.70), channel_id=1, source_target_pairs={{0,2},{1,3},{2,0},{3,1},{4,6},{5,7},{6,4},{7,5},{8,10},{9,11},{10,... | collective-permute-start | bytes 73832 | tf_op jit(solution)/shard_map/ppermute | solution.py:340
  247.1 3.9 %collective-permute-start.14 = (f32[8,769]{1,0:T(8,128)S(1)}, f32[8,769]{1,0:T(8,128)S(1)}, u32[]{:S(2)}, u32[]{:S(2)}) collective-permute-start(f32[8,769]{1,0:T(8,128)S(1)} %get-tuple-element.68), channel_id=1, source_target_pairs={{0,3},{1,0},{2,1},{3,2},{4,7},{5,4},{6,5},{7,6},{8,11},{9,8},{10,9... | collective-permute-start | bytes 73832 | tf_op jit(solution)/shard_map/ppermute | solution.py:340
  (20 other events, 67.6 us)
Sparse Core Ops, SparseCore 0:
  18.1 45.6 all-gather.1
